TPU v7x, 128 devices: a whole 4x4x4 slice. The times are simulated.
128 devices in a mesh: ctx: 16 (over y, x), tp: 8 (over z, core).
Axes of the slice: x: 4, y: 4, z: 4, core: 2. Of those that a mesh axis runs over, the one named last changes fastest.
Arguments:
- ssm_input: bfloat16 [4096, 8192], P('ctx', 'tp'), may hold values from -6 to 6
- dt_raw: float32 [4096, 128], P('ctx', 'tp'), may hold values from -5 to 5
- b_proj: bfloat16 [4096, 8, 256], P('ctx', 'tp'), may hold values from -0.59765625 to 0.59765625
- c_proj: bfloat16 [4096, 8, 256], P('ctx', 'tp'), may hold values from -0.59765625 to 0.59765625
- dt_bias: float32 [128], P('tp'), may hold values from -1.5 to 0.5
- decay_rate: float32 [128], P('tp'), may hold values from 0.0002 to 0.05
- skip_gain: float32 [128], P('tp'), may hold values from 0.5 to 1.5
- doc_start: int32 [4096], P('ctx'), may hold values 0 or 1
- out_weight: bfloat16 [8192, 8192], P('tp'), may hold values from -0.0625 to 0.0625
- grad_out: bfloat16 [4096, 8192], P(('ctx', 'tp')), may hold values from -6 to 6
Outputs:
- layer_out: bfloat16 [4096, 8192], P(('ctx', 'tp'))
- grad_input: bfloat16 [4096, 8192], P('ctx', 'tp')
- grad_dt: float32 [4096, 128], P('ctx', 'tp')
- grad_b: bfloat16 [4096, 8, 256], P('ctx', 'tp')
- grad_c: bfloat16 [4096, 8, 256], P('ctx', 'tp')
- weight_grad: bfloat16 [8192, 8192], P('ctx', 'tp')
Inputs may be any that keep to these rules, and one draw needn't show every extreme that they name: `doc_start`: 1 marks the first token of a document; a document runs on until the next 1, across slabs.
All inputs are finite; a program needn't handle non-finite values. No bound on the sum of `doc_start` on one device may be relied on, other than what follows from the above.
Results may differ from a plain program's by a relative error of at most 0.022.
Values may be sent and summed in bfloat16 or wider, within the bound.
No kernel may reach another device: no remote copies, remote signals or barrier semaphores. Data moves between devices by JAX's collectives and lax.ppermute only.
A program may use at most 256 MiB of HBM per device.

v0:
```python
import jax
import jax.numpy as jnp
from jax import lax
from jax.sharding import PartitionSpec as P

HIGHEST = lax.Precision.HIGHEST


def prefix(value, axis, combine, identity, reverse):
    devices, mine = (lax.axis_size(axis), lax.axis_index(axis))
    everything = jax.tree.map(
        lambda part, kind: lax.all_gather(part.astype(kind), axis),
        value,
        (jnp.bfloat16, jnp.bfloat16),
    )
    start = jax.tree.map(
        lambda part, zero: jnp.broadcast_to(jnp.asarray(zero, part.dtype), part.shape),
        value,
        identity,
    )

    def step(k, before):
        at = devices - 1 - k if reverse else k
        reached = at > mine if reverse else at < mine
        new = combine(
            before, jax.tree.map(lambda part, own: part[at].astype(own.dtype), everything, value)
        )
        return jax.tree.map(lambda a, b: jnp.where(reached, a, b), new, before)

    return lax.fori_loop(0, devices, step, start)


def block_ssd(
    seq_in, step_raw, b_rows, c_rows, scores, carried, doc_start, bias_heads, rate_heads, skip_heads
):
    length = seq_in.shape[0]
    step_size = jax.nn.softplus(step_raw + bias_heads)
    cumul = jnp.cumsum(-step_size * rate_heads, axis=0)
    segment = jnp.cumsum(doc_start)
    reach = (segment == 0).astype(jnp.float32)
    order = jnp.arange(length)
    causal = (segment[:, None] == segment[None, :]) & (order[:, None] >= order[None, :])
    cum_heads = jnp.transpose(cumul, (1, 2, 0))
    differ = cum_heads[:, :, :, None] - cum_heads[:, :, None, :]
    decays = jnp.exp(jnp.where(causal, differ, -jnp.inf))
    mixing = decays * scores[:, None] * jnp.transpose(step_size, (1, 2, 0))[:, :, None, :]
    inside = jnp.einsum("gkts,sgkp->tgkp", mixing, seq_in, precision=HIGHEST)
    entry = jnp.exp(cumul) * reach[:, None, None]
    from_carry = entry[..., None] * jnp.einsum("tgn,gkpn->tgkp", c_rows, carried, precision=HIGHEST)
    mixer = inside + from_carry + skip_heads[..., None] * seq_in
    same_last = (segment == segment[-1]).astype(jnp.float32)
    tail = jnp.exp(cumul[-1] - cumul) * same_last[:, None, None] * step_size
    local_state = jnp.einsum("sgk,sgkp,sgn->gkpn", tail, seq_in, b_rows, precision=HIGHEST)
    through = reach[-1] * jnp.exp(cumul[-1])
    return (mixer, local_state, through)


def chain_combine(earlier, later):
    return (earlier[0] * later[0], later[0][..., None, None] * earlier[1] + later[1])


def shards(
    ssm_input,
    dt_raw,
    b_proj,
    c_proj,
    dt_bias,
    decay_rate,
    skip_gain,
    doc_start,
    out_weight,
    grad_out,
):
    rows = ssm_input.shape[0]
    heads = dt_raw.shape[1]
    head_dim = ssm_input.shape[1] // heads
    seq_f32 = ssm_input.astype(jnp.float32).reshape(rows, 1, heads, head_dim)
    step_raw = dt_raw.reshape(rows, 1, heads)
    b_rows = b_proj.astype(jnp.float32)
    c_rows = c_proj.astype(jnp.float32)
    bias_heads = dt_bias.reshape(1, heads)
    rate_heads = decay_rate.reshape(1, heads)
    skip_heads = skip_gain.reshape(1, heads)
    scores = jnp.einsum("tgn,sgn->gts", c_proj, b_proj, preferred_element_type=jnp.float32)
    step_size = jax.nn.softplus(step_raw + bias_heads)
    cumul = jnp.cumsum(-step_size * rate_heads, axis=0)
    segment = jnp.cumsum(doc_start)
    reach = (segment == 0).astype(jnp.float32)
    same_last = (segment == segment[-1]).astype(jnp.float32)
    tail = jnp.exp(cumul[-1] - cumul) * same_last[:, None, None] * step_size
    local_state = jnp.einsum("sgk,sgkp,sgn->gkpn", tail, seq_f32, b_rows, precision=HIGHEST)
    through = reach[-1] * jnp.exp(cumul[-1])
    identity_pair = (jnp.ones_like(through), jnp.zeros_like(local_state))
    carried = prefix((through, local_state), "ctx", chain_combine, identity_pair, False)[1]

    def local_fn(seq_arg, step_arg, b_arg, c_arg, score_arg):
        return block_ssd(
            seq_arg,
            step_arg,
            b_arg,
            c_arg,
            score_arg,
            carried,
            doc_start,
            bias_heads,
            rate_heads,
            skip_heads,
        )

    (mixer, _, _), pullback = jax.vjp(local_fn, seq_f32, step_raw, b_rows, c_rows, scores)
    mixer_bf = mixer.reshape(rows, heads * head_dim).astype(jnp.bfloat16)
    layer_out = lax.psum_scatter(
        jnp.dot(mixer_bf, out_weight, preferred_element_type=jnp.float32).astype(jnp.bfloat16),
        "tp",
        scatter_dimension=0,
        tiled=True,
    )
    grad_full = lax.all_gather(grad_out, "tp", axis=0, tiled=True)
    grad_mix = lax.dot_general(
        grad_full, out_weight, (((1,), (1,)), ((), ())), preferred_element_type=jnp.float32
    ).astype(jnp.bfloat16)
    grad_heads = grad_mix.astype(jnp.float32).reshape(rows, 1, heads, head_dim)
    entry = jnp.exp(cumul) * reach[:, None, None]
    local_grad = jnp.einsum("tgk,tgkp,tgn->gkpn", entry, grad_heads, c_rows, precision=HIGHEST)
    grad_next = prefix((through, local_grad), "ctx", chain_combine, identity_pair, True)[1]
    through_grad = jnp.sum(grad_next * carried, axis=(2, 3))
    grad_seq, grad_step, grad_brows, grad_crows, grad_scores = pullback(
        (grad_heads, grad_next, through_grad)
    )
    grad_brows = grad_brows + jnp.einsum("gts,tgn->sgn", grad_scores, c_rows, precision=HIGHEST)
    grad_crows = grad_crows + jnp.einsum("gts,sgn->tgn", grad_scores, b_rows, precision=HIGHEST)
    weight_sum = lax.psum_scatter(
        lax.dot_general(
            grad_full, mixer_bf, (((0,), (0,)), ((), ())), preferred_element_type=jnp.float32
        ).astype(jnp.bfloat16),
        "ctx",
        scatter_dimension=0,
        tiled=True,
    )
    return (
        layer_out,
        grad_seq.reshape(rows, heads * head_dim).astype(jnp.bfloat16),
        grad_step.reshape(rows, heads),
        grad_brows.astype(jnp.bfloat16),
        grad_crows.astype(jnp.bfloat16),
        weight_sum,
    )


def solution(mesh):
    in_specs = (
        P("ctx", "tp"),
        P("ctx", "tp"),
        P("ctx", "tp", None),
        P("ctx", "tp", None),
        P("tp"),
        P("tp"),
        P("tp"),
        P("ctx"),
        P("tp", None),
        P(("ctx", "tp"), None),
    )
    out_specs = (
        P(("ctx", "tp"), None),
        P("ctx", "tp"),
        P("ctx", "tp"),
        P("ctx", "tp", None),
        P("ctx", "tp", None),
        P("ctx", "tp"),
    )
    return jax.shard_map(shards, mesh=mesh, in_specs=in_specs, out_specs=out_specs, check_vma=False)
```

profile of v0, /device:TPU:1, one launch (start us, length us, event | category | flops | bytes accessed | tf_op | source)
XLA Modules:
  0.0 450.2 jit_solution(1089252134521595264)
XLA Ops:
  12.2 33.5 %all-gather.6.cloned.1.call-done = bf16[256,8192]{1,0:T(8,128)(2,1)} async-done(((bf16[32,8192]{1,0:T(8,128)(2,1)}), bf16[256,8192]{1,0:T(8,128)(2,1)}) %all-gather.6.cloned.1.call-update) | async-done | bytes 4194320 | tf_op jit(solution)/shard_map/all_gather | solution.py:118
  45.7 11.6 %convolution_convert_fusion.3 = bf16[256,1024]{1,0:T(8,128)(2,1)S(1)} fusion(bf16[256,8192]{1,0:T(8,128)(2,1)} %all-gather.6.cloned.1.call-done, bf16[1024,8192]{1,0:T(8,128)(2,1)} %param.22), kind=kOutput, calls=%fused_computation.43 | convolution fusion | flops 4295229440 | bytes 21495808 | tf_op jit(solution)/shard_map/dot_general | solution.py:119
  61.8 18.4 %all_gather.21 = bf16[16,1,16]{2,1,0:T(2,128)(2,1)} all-gather(bf16[1,1,16]{2,1,0:T(2,128)(2,1)S(1)} %get-tuple-element.399), channel_id=1, replica_groups=mesh['ctx'=16,'tp'=8] {'ctx'}, dimensions={0}, use_global_device_ids=true | all-gather | bytes 544 | tf_op jit(solution)/shard_map/all_gather | solution.py:12
  80.2 1.9 compare_convert_fusion
  82.1 47.1 %all-gather.10.cloned.1.call-done = bf16[256,64,256]{2,1,0:T(8,128)(2,1)} async-done(((bf16[16,64,256]{2,1,0:T(8,128)(2,1)}), bf16[256,64,256]{2,1,0:T(8,128)(2,1)}) %all-gather.10.cloned.1.call-update) | async-done | bytes 8388624 | tf_op jit(solution)/shard_map/all_gather | solution.py:12
  129.2 31.4 %while.31 = (s32[]{:T(128)}, f32[1,16,64,256]{3,2,1,0:T(8,128)S(1)}, s32[]{:T(128)}, bf16[16,1,16]{2,1,0:T(2,128)(2,1)}, bf16[16,1,16,64,256]{4,3,2,1,0:T(8,128)...) while((s32[]{:T(128)}, f32[1,16,64,256]{3,2,1,0:T(8,128)S(1)}, s32[]{:T(128)}, ...), condition=%wide.region_8.9_spmd.clone, body=%wide.region_7.8_spmd.clone.sunk | while | flops 1310744 | bytes 2621775 | solution.py:30
  160.6 2.2 fusion.50
  164.3 1.6 multiply_multiply_fusion
  166.6 1.7 multiply_reduce_fusion.4
  170.4 1.6 copy.146
  172.0 2.2 convolution_convert_fusion.2
  181.0 1.6 copy.140
  182.6 62.1 %all-gather.8.cloned.1.call-done = bf16[256,64,256]{2,1,0:T(8,128)(2,1)} async-done(((bf16[16,64,256]{2,1,0:T(8,128)(2,1)}), bf16[256,64,256]{2,1,0:T(8,128)(2,1)}) %all-gather.8.cloned.1.call-update) | async-done | bytes 8388624 | tf_op jit(solution)/shard_map/all_gather | solution.py:12
  244.7 31.2 %while.30 = (s32[]{:T(128)}, f32[1,16,64,256]{3,2,1,0:T(8,128)S(1)}, s32[]{:T(128)}, bf16[16,1,16]{2,1,0:T(2,128)(2,1)}, bf16[16,1,16,64,256]{4,3,2,1,0:T(8,128)(2,1)}, /*index=5*/s32[]{:T(128)}, s32[]{:T(128)}) while((s32[]{:T(128)}, f32[1,16,64,256]{3,2,1,0:T(8,128)S(1)}, s32[]{:T(128)}, bf16[16,1,16]{2,1,0:T(2,128)(2,1)}, ...), condition=%wide.region_5.6_spmd.clone, body=%wide.region_4.5_spmd.clone.sunk | while | flops 1310740 | bytes 2621713 | solution.py:30
  277.1 5.8 %fusion.40 = bf16[256,1,16,64]{0,3,2,1:T(8,128)(2,1)} fusion(bf16[256,16,64]{0,2,1:T(8,128)(2,1)} %bitcast.245, f32[16,256]{1,0:T(8,128)} %copy.140, f32[256,256]{1,0:T(8,128)} %fusion.77, f32[16,256]{1,0:T(8,128)} %bitcast_add_fusion.2, pred[256,256]{1,0:T(8,128)(4,1)} %fusion.62, f32[256,1,16,64]{0,3,2,1:T(8,128)} %bitcast.256, ...), kind=kOutput, calls=%fused_computation.42 | convolution fusion | flops 810811392 | bytes 3522624 | tf_op jit(solution)/shard_map/jvp(gkts,sgkp->tgkp)/dot_general | solution.py:47
  283.0 12.6 %convert_bitcast_fusion = bf16[8192,1024]{0,1:T(8,128)(2,1)} fusion(bf16[256,1024]{0,1:T(8,128)(2,1)} %bitcast.248, bf16[256,8192]{1,0:T(8,128)(2,1)} %all-gather.6.cloned.1.call-done), kind=kOutput, calls=%fused_computation.6 | convolution fusion | flops 4303355904 | bytes 21495808 | tf_op jit(solution)/shard_map/dot_general | solution.py:133
  295.9 12.5 %convolution_convert_fusion = bf16[256,8192]{1,0:T(8,128)(2,1)} fusion(bf16[256,1024]{0,1:T(8,128)(2,1)} %bitcast.249, bf16[1024,8192]{1,0:T(8,128)(2,1)} %param.22), kind=kOutput, calls=%fused_computation.7 | convolution fusion | flops 4297064448 | bytes 21495808 | tf_op jit(solution)/shard_map/dot_general | solution.py:113
  308.4 2.1 copy.152
  310.4 5.1 %fusion.37 = bf16[256,1,16,64]{0,3,2,1:T(8,128)(2,1)} fusion(bf16[16,64,256]{2,1,0:T(8,128)(2,1)} %bitcast.260, f32[16,256]{1,0:T(8,128)} %copy.140, f32[256,256]{1,0:T(8,128)} %fusion.77, f32[16,256]{1,0:T(8,128)} %bitcast_add_fusion.2, pred[256,256]{1,0:T(8,128)(4,1)} %fusion.62, f32[256,16,64]{0,2,1:T(8,128)S(1)} %bitcast.242, ...), kind=kOutput, calls=%fused_computation.39 | convolution fusion | flops 810811392 | bytes 3522624 | tf_op jit(solution)/shard_map/transpose(jvp(gkts,sgkp->tgkp))/dot_general | solution.py:47
  315.6 2.1 copy.162
  317.6 5.2 %fusion.9 = (f32[16,256]{1,0:T(8,128)}, f32[16,256]{1,0:T(8,128)}, f32[16,256]{1,0:T(8,128)}, f32[256,256]{1,0:T(8,128)}) fusion(f32[16,256]{1,0:T(8,128)} %copy.140, f32[256,256]{1,0:T(8,128)} %fusion.77, f32[16,256]{1,0:T(8,128)} %bitcast_add_fusion.2, pred[256,256]{1,0:T(8,128)(4,1)} %fusion.62, bf16[16,64,256]{2,1,0:T(8,128)(2,1)} %bitcast.261, ...), kind=kOutput, calls=%fused_computation.17 | convolution fusion | flops 147771392 | bytes 1720320 | tf_op jit(solution)/shard_map/transpose(jvp(gkts,sgkp->tgkp))/dot_general | solution.py:47
  325.8 1.5 copy.153
  327.3 2.9 fusion.44
  330.1 1.9 fusion.49
  332.1 1.7 copy.164
  333.7 1.9 convolution_bitcast_fusion.2
  339.7 1.6 add_add_fusion
  341.4 2.5 reduce-window.29
  346.0 3.5 fusion.47
  349.5 56.1 %reduce-scatter.5.cloned.1.call-done = bf16[512,1024]{0,1:T(8,128)(2,1)} async-done(((bf16[8192,1024]{0,1:T(8,128)(2,1)}), bf16[512,1024]{0,1:T(8,128)(2,1)}) %reduce-scatter.5.cloned.1.call-update) | async-done | bytes 1048592 | tf_op jit(solution)/shard_map/reduce_scatter | solution.py:132
  405.6 2.3 copy.165
  407.9 35.8 %reduce-scatter.3.cloned.1.call-done = bf16[32,8192]{1,0:T(8,128)(2,1)} async-done(((bf16[256,8192]{1,0:T(8,128)(2,1)}), bf16[32,8192]{1,0:T(8,128)(2,1)}) %reduce-scatter.3.cloned.1.call-update) | async-done | bytes 524304 | tf_op jit(solution)/shard_map/reduce_scatter | solution.py:112
  (149 shorter events, 92.9 us)
Async XLA Ops:
  7.2 50.4 %copy-start = (bf16[256,1,256]{2,0,1:T(8,128)(2,1)S(1)}, bf16[256,1,256]{2,0,1:T(8,128)(2,1)}, u32[]{:S(2)}) copy-start(bf16[256,1,256]{2,0,1:T(8,128)(2,1)} %param.17) | copy-start | bytes 393220
  7.2 38.5 %all-gather.6.cloned.1.call-start = ((), (), s32[]{:S(2)}) async-start(), calls=%async_computation.3 | async-start | bytes 4718592 | tf_op jit(solution)/shard_map/all_gather | solution.py:118
  7.9 121.3 %all-gather.10.cloned.1.call-start = ((), (), s32[]{:S(2)}) async-start(), calls=%async_computation.6 | async-start | bytes 8912896 | tf_op jit(solution)/shard_map/all_gather | solution.py:12
  11.8 47.3 %copy-start.12 = (f32[256]{0:T(256)}, f32[256]{0:T(256)S(1)}, u32[]{:S(2)}) copy-start(f32[256]{0:T(256)S(1)} %get-tuple-element.392) | copy-start | bytes 3076
  11.8 47.9 %copy-start.11 = (s32[256]{0:T(256)}, s32[256]{0:T(256)S(1)}, u32[]{:S(2)}) copy-start(s32[256]{0:T(256)S(1)} %get-tuple-element.393) | copy-start | bytes 3076
  11.8 33.9 %copy-start.8 = (f32[16,2,128]{0,2,1:T(8,128)}, f32[16,2,128]{0,2,1:T(8,128)S(1)}, u32[]{:S(2)}) copy-start(f32[16,2,128]{0,2,1:T(8,128)S(1)} %broadcast.148) | copy-start | bytes 49156
  12.2 48.4 %copy-start.5 = (f32[256,1,16]{2,1,0:T(1,128)}, f32[256,1,16]{2,1,0:T(1,128)S(1)}, u32[]{:S(2)}) copy-start(f32[256,1,16]{2,1,0:T(1,128)S(1)} %get-tuple-element.391) | copy-start | bytes 49156
  12.2 45.3 %copy-start.9 = (f32[256,16]{0,1:T(8,128)}, f32[256,16]{0,1:T(8,128)S(1)}, u32[]{:S(2)}) copy-start(f32[256,16]{0,1:T(8,128)S(1)} %copy.144) | copy-start | bytes 49156
  57.3 1.8 copy-start.3
  57.3 3.0 copy-start.2
  59.0 185.7 %all-gather.8.cloned.1.call-start = ((), (), s32[]{:S(2)}) async-start(), calls=%async_computation.5 | async-start | bytes 8912896 | tf_op jit(solution)/shard_map/all_gather | solution.py:12
  60.5 111.4 %copy-start.1 = (bf16[256,1024]{0,1:T(8,128)(2,1)}, bf16[256,1024]{0,1:T(8,128)(2,1)S(1)}, u32[]{:S(2)}) copy-start(bf16[256,1024]{0,1:T(8,128)(2,1)S(1)} %copy.141) | copy-start | bytes 1572868
  129.2 31.4 %copy-start.4 = (bf16[256,1,256]{2,0,1:T(8,128)(2,1)S(1)}, bf16[256,1,256]{2,0,1:T(8,128)(2,1)}, u32[]{:S(2)}) copy-start(bf16[256,1,256]{2,0,1:T(8,128)(2,1)} %param.16) | copy-start | bytes 393220
  165.9 0.6 copy-start.7
  168.3 0.6 copy-start.6
  174.2 231.4 %reduce-scatter.5.cloned.1.call-start = ((), (), s32[]{:S(2)}) async-start(), calls=%async_computation.4 | async-start | bytes 17825792 | tf_op jit(solution)/shard_map/reduce_scatter | solution.py:132
  244.7 32.5 %copy-start.10 = (f32[256,16]{0,1:T(8,128)S(1)}, f32[256,16]{0,1:T(8,128)}, u32[]{:S(2)}) copy-start(f32[256,16]{0,1:T(8,128)} %copy-done.9) | copy-start | bytes 49156
  295.6 148.0 %reduce-scatter.3.cloned.1.call-start = ((), (), s32[]{:S(2)}) async-start(), calls=%async_computation.2 | async-start | bytes 4718592 | tf_op jit(solution)/shard_map/reduce_scatter | solution.py:112
Sparse Core Ops, SparseCore 0:
  9.7 35.9 all-gather.5
  59.1 70.0 all-gather.9
  174.3 70.3 all-gather.7
  295.7 109.8 reduce-scatter.4
  408.4 35.1 reduce-scatter.2
where the time goes:
time: 455 us; the launch traced here: 450 us
  waiting for transfers between devices  235 us (52%)
  other arithmetic  83.2 us (18%)
  matrix products  71 us (16%)
  local copies, waits for them, and re-layouts  26.8 us (6%)
  blocking collectives  18.4 us (4%)
  between operations  14 us (3%)
    all_gather x2, waiting for transfers between devices, prefix(): lax.all_gather(part.astype(kind), axis)  109 us
    reduce_scatter x1, waiting for transfers between devices, shards(): lax.psum_scatter(lax.dot_general(grad_full, mixer_bf, (((0,), (0,)), ((),...  56.1 us
    select_n x32, other arithmetic, step(): return jax.tree.map(lambda a, b: jnp.where(reached, a, b), new, before)  41.2 us
    reduce_scatter x1, waiting for transfers between devices, shards(): lax.psum_scatter(jnp.dot(mixer_bf, out_weight, preferred_element_type=jnp...  35.8 us
    all_gather x1, waiting for transfers between devices, shards(): grad_full = lax.all_gather(grad_out, 'tp', axis=0, tiled=True)  33.5 us
    convert_element_type x32, other arithmetic, step(): part[at].astype(own.dtype)  20.5 us
    all_gather x1, blocking collectives, prefix(): lax.all_gather(part.astype(kind), axis)  18.4 us
    dot_general x3, matrix products, block_ssd(): inside = jnp.einsum('gkts,sgkp->tgkp', mixing, seq_in, precision=HIGHEST)  16.2 us
  transfers between devices with their start and end apart: 5, of which 5 were waited for; matrix products, arithmetic and copies ran while one was open for 16% of the time, Pallas kernels for 0%

commit v1 on v0

v1 whole, which is shorter than its diff:
```python
import jax
import jax.numpy as jnp
from jax import lax
from jax.experimental import pallas as pl
from jax.experimental.pallas import tpu as pltpu
from jax.sharding import PartitionSpec as P

F32 = jnp.float32
BF16 = jnp.bfloat16
HIGHEST = lax.Precision.HIGHEST
ROWS = 256
HEADS = 16
DIM = 64
STATE = 256
WIDE = HEADS * DIM
PAIRS = HEADS // 2
EXTRA = 8
MASKED = -1e30
CUM, STEP, ENTRY, ETAIL, TAIL, THROUGH, SEG, SIG = range(8)


def dot(a, b, dims, precision=None):
    return lax.dot_general(a, b, (dims, ((), ())), precision=precision, preferred_element_type=F32)


def nn(a, b):
    return dot(a, b, ((1,), (0,)))


def nt(a, b):
    return dot(a, b, ((1,), (1,)))


def tn(a, b):
    return dot(a, b, ((0,), (0,)))


def vmem(n):
    return [pl.BlockSpec(memory_space=pltpu.VMEM)] * n


def smem(n):
    return [pl.BlockSpec(memory_space=pltpu.SMEM)] * n


def params():
    return pltpu.CompilerParams(vmem_limit_bytes=48 * 1024 * 1024)


def iota(shape, axis):
    return lax.broadcasted_iota(jnp.int32, shape, axis)


def col(tab, which, head):
    at = which * HEADS + head
    return tab[:, at : at + 1]


def pair_cols(tab, which, pair):
    low = iota((ROWS, 2 * DIM), 1) < DIM
    return jnp.where(low, col(tab, which, 2 * pair), col(tab, which, 2 * pair + 1))


def cols_of(pair):
    return slice(pair * 2 * DIM, (pair + 1) * 2 * DIM)


def states_kernel(bias, rate, x, dt, doc, b, payload, tab_rows, tab_cols):
    head = iota((HEADS, ROWS), 0)
    bias_rows = jnp.zeros((HEADS, ROWS), F32)
    rate_rows = jnp.zeros((HEADS, ROWS), F32)
    for h in range(HEADS):
        bias_rows = jnp.where(head == h, bias[h], bias_rows)
        rate_rows = jnp.where(head == h, rate[h], rate_rows)
    raw = dt[...] + bias_rows
    small = jnp.exp(-jnp.abs(raw))
    step = jnp.maximum(raw, 0.0) + jnp.log1p(small)
    sig = jnp.where(raw >= 0, 1.0, small) / (1.0 + small)
    upto = (iota((ROWS, ROWS), 0) <= iota((ROWS, ROWS), 1)).astype(F32)
    cum = dot(-step * rate_rows, upto, ((1,), (0,)), HIGHEST)
    starts = jnp.broadcast_to(doc[...].astype(F32), (HEADS, ROWS))
    seg = nn(starts.astype(BF16), upto.astype(BF16))
    last = cum[:, ROWS - 1 :]
    seg_last = seg[:, ROWS - 1 :]
    entry = jnp.where(seg == 0.0, jnp.exp(cum), 0.0)
    etail = jnp.where(seg == seg_last, jnp.exp(last - cum), 0.0)
    through = jnp.broadcast_to(jnp.where(seg_last == 0.0, jnp.exp(last), 0.0), (HEADS, ROWS))
    rows = jnp.concatenate([cum, step, entry, etail, etail * step, through, seg, sig], axis=0)
    tab_rows[...] = rows
    tab = rows.T
    tab_cols[...] = tab
    for j in range(PAIRS):
        weighted = (x[:, cols_of(j)].astype(F32) * pair_cols(tab, TAIL, j)).astype(BF16)
        state = tn(weighted, b[...]).astype(BF16)
        payload[2 * j, :DIM, :] = state[:DIM]
        payload[2 * j + 1, :DIM, :] = state[DIM:]
    upper = through.astype(BF16).astype(F32)
    lower = through - upper
    which = iota((EXTRA, ROWS), 0)
    for h in range(HEADS):
        tail_rows = jnp.where(which == 0, upper[h : h + 1], jnp.where(which == 1, lower[h : h + 1], 0.0))
        payload[h, DIM:, :] = tail_rows.astype(BF16)


def states(bias, rate, x, dt, doc, b):
    return pl.pallas_call(
        states_kernel,
        in_specs=smem(2) + vmem(4),
        out_specs=vmem(3),
        out_shape=(
            jax.ShapeDtypeStruct((HEADS, DIM + EXTRA, STATE), BF16),
            jax.ShapeDtypeStruct((8 * HEADS, ROWS), F32),
            jax.ShapeDtypeStruct((ROWS, 8 * HEADS), F32),
        ),
        compiler_params=params(),
    )(bias, rate, x, dt, doc, b)


def prefix_kernel(got, out, decay):
    slabs = got.shape[0]
    carry = jnp.zeros((DIM, STATE), F32)
    for c in range(slabs):
        out[c] = carry.astype(BF16)
        extra = got[c, DIM:, :].astype(F32)
        through = extra[0:1] + extra[1:2]
        decay[c : c + 1, :] = through
        carry = through * carry + got[c, :DIM, :].astype(F32)


def prefix(got):
    slabs = got.shape[0]
    return pl.pallas_call(
        prefix_kernel,
        in_specs=vmem(1),
        out_specs=vmem(2),
        out_shape=(
            jax.ShapeDtypeStruct((slabs, DIM, STATE), BF16),
            jax.ShapeDtypeStruct((slabs, STATE), F32),
        ),
        compiler_params=params(),
    )(got)


def suffix_kernel(got, decay, out):
    slabs = got.shape[0]
    carry = jnp.zeros((DIM, STATE), F32)
    for c in reversed(range(slabs)):
        out[c] = carry.astype(BF16)
        carry = decay[c : c + 1, :] * carry + got[c].astype(F32)


def suffix(got, decay):
    return pl.pallas_call(
        suffix_kernel,
        in_specs=vmem(2),
        out_specs=vmem(1)[0],
        out_shape=jax.ShapeDtypeStruct(got.shape, BF16),
        compiler_params=params(),
    )(got, decay)


def mixer_kernel(skip, x, b, c, rows, tab_ref, carried, mixed, inner):
    tab = tab_ref[...]
    scores = nt(c[...], b[...])
    order_t, order_s = iota((ROWS, ROWS), 0), iota((ROWS, ROWS), 1)
    seg_row = rows[SEG * HEADS : SEG * HEADS + 1, :]
    mask = jnp.where((order_t >= order_s) & (col(tab, SEG, 0) == seg_row), 0.0, MASKED)
    low = iota((ROWS, 2 * DIM), 1) < DIM
    for j in range(PAIRS):
        x_pair = x[:, cols_of(j)].astype(F32)
        scaled = (x_pair * pair_cols(tab, STEP, j)).astype(BF16)
        parts = []
        for h in (2 * j, 2 * j + 1):
            row = rows[CUM * HEADS + h : CUM * HEADS + h + 1, :]
            weight = jnp.exp(col(tab, CUM, h) - row + mask) * scores
            parts.append(nn(weight.astype(BF16), scaled))
        state = carried[2 * j : 2 * j + 2].reshape(2 * DIM, STATE)
        got = jnp.where(low, parts[0], parts[1]) + pair_cols(tab, ENTRY, j) * nt(c[...], state)
        inner[:, cols_of(j)] = got
        gain = jnp.where(low, skip[2 * j], skip[2 * j + 1])
        mixed[:, cols_of(j)] = (got + gain * x_pair).astype(BF16)


def mixer(skip, x, b, c, rows, tab, carried):
    return pl.pallas_call(
        mixer_kernel,
        in_specs=smem(1) + vmem(6),
        out_specs=vmem(2),
        out_shape=(
            jax.ShapeDtypeStruct((ROWS, WIDE), BF16),
            jax.ShapeDtypeStruct((ROWS, WIDE), F32),
        ),
        compiler_params=params(),
    )(skip, x, b, c, rows, tab, carried)


def local_grad_kernel(grad, c, tab_ref, out):
    tab = tab_ref[...]
    for j in range(PAIRS):
        weighted = (grad[:, cols_of(j)].astype(F32) * pair_cols(tab, ENTRY, j)).astype(BF16)
        state = tn(weighted, c[...]).astype(BF16)
        out[2 * j] = state[:DIM]
        out[2 * j + 1] = state[DIM:]


def local_grad(grad, c, tab):
    return pl.pallas_call(
        local_grad_kernel,
        in_specs=vmem(3),
        out_specs=vmem(1)[0],
        out_shape=jax.ShapeDtypeStruct((HEADS, DIM, STATE), BF16),
        compiler_params=params(),
    )(grad, c, tab)


def head_sums(pair, values):
    head = iota((HEADS, 2 * DIM), 0)
    own = (head == 2 * pair + iota((HEADS, 2 * DIM), 1) // DIM).astype(BF16)
    upper = values.astype(BF16)
    lower = (values - upper.astype(F32)).astype(BF16)
    return nt(own, upper) + nt(own, lower)


def backward_kernel(
    skip, rate, x, b, c, rows, tab_ref, carried, inner, grad, after, grad_x, grad_dt, grad_b, grad_c
):
    tab = tab_ref[...]
    scores = nt(b[...], c[...])
    order_s, order_t = iota((ROWS, ROWS), 0), iota((ROWS, ROWS), 1)
    seg_row = rows[SEG * HEADS : SEG * HEADS + 1, :]
    mask = jnp.where((order_t >= order_s) & (col(tab, SEG, 0) == seg_row), 0.0, MASKED)
    low = iota((ROWS, 2 * DIM), 1) < DIM
    grad_scores = jnp.zeros((ROWS, ROWS), F32)
    b_sum = jnp.zeros((ROWS, STATE), F32)
    c_sum = jnp.zeros((ROWS, STATE), F32)
    step_grad = jnp.zeros((HEADS, ROWS), F32)
    cum_grad = jnp.zeros((HEADS, ROWS), F32)
    state_dot = jnp.zeros((HEADS, ROWS), F32)
    tail_dot = jnp.zeros((HEADS, ROWS), F32)
    for j in range(PAIRS):
        x_pair = x[:, cols_of(j)].astype(F32)
        step = pair_cols(tab, STEP, j)
        scaled_f = x_pair * step
        scaled = scaled_f.astype(BF16)
        g = grad[:, cols_of(j)]
        g_f = g.astype(F32)
        zero = jnp.zeros_like(g)
        parts = []
        for k in range(2):
            h = 2 * j + k
            row = rows[CUM * HEADS + h : CUM * HEADS + h + 1, :]
            decay = jnp.exp(row - col(tab, CUM, h) + mask)
            own = jnp.where(low if k == 0 else jnp.logical_not(low), g, zero)
            grad_scores = grad_scores + nt(scaled, own) * decay
            parts.append(nn((decay * scores).astype(BF16), g))
        nxt = after[2 * j : 2 * j + 2].reshape(2 * DIM, STATE)
        prev = carried[2 * j : 2 * j + 2].reshape(2 * DIM, STATE)
        etail = pair_cols(tab, ETAIL, j)
        from_tail = etail * nt(b[...], nxt)
        total = jnp.where(low, parts[0], parts[1]) + from_tail
        gain = jnp.where(low, skip[2 * j], skip[2 * j + 1])
        grad_x[:, cols_of(j)] = (step * total + gain * g_f).astype(BF16)
        step_grad = step_grad + head_sums(j, x_pair * total)
        cum_grad = cum_grad + head_sums(j, g_f * inner[:, cols_of(j)])
        tail_dot = tail_dot + head_sums(j, scaled_f * from_tail)
        product = nxt.astype(F32) * prev.astype(F32)
        head = iota((HEADS, 2 * DIM), 0)
        own_rows = (head == 2 * j + iota((HEADS, 2 * DIM), 1) // DIM).astype(BF16)
        upper = product.astype(BF16)
        lower = (product - upper.astype(F32)).astype(BF16)
        state_dot = state_dot + nn(own_rows, upper) + nn(own_rows, lower)
        b_sum = b_sum + nn((etail * scaled_f).astype(BF16), nxt)
        c_sum = c_sum + nn((pair_cols(tab, ENTRY, j) * g_f).astype(BF16), prev)
    flow = grad_scores.astype(BF16)
    grad_b[...] = (b_sum + nn(flow, c[...])).astype(BF16)
    grad_c[...] = (c_sum + tn(flow, b[...])).astype(BF16)
    step_rows = rows[STEP * HEADS : (STEP + 1) * HEADS, :]
    through = rows[THROUGH * HEADS : (THROUGH + 1) * HEADS, :]
    end = jnp.sum(tail_dot, axis=1, keepdims=True) + jnp.sum(
        through * state_dot, axis=1, keepdims=True
    )
    cum_grad = cum_grad - step_rows * step_grad
    since = (iota((ROWS, ROWS), 0) >= iota((ROWS, ROWS), 1)).astype(F32)
    decay_grad = dot(cum_grad, since, ((1,), (0,)), HIGHEST) + end
    head = iota((HEADS, ROWS), 0)
    rate_rows = jnp.zeros((HEADS, ROWS), F32)
    for h in range(HEADS):
        rate_rows = jnp.where(head == h, rate[h], rate_rows)
    sig = rows[SIG * HEADS : (SIG + 1) * HEADS, :]
    grad_dt[...] = (step_grad - rate_rows * decay_grad) * sig


def backward(skip, rate, x, b, c, rows, tab, carried, inner, grad, after):
    return pl.pallas_call(
        backward_kernel,
        in_specs=smem(2) + vmem(9),
        out_specs=vmem(4),
        out_shape=(
            jax.ShapeDtypeStruct((ROWS, WIDE), BF16),
            jax.ShapeDtypeStruct((HEADS, ROWS), F32),
            jax.ShapeDtypeStruct((ROWS, STATE), BF16),
            jax.ShapeDtypeStruct((ROWS, STATE), BF16),
        ),
        compiler_params=params(),
    )(skip, rate, x, b, c, rows, tab, carried, inner, grad, after)


def weight_kernel(core, own, other, mixed, out, acc):
    at = pl.program_id(0)

    @pl.when(at == 0)
    def _():
        acc[...] = jnp.zeros_like(acc)

    mine = core[0]
    slabs, planes, _, share, wide = mixed.shape
    total = None
    for source, which in ((own, mine), (other, 1 - mine)):
        left = jnp.concatenate(
            [source[z, k * share : (k + 1) * share] for k in range(slabs) for z in range(planes)], 0
        )
        right = jnp.concatenate(
            [mixed[k, z, which] for k in range(slabs) for z in range(planes)], 0
        )
        part = tn(left, right)
        total = part if total is None else total + part
    acc[...] += total

    @pl.when(at == pl.num_programs(0) - 1)
    def _():
        out[...] = acc[...].astype(BF16)


def weight_grad(core, own, other, mixed):
    planes, spread, cols = own.shape
    slabs, _, _, share, wide = mixed.shape
    block = 2
    return pl.pallas_call(
        weight_kernel,
        grid=(slabs // block,),
        in_specs=[
            pl.BlockSpec(memory_space=pltpu.SMEM),
            pl.BlockSpec((planes, block * share, cols), lambda i: (0, i, 0)),
            pl.BlockSpec((planes, block * share, cols), lambda i: (0, i, 0)),
            pl.BlockSpec((block, planes, 2, share, wide), lambda i: (i, 0, 0, 0, 0)),
        ],
        out_specs=pl.BlockSpec((cols, wide), lambda i: (0, 0)),
        out_shape=jax.ShapeDtypeStruct((cols, wide), BF16),
        scratch_shapes=[pltpu.VMEM((cols, wide), F32)],
        compiler_params=params(),
    )(core, own, other, mixed)


SWAP = [(i, i ^ 1) for i in range(8)]
PLANES = [[0, 2, 4, 6], [1, 3, 5, 7]]


def over_planes(value):
    return lax.all_to_all(value, "tp", 0, 0, tiled=True, axis_index_groups=PLANES)


def shards(
    ssm_input,
    dt_raw,
    b_proj,
    c_proj,
    dt_bias,
    decay_rate,
    skip_gain,
    doc_start,
    out_weight,
    grad_out,
):
    share, width = grad_out.shape
    n_ctx = lax.axis_size("ctx")
    n_tp = lax.axis_size("tp")
    core = lax.axis_index("tp") % 2
    b = b_proj.reshape(ROWS, STATE)
    c = c_proj.reshape(ROWS, STATE)
    grad_full = lax.all_gather(grad_out, "tp", axis=0, tiled=True)
    payload, rows, tab = states(
        dt_bias, decay_rate, ssm_input, dt_raw.T, doc_start.reshape(1, ROWS), b
    )
    carried, decay = prefix(lax.all_to_all(payload, "ctx", 0, 0, tiled=True))
    carried = lax.all_to_all(carried, "ctx", 0, 0, tiled=True)
    mixed, inner = mixer(skip_gain, ssm_input, b, c, rows, tab, carried)

    mixed_all = lax.all_gather(mixed, "ctx", axis=0, tiled=True)
    columns = lax.all_to_all(grad_out, "ctx", 1, 0, tiled=True)
    own = over_planes(jnp.broadcast_to(columns, (4,) + columns.shape))
    other = lax.ppermute(own, "tp", SWAP)

    partial = nn(mixed, out_weight).astype(BF16).reshape(n_tp // 2, 2, share, width)
    keep = lax.dynamic_index_in_dim(partial, core, 1, False)
    send = lax.dynamic_index_in_dim(partial, 1 - core, 1, False)
    both = keep.astype(F32) + lax.ppermute(send, "tp", SWAP).astype(F32)
    layer_out = jnp.sum(over_planes(both.astype(BF16)).astype(F32), axis=0).astype(BF16)

    grad_mix = nt(grad_full, out_weight).astype(BF16)
    after = suffix(
        lax.all_to_all(local_grad(grad_mix, c, tab), "ctx", 0, 0, tiled=True), decay
    )
    after = lax.all_to_all(after, "ctx", 0, 0, tiled=True)
    grad_x, grad_dt, grad_b, grad_c = backward(
        skip_gain, decay_rate, ssm_input, b, c, rows, tab, carried, inner, grad_mix, after
    )
    weight = weight_grad(
        core.reshape(1),
        own,
        other,
        mixed_all.reshape(n_ctx, n_tp // 2, 2, share, WIDE),
    )
    return (
        layer_out,
        grad_x,
        grad_dt.T,
        grad_b.reshape(ROWS, 1, STATE),
        grad_c.reshape(ROWS, 1, STATE),
        weight,
    )


def solution(mesh):
    in_specs = (
        P("ctx", "tp"),
        P("ctx", "tp"),
        P("ctx", "tp", None),
        P("ctx", "tp", None),
        P("tp"),
        P("tp"),
        P("tp"),
        P("ctx"),
        P("tp", None),
        P(("ctx", "tp"), None),
    )
    out_specs = (
        P(("ctx", "tp"), None),
        P("ctx", "tp"),
        P("ctx", "tp"),
        P("ctx", "tp", None),
        P("ctx", "tp", None),
        P("ctx", "tp"),
    )
    return jax.shard_map(shards, mesh=mesh, in_specs=in_specs, out_specs=out_specs, check_vma=False)
```

time: 455 us -> 208 us (0.46)
  waiting for transfers between devices: 235 us -> 49.6 us
  other arithmetic: 83.2 us -> 7.02 us
  matrix products: 71 us -> 23.4 us
  starting transfers between devices: 0.6 us -> 33.9 us
  Pallas kernels: 0 us -> 25.4 us
  blocking collectives: 18.4 us -> 31.2 us
  local copies, waits for them, and re-layouts: 26.8 us -> 21 us
    all_gather x2 -> x1, waiting for transfers between devices: 109 us -> 0.01 us  [shards(): mixed_all = lax.all_gather(mixed, 'ctx', axis=0, tiled=True)]
    reduce_scatter x2 -> x0, waiting for transfers between devices: 91.9 us -> none  [the longest x1 56.1 us: shards(): lax.psum_scatter(lax.dot_general(grad_full, mixer_bf, (((0,), (0,)), ((),...]
    all_to_all x0 -> x5, waiting for transfers between devices: none -> 48.8 us  [the longest x2 25.1 us: over_planes(): lax.all_to_all(value, 'tp', 0, 0, tiled=True, axis_index_groups=PLANES)]
    dot_general x15 -> x2, matrix products: 71 us -> 23.4 us  [dot(): lax.dot_general(a, b, (dims, ((), ())), precision=precision, preferred_el...]
    select_n x32 -> x0, other arithmetic: 41.2 us -> none  [step(): return jax.tree.map(lambda a, b: jnp.where(reached, a, b), new, before)]
    all_gather x1, waiting for transfers between devices: 33.5 us -> 0.01 us  [shards(): grad_full = lax.all_gather(grad_out, 'tp', axis=0, tiled=True)]
    all_to_all x0 -> x2, blocking collectives: none -> 31.2 us  [the longest x1 18.7 us: shards(): carried, decay = prefix(lax.all_to_all(payload, 'ctx', 0, 0, tiled=True))]
    pallas_call x0 -> x7, Pallas kernels: none -> 25.4 us  [the longest x1 10.6 us: weight_grad(): pl.pallas_call(weight_kernel, grid=(slabs // block,), in_specs=[pl.BlockS...]
  transfers between devices with their start and end apart: 5 -> 9, of which waited for: 5 -> 5; matrix products, arithmetic and copies ran while one was open for 16% -> 17% of each run, Pallas kernels for 0% -> 7%
where the time goes in v1:
time: 208 us; the launch traced here: 206 us
  waiting for transfers between devices  49.6 us (24%)
  starting transfers between devices  33.9 us (16%)
  blocking collectives  31.2 us (15%)
  Pallas kernels  25.4 us (12%)
  matrix products  23.4 us (11%)
  local copies, waits for them, and re-layouts  21 us (10%)
  between operations  14.2 us (7%)
  other arithmetic  7.02 us (3%)
    all_to_all x2, waiting for transfers between devices, over_planes(): lax.all_to_all(value, 'tp', 0, 0, tiled=True, axis_index_groups=PLANES)  25.1 us
    dot_general x2, matrix products, dot(): lax.dot_general(a, b, (dims, ((), ())), precision=precision, preferred_el...  23.4 us
    all_to_all x1, blocking collectives, shards(): carried, decay = prefix(lax.all_to_all(payload, 'ctx', 0, 0, tiled=True))  18.7 us
    unnamed x48, local copies, waits for them, and re-layouts  17.1 us
    all_to_all x1, blocking collectives, shards(): carried = lax.all_to_all(carried, 'ctx', 0, 0, tiled=True)  12.6 us
    pallas_call x1, Pallas kernels, weight_grad(): pl.pallas_call(weight_kernel, grid=(slabs // block,), in_specs=[pl.BlockS...  10.6 us
    all_to_all x2, starting transfers between devices, over_planes(): lax.all_to_all(value, 'tp', 0, 0, tiled=True, axis_index_groups=PLANES)  9.47 us
    all_to_all x1, waiting for transfers between devices, shards(): columns = lax.all_to_all(grad_out, 'ctx', 1, 0, tiled=True)  8.94 us
  transfers between devices with their start and end apart: 9, of which 5 were waited for; matrix products, arithmetic and copies ran while one was open for 17% of the time, Pallas kernels for 7%

profile of v1, /device:TPU:1, one launch (start us, length us, event | category | flops | bytes accessed | tf_op | source)
XLA Modules:
  0.0 205.7 jit_solution(17662508005890405358)
XLA Ops:
  8.0 1.0 copy-done
  12.6 2.2 %shard_map.145 = (bf16[16,72,256]{2,1,0:T(8,128)(2,1)S(1)}, f32[128,256]{1,0:T(8,128)S(1)}, f32[256,128]{1,0:T(8,128)S(1)}) custom-call(f32[16]{0:T(128)S(1)} %copy-done.21, f32[16]{0:T(128)S(1)} %copy-done.18, bf16[256,1024]{1,0:T(8,128)(2,1)S(1)} %copy-done, f32[16,256]{1,0:T(8,128)S(1)} %bitcast.32, s32[1,256]{1,0:T(1,128)S(1)} %bitcast.33, ...), custom_call_target="tpu_custom_call" | custom-call | tf_op jit(solution)/shard_map/pallas_call | solution.py:106
  14.8 18.7 %all_to_all.49.got = bf16[16,72,256]{2,1,0:T(8,128)(2,1)S(1)} all-to-all(bf16[16,72,256]{2,1,0:T(8,128)(2,1)S(1)} %get-tuple-element.19), channel_id=1, replica_groups=mesh['ctx'=16,'tp'=8] {'ctx'}, dimensions={0} | all-to-all | bytes 1179648 | tf_op jit(solution)/shard_map/all_to_all | solution.py:384
  33.6 12.6 %all_to_all.50.carried = bf16[16,64,256]{2,1,0:T(8,128)(2,1)S(1)} all-to-all(bf16[16,64,256]{2,1,0:T(8,128)(2,1)S(1)} %get-tuple-element.20), channel_id=1, replica_groups=mesh['ctx'=16,'tp'=8] {'ctx'}, dimensions={0} | all-to-all | bytes 1048576 | tf_op jit(solution)/shard_map/all_to_all | solution.py:385
  48.6 3.6 %shard_map.147 = (bf16[256,1024]{1,0:T(8,128)(2,1)}, f32[256,1024]{1,0:T(8,128)S(1)}) custom-call(f32[16]{0:T(128)S(1)} %copy-done.16, bf16[256,1024]{1,0:T(8,128)(2,1)S(1)} %copy-done.1, bf16[256,256]{1,0:T(8,128)(2,1)S(1)} %bitcast.30, bf16[256,256]{1,0:T(8,128)(2,1)S(1)} %bitcast.26, f32[128,256]{1,0:T(8,128)S(1)} %get-tuple-element.17.rows, ...), custom_call_target="tpu_custom_call" | custom-call | tf_op jit(solution)/shard_map/pallas_call | solution.py:185
  52.2 1.0 copy-done.11
  54.0 3.6 %all-to-all-start.5 = ((bf16[32,16,512]{2,0,1:T(8,128)(2,1)}), bf16[32,16,512]{2,0,1:T(8,128)(2,1)S(1)}, u32[]{:S(2)}, u32[]{:S(2)}) async-start(bf16[32,16,512]{2,0,1:T(8,128)(2,1)} %bitcast.25), calls=%async_computation.5 | async-start | bytes 1048576 | tf_op jit(solution)/shard_map/all_to_all | solution.py:389
  57.6 8.9 %all-to-all-done.5 = bf16[32,16,512]{2,0,1:T(8,128)(2,1)S(1)} async-done(((bf16[32,16,512]{2,0,1:T(8,128)(2,1)}), bf16[32,16,512]{2,0,1:T(8,128)(2,1)S(1)}, u32[]{:S(2)}, u32[]{:S(2)}) %all-to-all-start.5) | async-done | bytes 524320 | tf_op jit(solution)/shard_map/all_to_all | solution.py:389
  66.6 1.5 broadcast_in_dim.3
  68.0 5.0 %all-to-all-start.6 = ((bf16[4,512,512]{2,1,0:T(8,128)(2,1)}), bf16[4,512,512]{2,1,0:T(8,128)(2,1)S(1)}, u32[]{:S(2)}, u32[]{:S(2)}) async-start(bf16[4,512,512]{2,1,0:T(8,128)(2,1)} %broadcast_in_dim.3), calls=%async_computation.6 | async-start | bytes 4194304 | tf_op jit(solution)/shard_map/all_to_all | solution.py:359
  73.1 10.6 %convolution_convert_fusion = bf16[256,8192]{1,0:T(8,128)(2,1)S(1)} fusion(bf16[256,1024]{1,0:T(8,128)(2,1)} %get-tuple-element.21, bf16[1024,8192]{1,0:T(8,128)(2,1)} %param.18), kind=kOutput, calls=%fused_computation | convolution fusion | flops 4297064448 | bytes 21495808 | tf_op jit(solution)/shard_map/dot_general | solution.py:23
  83.7 1.9 copy-done.22
  85.6 1.5 dynamic-slice_bitcast_fusion
  87.1 5.4 %collective-permute-start = (bf16[4,32,8192]{2,1,0:T(8,128)(2,1)}, bf16[4,32,8192]{2,1,0:T(8,128)(2,1)}, u32[]{:S(2)}, u32[]{:S(2)}) collective-permute-start(bf16[4,32,8192]{2,1,0:T(8,128)(2,1)} %dynamic-slice_bitcast_fusion), channel_id=1, source_target_pairs={{0,1},{1,0},{2,3},{3,2},{4,5},{5,4},{6,7},{7,6},{8,9},{9,8},{10,11... | collective-permute-start | bytes 6291464 | tf_op jit(solution)/shard_map/ppermute | solution.py:396
  92.5 1.2 all-to-all-done.6.own
  93.7 6.7 %collective-permute-start.1 = (bf16[4,512,512]{2,1,0:T(8,128)(2,1)S(1)}, bf16[4,512,512]{2,1,0:T(8,128)(2,1)}, u32[]{:S(2)}, u32[]{:S(2)}) collective-permute-start(bf16[4,512,512]{2,1,0:T(8,128)(2,1)S(1)} %all-to-all-done.6.own), channel_id=1, source_target_pairs={{0,1},{1,0},{2,3},{3,2},{4,5},{5,4},{6,7},{7,6},{8,9},{9,8},{10,11... | collective-permute-start | bytes 6291464 | tf_op jit(solution)/shard_map/ppermute | solution.py:391
  100.4 12.8 %convolution_convert_fusion.1.grad = bf16[256,1024]{1,0:T(8,128)(2,1)} fusion(bf16[256,8192]{1,0:T(8,128)(2,1)} %all-gather.3.cloned.1.call-done, bf16[1024,8192]{1,0:T(8,128)(2,1)} %param.18), kind=kOutput, calls=%fused_computation.4 | convolution fusion | flops 4295229440 | bytes 21495808 | tf_op jit(solution)/shard_map/dot_general | solution.py:23
  113.1 1.0 copy-done.4
  114.2 1.3 shard_map.148
  116.3 4.3 %all-to-all-start.3 = ((bf16[16,64,256]{2,1,0:T(8,128)(2,1)}), bf16[16,64,256]{2,1,0:T(8,128)(2,1)}, u32[]{:S(2)}, u32[]{:S(2)}) async-start(bf16[16,64,256]{2,1,0:T(8,128)(2,1)} %copy-done.3), calls=%async_computation.3 | async-start | bytes 1048576 | tf_op jit(solution)/shard_map/all_to_all | solution.py:401
  120.6 4.2 %fusion = bf16[4,32,8192]{2,1,0:T(8,128)(2,1)} fusion(bf16[4,32,8192]{2,1,0:T(8,128)(2,1)} %collective-permute-done, bf16[4,2,32,8192]{3,2,1,0:T(8,128)(2,1)} %bitcast.36, s32[]{:T(128)S(6)} %select_n.15), kind=kLoop, calls=%fused_computation.2 | loop fusion | flops 4194304 | bytes 6291460 | tf_op jit(solution)/shard_map/convert_element_type | solution.py:397
  124.7 7.8 %all-to-all-done.3.got = bf16[16,64,256]{2,1,0:T(8,128)(2,1)} async-done(((bf16[16,64,256]{2,1,0:T(8,128)(2,1)}), bf16[16,64,256]{2,1,0:T(8,128)(2,1)}, u32[]{:S(2)}, u32[]{:S(2)}) %all-to-all-start.3) | async-done | bytes 524320 | tf_op jit(solution)/shard_map/all_to_all | solution.py:401
  132.5 4.4 %all-to-all-start.2 = ((bf16[4,32,8192]{2,1,0:T(8,128)(2,1)}), bf16[4,32,8192]{2,1,0:T(8,128)(2,1)}, u32[]{:S(2)}, u32[]{:S(2)}) async-start(bf16[4,32,8192]{2,1,0:T(8,128)(2,1)} %fusion), calls=%async_computation.2 | async-start | bytes 4194304 | tf_op jit(solution)/shard_map/all_to_all | solution.py:359
  137.0 1.2 shard_map.149
  138.9 23.9 %all-to-all-done.2 = bf16[4,32,8192]{2,1,0:T(8,128)(2,1)} async-done(((bf16[4,32,8192]{2,1,0:T(8,128)(2,1)}), bf16[4,32,8192]{2,1,0:T(8,128)(2,1)}, u32[]{:S(2)}, u32[]{:S(2)}) %all-to-all-start.2) | async-done | bytes 2097184 | tf_op jit(solution)/shard_map/all_to_all | solution.py:359
  162.8 4.5 %all-to-all-start.4 = ((bf16[16,64,256]{2,1,0:T(8,128)(2,1)}), bf16[16,64,256]{2,1,0:T(8,128)(2,1)}, u32[]{:S(2)}, u32[]{:S(2)}) async-start(bf16[16,64,256]{2,1,0:T(8,128)(2,1)} %copy-done.2), calls=%async_computation.4 | async-start | bytes 1048576 | tf_op jit(solution)/shard_map/all_to_all | solution.py:403
  167.3 2.8 %reduce_sum.12 = bf16[32,8192]{1,0:T(8,128)(2,1)} reduce(bf16[4,32,8192]{2,1,0:T(8,128)(2,1)} %all-to-all-done.2, bf16[]{:T(256)} %constant.28.clone.1), dimensions={0}, to_apply=%region_0.1 | reduce | flops 786432 | bytes 2621442 | tf_op jit(solution)/shard_map/reduce_sum | solution.py:397
  170.2 7.0 %all-to-all-done.4.after = bf16[16,64,256]{2,1,0:T(8,128)(2,1)} async-done(((bf16[16,64,256]{2,1,0:T(8,128)(2,1)}), bf16[16,64,256]{2,1,0:T(8,128)(2,1)}, u32[]{:S(2)}, u32[]{:S(2)}) %all-to-all-start.4) | async-done | bytes 524320 | tf_op jit(solution)/shard_map/all_to_all | solution.py:403
  177.2 1.0 copy-done.5
  178.3 1.2 copy-done.12
  181.7 6.6 %shard_map.150 = (bf16[256,1024]{1,0:T(8,128)(2,1)}, f32[16,256]{1,0:T(8,128)}, bf16[256,256]{1,0:T(8,128)(2,1)}, bf16[256,256]{1,0:T(8,128)(2,1)}) custom-call(f32[16]{0:T(128)S(1)} %copy-done.17, f32[16]{0:T(128)S(1)} %copy-done.19, bf16[256,1024]{1,0:T(8,128)(2,1)S(1)} %copy-done.1, bf16[256,256]{1,0:T(8,128)(2,1)S(1)} %bitcast.31, ...), custom_call_target="tpu_custom_call" | custom-call | tf_op jit(solution)/shard_map/pallas_call | solution.py:294
  188.3 10.6 %shard_map.151 = bf16[512,1024]{1,0:T(8,128)(2,1)} custom-call(s32[1]{0:T(128)} %bitcast.10.core, bf16[4,512,512]{2,1,0:T(8,128)(2,1)S(1)} %all-to-all-done.6.own, bf16[4,512,512]{2,1,0:T(8,128)(2,1)} %collective-permute-done.1.other, bf16[16,4,2,32,1024]{4,3,2,1,0:T(8,128)(2,1)} %bitcast.34), custom_call_target="tpu_custom_call" | custom-call | tf_op jit(solution)/shard_map/pallas_call | solution.py:338
  (52 shorter events, 11.7 us)
Async XLA Ops:
  7.2 39.0 %copy-start.1 = (bf16[256,1024]{1,0:T(8,128)(2,1)S(1)}, bf16[256,1024]{1,0:T(8,128)(2,1)}, u32[]{:S(2)}) copy-start(bf16[256,1024]{1,0:T(8,128)(2,1)} %x.5) | copy-start | bytes 1572868
  7.2 93.2 %all-gather.3.cloned.1.call-start = ((), (), s32[]{:S(2)}) async-start(), calls=%async_computation.7 | async-start | bytes 4718592 | tf_op jit(solution)/shard_map/all_gather | solution.py:380
  7.9 180.4 %all-gather.5.cloned.1.call-start = ((), (), s32[]{:S(2)}) async-start(), calls=%async_computation.8 | async-start | bytes 8912896 | tf_op jit(solution)/shard_map/all_gather | solution.py:388
  8.0 1.0 copy-start
  9.0 0.9 copy-start.8
  9.9 0.7 copy-start.15
  10.6 0.7 copy-start.18
  11.3 0.7 copy-start.20
  12.0 0.7 copy-start.21
  12.6 40.6 %copy-start.23 = (bf16[32,8192]{1,0:T(8,128)(2,1)S(1)}, bf16[32,8192]{1,0:T(8,128)(2,1)}, u32[]{:S(2)}) copy-start(bf16[32,8192]{1,0:T(8,128)(2,1)} %param.19) | copy-start | bytes 1572868
  14.8 37.4 %copy-start.13 = (f32[128,256]{1,0:T(8,128)}, f32[128,256]{1,0:T(8,128)S(1)}, u32[]{:S(2)}) copy-start(f32[128,256]{1,0:T(8,128)S(1)} %get-tuple-element.17.rows) | copy-start | bytes 393220
  46.2 0.9 copy-start.6
  47.1 0.9 copy-start.9
  48.0 0.7 copy-start.16
  52.2 1.0 copy-start.11
  54.0 12.5 %all-to-all-start.5 = ((bf16[32,16,512]{2,0,1:T(8,128)(2,1)}), bf16[32,16,512]{2,0,1:T(8,128)(2,1)S(1)}, u32[]{:S(2)}, u32[]{:S(2)}) async-start(bf16[32,16,512]{2,0,1:T(8,128)(2,1)} %bitcast.25), calls=%async_computation.5 | async-start | bytes 1048576 | tf_op jit(solution)/shard_map/all_to_all | solution.py:389
  68.0 25.6 %all-to-all-start.6 = ((bf16[4,512,512]{2,1,0:T(8,128)(2,1)}), bf16[4,512,512]{2,1,0:T(8,128)(2,1)S(1)}, u32[]{:S(2)}, u32[]{:S(2)}) async-start(bf16[4,512,512]{2,1,0:T(8,128)(2,1)} %broadcast_in_dim.3), calls=%async_computation.6 | async-start | bytes 4194304 | tf_op jit(solution)/shard_map/all_to_all | solution.py:359
  83.7 1.9 copy-start.22
  87.1 33.4 %collective-permute-start = (bf16[4,32,8192]{2,1,0:T(8,128)(2,1)}, bf16[4,32,8192]{2,1,0:T(8,128)(2,1)}, u32[]{:S(2)}, u32[]{:S(2)}) collective-permute-start(bf16[4,32,8192]{2,1,0:T(8,128)(2,1)} %dynamic-slice_bitcast_fusion), channel_id=1, source_target_pairs={{0,1},{1,0},{2,3},{3,2},{4,5},{5,4},{6,7},{7,6},{8,9},{9,8},{10,11... | collective-permute-start | bytes 6291464 | tf_op jit(solution)/shard_map/ppermute | solution.py:396
  92.5 20.6 %copy-start.7 = (bf16[256,1,256]{2,0,1:T(8,128)(2,1)S(1)}, bf16[256,1,256]{2,0,1:T(8,128)(2,1)}, u32[]{:S(2)}) copy-start(bf16[256,1,256]{2,0,1:T(8,128)(2,1)} %param.13) | copy-start | bytes 393220
  93.7 94.6 %collective-permute-start.1 = (bf16[4,512,512]{2,1,0:T(8,128)(2,1)S(1)}, bf16[4,512,512]{2,1,0:T(8,128)(2,1)}, u32[]{:S(2)}, u32[]{:S(2)}) collective-permute-start(bf16[4,512,512]{2,1,0:T(8,128)(2,1)S(1)} %all-to-all-done.6.own), channel_id=1, source_target_pairs={{0,1},{1,0},{2,3},{3,2},{4,5},{5,4},{6,7},{7,6},{8,9},{9,8},{10,11... | collective-permute-start | bytes 6291464 | tf_op jit(solution)/shard_map/ppermute | solution.py:391
  113.1 1.0 copy-start.4
  115.5 0.8 copy-start.3
  116.3 16.2 %all-to-all-start.3 = ((bf16[16,64,256]{2,1,0:T(8,128)(2,1)}), bf16[16,64,256]{2,1,0:T(8,128)(2,1)}, u32[]{:S(2)}, u32[]{:S(2)}) async-start(bf16[16,64,256]{2,1,0:T(8,128)(2,1)} %copy-done.3), calls=%async_computation.3 | async-start | bytes 1048576 | tf_op jit(solution)/shard_map/all_to_all | solution.py:401
  124.7 52.5 %copy-start.10 = (bf16[256,1,256]{2,0,1:T(8,128)(2,1)S(1)}, bf16[256,1,256]{2,0,1:T(8,128)(2,1)}, u32[]{:S(2)}) copy-start(bf16[256,1,256]{2,0,1:T(8,128)(2,1)} %param.12) | copy-start | bytes 393220
  132.5 30.3 %all-to-all-start.2 = ((bf16[4,32,8192]{2,1,0:T(8,128)(2,1)}), bf16[4,32,8192]{2,1,0:T(8,128)(2,1)}, u32[]{:S(2)}, u32[]{:S(2)}) async-start(bf16[4,32,8192]{2,1,0:T(8,128)(2,1)} %fusion), calls=%async_computation.2 | async-start | bytes 4194304 | tf_op jit(solution)/shard_map/all_to_all | solution.py:359
  138.1 0.8 copy-start.2
  162.8 14.4 %all-to-all-start.4 = ((bf16[16,64,256]{2,1,0:T(8,128)(2,1)}), bf16[16,64,256]{2,1,0:T(8,128)(2,1)}, u32[]{:S(2)}, u32[]{:S(2)}) async-start(bf16[16,64,256]{2,1,0:T(8,128)(2,1)} %copy-done.2), calls=%async_computation.4 | async-start | bytes 1048576 | tf_op jit(solution)/shard_map/all_to_all | solution.py:403
  177.2 1.0 copy-start.5
  178.3 1.2 copy-start.12
  179.5 0.9 copy-start.14
  180.4 0.7 copy-start.17
  (1 other events, 0.7 us)
Sparse Core Ops, SparseCore 0:
  9.7 35.9 all-gather.2
  53.3 71.5 all-gather.4

commit v2 on v1

--- a/solution.py
+++ b/solution.py
@@ -35,16 +35,57 @@
     return dot(a, b, ((0,), (0,)))
 
 
-def vmem(n):
-    return [pl.BlockSpec(memory_space=pltpu.VMEM)] * n
-
-
 def smem(n):
     return [pl.BlockSpec(memory_space=pltpu.SMEM)] * n
 
 
+def hbm(n):
+    return [pl.BlockSpec(memory_space=pltpu.HBM)] * n
+
+
+def pinned(*arrays):
+    return [pltpu.with_memory_space_constraint(a, pltpu.HBM) for a in arrays]
+
+
+def staged(kernel, scalars, arrays, outs):
+    given = list(scalars) + list(arrays)
+    n, m = len(given), len(outs)
+
+    def body(*refs):
+        sources, results, local, sems = refs[:n], refs[n : n + m], refs[n + m : -1], refs[-1]
+        copies = [
+            pltpu.make_async_copy(a, b, sems.at[i])
+            for i, (a, b) in enumerate(zip(sources, local[:n], strict=True))
+        ]
+        for copy in copies:
+            copy.start()
+        for copy in copies:
+            copy.wait()
+        kernel(*local)
+        copies = [
+            pltpu.make_async_copy(a, b, sems.at[n + i])
+            for i, (a, b) in enumerate(zip(local[n:], results, strict=True))
+        ]
+        for copy in copies:
+            copy.start()
+        for copy in copies:
+            copy.wait()
+
+    return pl.pallas_call(
+        body,
+        in_specs=hbm(n),
+        out_specs=hbm(m),
+        out_shape=tuple(jax.ShapeDtypeStruct(*out) for out in outs),
+        scratch_shapes=[pltpu.SMEM(a.shape, a.dtype) for a in scalars]
+        + [pltpu.VMEM(a.shape, a.dtype) for a in arrays]
+        + [pltpu.VMEM(*out) for out in outs]
+        + [pltpu.SemaphoreType.DMA((n + m,))],
+        compiler_params=params(),
+    )(*given)
+
+
 def params():
-    return pltpu.CompilerParams(vmem_limit_bytes=48 * 1024 * 1024)
+    return pltpu.CompilerParams(vmem_limit_bytes=32 * 1024 * 1024)
 
 
 def iota(shape, axis):
@@ -103,17 +144,12 @@
 
 
 def states(bias, rate, x, dt, doc, b):
-    return pl.pallas_call(
-        states_kernel,
-        in_specs=smem(2) + vmem(4),
-        out_specs=vmem(3),
-        out_shape=(
-            jax.ShapeDtypeStruct((HEADS, DIM + EXTRA, STATE), BF16),
-            jax.ShapeDtypeStruct((8 * HEADS, ROWS), F32),
-            jax.ShapeDtypeStruct((ROWS, 8 * HEADS), F32),
-        ),
-        compiler_params=params(),
-    )(bias, rate, x, dt, doc, b)
+    outs = [
+        ((HEADS, DIM + EXTRA, STATE), BF16),
+        ((8 * HEADS, ROWS), F32),
+        ((ROWS, 8 * HEADS), F32),
+    ]
+    return staged(states_kernel, (bias, rate), (x, dt, doc, b), outs)
 
 
 def prefix_kernel(got, out, decay):
@@ -129,16 +165,8 @@
 
 def prefix(got):
     slabs = got.shape[0]
-    return pl.pallas_call(
-        prefix_kernel,
-        in_specs=vmem(1),
-        out_specs=vmem(2),
-        out_shape=(
-            jax.ShapeDtypeStruct((slabs, DIM, STATE), BF16),
-            jax.ShapeDtypeStruct((slabs, STATE), F32),
-        ),
-        compiler_params=params(),
-    )(got)
+    outs = [((slabs, DIM, STATE), BF16), ((slabs, STATE), F32)]
+    return staged(prefix_kernel, (), (got,), outs)
 
 
 def suffix_kernel(got, decay, out):
@@ -150,13 +178,7 @@
 
 
 def suffix(got, decay):
-    return pl.pallas_call(
-        suffix_kernel,
-        in_specs=vmem(2),
-        out_specs=vmem(1)[0],
-        out_shape=jax.ShapeDtypeStruct(got.shape, BF16),
-        compiler_params=params(),
-    )(got, decay)
+    return staged(suffix_kernel, (), (got, decay), [(got.shape, BF16)])[0]
 
 
 def mixer_kernel(skip, x, b, c, rows, tab_ref, carried, mixed, inner):
@@ -182,35 +204,8 @@
 
 
 def mixer(skip, x, b, c, rows, tab, carried):
-    return pl.pallas_call(
-        mixer_kernel,
-        in_specs=smem(1) + vmem(6),
-        out_specs=vmem(2),
-        out_shape=(
-            jax.ShapeDtypeStruct((ROWS, WIDE), BF16),
-            jax.ShapeDtypeStruct((ROWS, WIDE), F32),
-        ),
-        compiler_params=params(),
-    )(skip, x, b, c, rows, tab, carried)
-
-
-def local_grad_kernel(grad, c, tab_ref, out):
-    tab = tab_ref[...]
-    for j in range(PAIRS):
-        weighted = (grad[:, cols_of(j)].astype(F32) * pair_cols(tab, ENTRY, j)).astype(BF16)
-        state = tn(weighted, c[...]).astype(BF16)
-        out[2 * j] = state[:DIM]
-        out[2 * j + 1] = state[DIM:]
-
-
-def local_grad(grad, c, tab):
-    return pl.pallas_call(
-        local_grad_kernel,
-        in_specs=vmem(3),
-        out_specs=vmem(1)[0],
-        out_shape=jax.ShapeDtypeStruct((HEADS, DIM, STATE), BF16),
-        compiler_params=params(),
-    )(grad, c, tab)
+    outs = [((ROWS, WIDE), BF16), ((ROWS, WIDE), F32)]
+    return staged(mixer_kernel, (skip,), (x, b, c, rows, tab, carried), outs)
 
 
 def head_sums(pair, values):
@@ -291,72 +286,173 @@
 
 
 def backward(skip, rate, x, b, c, rows, tab, carried, inner, grad, after):
-    return pl.pallas_call(
-        backward_kernel,
-        in_specs=smem(2) + vmem(9),
-        out_specs=vmem(4),
-        out_shape=(
-            jax.ShapeDtypeStruct((ROWS, WIDE), BF16),
-            jax.ShapeDtypeStruct((HEADS, ROWS), F32),
-            jax.ShapeDtypeStruct((ROWS, STATE), BF16),
-            jax.ShapeDtypeStruct((ROWS, STATE), BF16),
-        ),
-        compiler_params=params(),
-    )(skip, rate, x, b, c, rows, tab, carried, inner, grad, after)
-
-
-def weight_kernel(core, own, other, mixed, out, acc):
+    outs = [
+        ((ROWS, WIDE), BF16),
+        ((HEADS, ROWS), F32),
+        ((ROWS, STATE), BF16),
+        ((ROWS, STATE), BF16),
+    ]
+    arrays = (x, b, c, rows, tab, carried, inner, grad, after)
+    return staged(backward_kernel, (skip, rate), arrays, outs)
+
+
+NEAR_FAR = (0, 1, 3, 2)
+
+
+def project_kernel(
+    place, grad, mixed, weight, rows, c, keep, send, grad_mix, out, ordered, acc
+):
     at = pl.program_id(0)
+    plane, core = place[0], place[1]
+    planes, _, share, _ = mixed.shape
 
     @pl.when(at == 0)
     def _():
         acc[...] = jnp.zeros_like(acc)
-
-    mine = core[0]
-    slabs, planes, _, share, wide = mixed.shape
-    total = None
-    for source, which in ((own, mine), (other, 1 - mine)):
-        left = jnp.concatenate(
-            [source[z, k * share : (k + 1) * share] for k in range(slabs) for z in range(planes)], 0
-        )
-        right = jnp.concatenate(
-            [mixed[k, z, which] for k in range(slabs) for z in range(planes)], 0
-        )
-        part = tn(left, right)
-        total = part if total is None else total + part
-    acc[...] += total
+        for k, step in enumerate(NEAR_FAR):
+            to = (plane + step) % planes
+            ordered[k * share : (k + 1) * share] = mixed[to, core]
+            ordered[(planes + k) * share : (planes + k + 1) * share] = mixed[to, 1 - core]
+
+    acc[...] += nt(weight[...], grad[...])
+    both = nn(ordered[...], weight[...]).astype(BF16)
+    keep[...] = both[: planes * share].reshape(keep.shape)
+    send[...] = both[planes * share :].reshape(send.shape)
+
+    @pl.when(at == pl.num_programs(0) - 1)
+    def _():
+        for h in range(HEADS):
+            part = acc[h * DIM : (h + 1) * DIM].astype(BF16)
+            entry = rows[ENTRY * HEADS + h : ENTRY * HEADS + h + 1, :]
+            out[h] = nn((part.astype(F32) * entry).astype(BF16), c[...]).astype(BF16)
+        for j in range(PAIRS):
+            grad_mix[:, cols_of(j)] = acc[cols_of(j)].T.astype(BF16)
+
+
+def project(place, grad, mixed, weight, rows, c):
+    inner, width = weight.shape
+    planes, sides, share, _ = mixed.shape
+    tile = 1024
+    fixed = lambda s: pl.BlockSpec(s, lambda i, r=len(s): (0,) * r)
+    half = pl.BlockSpec((planes, share, tile), lambda i: (0, 0, i))
+    tall = pl.BlockSpec((inner, tile), lambda i: (0, i))
+    local = (HEADS, DIM, STATE)
+    return pl.pallas_call(
+        project_kernel,
+        grid=(width // tile,),
+        in_specs=smem(1)
+        + [pl.BlockSpec((ROWS, tile), lambda i: (0, i)), fixed(mixed.shape), tall]
+        + [fixed(rows.shape), fixed(c.shape)],
+        out_specs=[half, half, fixed((ROWS, inner)), fixed(local)],
+        out_shape=(
+            jax.ShapeDtypeStruct((planes, share, width), BF16),
+            jax.ShapeDtypeStruct((planes, share, width), BF16),
+            jax.ShapeDtypeStruct((ROWS, inner), BF16),
+            jax.ShapeDtypeStruct(local, BF16),
+        ),
+        scratch_shapes=[pltpu.VMEM((ROWS, inner), BF16), pltpu.VMEM((inner, ROWS), F32)],
+        compiler_params=params(),
+    )(place, grad, mixed, weight, rows, c)
+
+
+def arrange_kernel(place, *refs):
+    pieces, out, tokens, sems = refs[:10], refs[10], refs[11], refs[12]
+    slabs, sides, share, cols = tokens.shape
+    copies = []
+    for side in range(2):
+        core = place[1] if side == 0 else 1 - place[1]
+        steps = (0, 3, 1, 2, 2)
+        for k, piece in enumerate(pieces[side * 5 : side * 5 + 5]):
+            at = 2 * ((place[0] + steps[k]) % 4) + core
+            half = slabs // 2
+            low, many = ((0, slabs), (0, slabs), (0, slabs), (0, half), (half, half))[k]
+            target = tokens.at[low : low + many, at]
+            copies.append(pltpu.make_async_copy(piece, target, sems.at[side * 5 + k]))
+    for copy in copies:
+        copy.start()
+    for copy in copies:
+        copy.wait()
+    wide = sides * share
+    for k in range(slabs):
+        out[:, k * wide : (k + 1) * wide] = tokens[k].reshape(wide, cols).T
+
+
+def arrange(place, pieces, slabs):
+    share = 32
+    cols = pieces[0].shape[1]
+    views = [p.reshape(-1, share, cols) for p in pieces]
+    return pl.pallas_call(
+        arrange_kernel,
+        in_specs=smem(1) + hbm(len(views)),
+        out_specs=pl.BlockSpec(memory_space=pltpu.VMEM),
+        out_shape=jax.ShapeDtypeStruct((cols, slabs * 8 * share), BF16),
+        scratch_shapes=[
+            pltpu.VMEM((slabs, 8, share, cols), BF16),
+            pltpu.SemaphoreType.DMA((len(views),)),
+        ],
+        compiler_params=params(),
+    )(place, *views)
+
+
+def weight_kernel(left, right, out, acc):
+    at = pl.program_id(0)
+
+    @pl.when(at == 0)
+    def _():
+        acc[...] = nn(left[...], right[...])
+
+    @pl.when(at > 0)
+    def _():
+        acc[...] += nn(left[...], right[...])
 
     @pl.when(at == pl.num_programs(0) - 1)
     def _():
         out[...] = acc[...].astype(BF16)
 
 
-def weight_grad(core, own, other, mixed):
-    planes, spread, cols = own.shape
-    slabs, _, _, share, wide = mixed.shape
-    block = 2
+def weight_grad(left, right):
+    cols, deep = left.shape
+    wide = right.shape[1]
+    tile = 512
     return pl.pallas_call(
         weight_kernel,
-        grid=(slabs // block,),
+        grid=(deep // tile,),
         in_specs=[
-            pl.BlockSpec(memory_space=pltpu.SMEM),
-            pl.BlockSpec((planes, block * share, cols), lambda i: (0, i, 0)),
-            pl.BlockSpec((planes, block * share, cols), lambda i: (0, i, 0)),
-            pl.BlockSpec((block, planes, 2, share, wide), lambda i: (i, 0, 0, 0, 0)),
+            pl.BlockSpec((cols, tile), lambda i: (0, i)),
+            pl.BlockSpec((tile, wide), lambda i: (i, 0)),
         ],
         out_specs=pl.BlockSpec((cols, wide), lambda i: (0, 0)),
         out_shape=jax.ShapeDtypeStruct((cols, wide), BF16),
         scratch_shapes=[pltpu.VMEM((cols, wide), F32)],
         compiler_params=params(),
-    )(core, own, other, mixed)
+    )(*pinned(left, right))
 
 
 SWAP = [(i, i ^ 1) for i in range(8)]
-PLANES = [[0, 2, 4, 6], [1, 3, 5, 7]]
-
-
-def over_planes(value):
-    return lax.all_to_all(value, "tp", 0, 0, tiled=True, axis_index_groups=PLANES)
+
+
+def along_z(d):
+    return [(2 * z + c, 2 * ((z + d) % 4) + c) for z in range(4) for c in range(2)]
+
+
+def after(value, *others):
+    return lax.optimization_barrier((value,) + others)[0]
+
+
+def swap(value):
+    return lax.ppermute(value, "tp", SWAP)
+
+
+def up(value):
+    return lax.ppermute(value, "tp", along_z(1))
+
+
+def down(value):
+    return lax.ppermute(value, "tp", along_z(-1))
+
+
+def over_slabs(value):
+    return lax.all_to_all(value, "ctx", 0, 0, tiled=True)
 
 
 def shards(
@@ -373,50 +469,58 @@
 ):
     share, width = grad_out.shape
     n_ctx = lax.axis_size("ctx")
-    n_tp = lax.axis_size("tp")
-    core = lax.axis_index("tp") % 2
-    b = b_proj.reshape(ROWS, STATE)
-    c = c_proj.reshape(ROWS, STATE)
+    tp = lax.axis_index("tp").astype(jnp.int32)
+    place = jnp.stack([tp // 2, tp % 2])
+    b, c, x, dt, doc, weight = pinned(
+        b_proj.reshape(ROWS, STATE),
+        c_proj.reshape(ROWS, STATE),
+        ssm_input,
+        dt_raw.T,
+        doc_start.reshape(1, ROWS),
+        out_weight,
+    )
+    bias, rate, skip = pinned(dt_bias, decay_rate, skip_gain)
+
     grad_full = lax.all_gather(grad_out, "tp", axis=0, tiled=True)
-    payload, rows, tab = states(
-        dt_bias, decay_rate, ssm_input, dt_raw.T, doc_start.reshape(1, ROWS), b
-    )
-    carried, decay = prefix(lax.all_to_all(payload, "ctx", 0, 0, tiled=True))
-    carried = lax.all_to_all(carried, "ctx", 0, 0, tiled=True)
-    mixed, inner = mixer(skip_gain, ssm_input, b, c, rows, tab, carried)
-
+    payload, rows, tab = states(bias, rate, x, dt, doc, b)
+    carried, decay = prefix(over_slabs(payload))
+    carried = over_slabs(carried)
+    mixed, inner = mixer(skip, x, b, c, rows, tab, carried)
+    (inner,) = pinned(inner)
     mixed_all = lax.all_gather(mixed, "ctx", axis=0, tiled=True)
-    columns = lax.all_to_all(grad_out, "ctx", 1, 0, tiled=True)
-    own = over_planes(jnp.broadcast_to(columns, (4,) + columns.shape))
-    other = lax.ppermute(own, "tp", SWAP)
-
-    partial = nn(mixed, out_weight).astype(BF16).reshape(n_tp // 2, 2, share, width)
-    keep = lax.dynamic_index_in_dim(partial, core, 1, False)
-    send = lax.dynamic_index_in_dim(partial, 1 - core, 1, False)
-    both = keep.astype(F32) + lax.ppermute(send, "tp", SWAP).astype(F32)
-    layer_out = jnp.sum(over_planes(both.astype(BF16)).astype(F32), axis=0).astype(BF16)
-
-    grad_mix = nt(grad_full, out_weight).astype(BF16)
-    after = suffix(
-        lax.all_to_all(local_grad(grad_mix, c, tab), "ctx", 0, 0, tiled=True), decay
-    )
-    after = lax.all_to_all(after, "ctx", 0, 0, tiled=True)
+    columns = lax.all_to_all(after(grad_out, decay), "ctx", 1, 0, tiled=True)
+
+    keep, send, grad_mix, local = project(
+        place, grad_full, mixed.reshape(4, 2, share, WIDE), weight, rows, c
+    )
+    local = over_slabs(local)
+    taken = swap(send)
+    half = share // 2
+    columns = after(columns, keep)
+    c_up, c_down = up(columns), down(columns)
+
+    next_grad = over_slabs(suffix(local, decay))
+    pair = keep.astype(F32) + taken.astype(F32)
+    far_up, far_down = up(pair[3, :half].astype(BF16)), down(pair[3, half:].astype(BF16))
+    split = columns.shape[0] // 2
+    mine = (columns, c_up, c_down, up(c_up[:split]), down(c_down[split:]))
+    pieces = mine + tuple(swap(piece) for piece in mine)
+    top = jnp.concatenate([pair[1, :half] + far_up.astype(F32), pair[1, half:]], 0)
+    low = jnp.concatenate([pair[2, :half], pair[2, half:] + far_down.astype(F32)], 0)
+    from_low, from_top = up(top.astype(BF16)), down(low.astype(BF16))
     grad_x, grad_dt, grad_b, grad_c = backward(
-        skip_gain, decay_rate, ssm_input, b, c, rows, tab, carried, inner, grad_mix, after
-    )
-    weight = weight_grad(
-        core.reshape(1),
-        own,
-        other,
-        mixed_all.reshape(n_ctx, n_tp // 2, 2, share, WIDE),
-    )
+        skip, rate, x, b, c, rows, tab, carried, inner, grad_mix, next_grad
+    )
+    layer_out = (pair[0] + from_low.astype(F32) + from_top.astype(F32)).astype(BF16)
+    left = arrange(place, pieces, n_ctx)
+    weight_sum = weight_grad(left, mixed_all)
     return (
         layer_out,
         grad_x,
         grad_dt.T,
         grad_b.reshape(ROWS, 1, STATE),
         grad_c.reshape(ROWS, 1, STATE),
-        weight,
+        weight_sum,
     )
 
 

time: 208 us -> 168 us (0.81)
  waiting for transfers between devices: 49.6 us -> 16.5 us
  matrix products: 23.4 us -> 0 us
  Pallas kernels: 25.4 us -> 44.6 us
  blocking collectives: 31.2 us -> 44.7 us
  local copies, waits for them, and re-layouts: 21 us -> 8.85 us
  starting transfers between devices: 33.9 us -> 28.5 us
  other arithmetic: 7.02 us -> 9.27 us
    all_to_all x5 -> x2, waiting for transfers between devices: 48.8 us -> 14.9 us  [over_slabs(): return lax.all_to_all(value, 'ctx', 0, 0, tiled=True)]
    dot_general x2 -> x0, matrix products: 23.4 us -> none  [dot(): lax.dot_general(a, b, (dims, ((), ())), precision=precision, preferred_el...]
    pallas_call x7 -> x8, Pallas kernels: 25.4 us -> 44.6 us  [the longest x5 16.2 us: staged(): pl.pallas_call(body, in_specs=hbm(n), out_specs=hbm(m), out_shape=tuple((...]
    all_to_all x5 -> x2, starting transfers between devices: 21.7 us -> 7.16 us  [over_slabs(): return lax.all_to_all(value, 'ctx', 0, 0, tiled=True)]
    all_to_all x2 -> x3, blocking collectives: 31.2 us -> 44.7 us  [the longest x2 31 us: over_slabs(): return lax.all_to_all(value, 'ctx', 0, 0, tiled=True)]
    unnamed x48 -> x20, local copies, waits for them, and re-layouts: 17.1 us -> 7.09 us
    ppermute x2 -> x14, starting transfers between devices: 12.1 us -> 21.3 us  [the longest x6 10.1 us: swap(): return lax.ppermute(value, 'tp', SWAP)]
    another operation x0 -> x3, other arithmetic: none -> 4.18 us
  transfers between devices with their start and end apart: 9 -> 18, of which waited for: 5 -> 3; matrix products, arithmetic and copies ran while one was open for 17% -> 7% of each run, Pallas kernels for 7% -> 20%
where the time goes in v2:
time: 168 us; the launch traced here: 167 us
  blocking collectives  44.7 us (27%)
  Pallas kernels  44.6 us (27%)
  starting transfers between devices  28.5 us (17%)
  waiting for transfers between devices  16.5 us (10%)
  between operations  14.3 us (9%)
  other arithmetic  9.27 us (6%)
  local copies, waits for them, and re-layouts  8.85 us (5%)
    all_to_all x2, blocking collectives, over_slabs(): return lax.all_to_all(value, 'ctx', 0, 0, tiled=True)  31 us
    pallas_call x5, Pallas kernels, staged(): pl.pallas_call(body, in_specs=hbm(n), out_specs=hbm(m), out_shape=tuple((...  16.2 us
    all_to_all x2, waiting for transfers between devices, over_slabs(): return lax.all_to_all(value, 'ctx', 0, 0, tiled=True)  14.9 us
    pallas_call x1, Pallas kernels, project(): pl.pallas_call(project_kernel, grid=(width // tile,), in_specs=smem(1) +...  14.4 us
    all_to_all x1, blocking collectives, shards(): columns = lax.all_to_all(after(grad_out, decay), 'ctx', 1, 0, tiled=True)  13.7 us
    pallas_call x1, Pallas kernels, weight_grad(): pl.pallas_call(weight_kernel, grid=(deep // tile,), in_specs=[pl.BlockSpe...  10.6 us
    ppermute x6, starting transfers between devices, swap(): return lax.ppermute(value, 'tp', SWAP)  10.1 us
    ppermute x4, starting transfers between devices, down(): return lax.ppermute(value, 'tp', along_z(-1))  9.43 us
  transfers between devices with their start and end apart: 18, of which 3 were waited for; matrix products, arithmetic and copies ran while one was open for 7% of the time, Pallas kernels for 20%

profile of v2, /device:TPU:1, one launch (start us, length us, event | category | flops | bytes accessed | tf_op | source)
XLA Modules:
  0.0 166.8 jit_solution(13486709626705272192)
XLA Ops:
  7.9 3.3 %shard_map.145 = (bf16[16,72,256]{2,1,0:T(8,128)(2,1)S(1)}, f32[128,256]{1,0:T(8,128)S(1)}, f32[256,128]{1,0:T(8,128)S(1)}) custom-call(f32[16]{0:T(128)} %refs_0_.3, f32[16]{0:T(128)} %refs_1_.5, bf16[256,1024]{1,0:T(8,128)(2,1)} %refs_2_.3, f32[16,256]{1,0:T(8,128)} %bitcast.71, s32[1,256]{1,0:T(1,128)} %bitcast.72, bf16[256,256]{1,0:T(8,128)(2,1)} %bitcast.68), custom_call_target="tpu_custom_call" | custom-call | tf_op jit(solution)/shard_map/pallas_call | solution.py:74
  11.2 18.7 %all_to_all.39.refs_0_ = bf16[16,72,256]{2,1,0:T(8,128)(2,1)S(1)} all-to-all(bf16[16,72,256]{2,1,0:T(8,128)(2,1)S(1)} %get-tuple-element.25), channel_id=1, replica_groups=mesh['ctx'=16,'tp'=8] {'ctx'}, dimensions={0} | all-to-all | bytes 1179648 | tf_op jit(solution)/shard_map/all_to_all | solution.py:455
  30.2 12.3 %all_to_all.40.refs_6_.refs_7_ = bf16[16,64,256]{2,1,0:T(8,128)(2,1)S(1)} all-to-all(bf16[16,64,256]{2,1,0:T(8,128)(2,1)S(1)} %get-tuple-element.26), channel_id=1, replica_groups=mesh['ctx'=16,'tp'=8] {'ctx'}, dimensions={0} | all-to-all | bytes 1048576 | tf_op jit(solution)/shard_map/all_to_all | solution.py:455
  42.6 4.2 %shard_map.147 = (bf16[256,1024]{1,0:T(8,128)(2,1)}, f32[256,1024]{1,0:T(8,128)S(1)}) custom-call(f32[16]{0:T(128)} %refs_0_.5, bf16[256,1024]{1,0:T(8,128)(2,1)} %refs_2_.3, bf16[256,256]{1,0:T(8,128)(2,1)} %bitcast.69, bf16[256,256]{1,0:T(8,128)(2,1)} %bitcast.65, f32[128,256]{1,0:T(8,128)S(1)} %get-tuple-element.23.refs_4_.rows.refs_5_, ...), custom_call_target="tpu_custom_call" | custom-call | tf_op jit(solution)/shard_map/pallas_call | solution.py:74
  46.9 2.4 %copy-done.1 = bf16[256,8192]{1,0:T(8,128)(2,1)S(1)} copy-done((bf16[256,8192]{1,0:T(8,128)(2,1)S(1)}, bf16[256,8192]{1,0:T(8,128)(2,1)}, u32[]{:S(2)}) %copy-start.1) | copy-done | bytes 4194328
  49.4 14.4 %shard_map.148 = (bf16[4,32,8192]{2,1,0:T(8,128)(2,1)S(1)}, bf16[4,32,8192]{2,1,0:T(8,128)(2,1)S(1)}, bf16[256,1024]{1,0:T(8,128)(2,1)S(1)}, bf16[16,64,256]{2,1,0:T(8,128)(2,1)S(1)}) custom-call(s32[2]{0:T(128)S(1)} %pad_add_fusion.place, bf16[256,8192]{1,0:T(8,128)(2,1)S(1)} %copy-done.1, bf16[4,2,32,1024]{3,2,1,0:T(8,128)(2,1)} %bitcast.6.mixed, ...), custom_call_target="tpu_custom_call" | custom-call | tf_op jit(solution)/shard_map/pallas_call | solution.py:340
  63.8 3.1 %collective-permute-start = (bf16[4,32,8192]{2,1,0:T(8,128)(2,1)S(1)}, bf16[4,32,8192]{2,1,0:T(8,128)(2,1)S(1)}, u32[]{:S(2)}, u32[]{:S(2)}) collective-permute-start(bf16[4,32,8192]{2,1,0:T(8,128)(2,1)S(1)} %get-tuple-element.29), channel_id=1, source_target_pairs={{0,1},{1,0},{2,3},{3,2},{4,5},{5,4},{6,7},{7,6},{8,9},{9,8},{10,11... | collective-permute-start | bytes 6291464 | tf_op jit(solution)/shard_map/ppermute | solution.py:443
  66.9 13.7 %all_to_all.41 = bf16[32,16,512]{2,0,1:T(8,128)(2,1)S(1)} all-to-all(bf16[32,16,512]{2,0,1:T(8,128)(2,1)S(1)} %bitcast.64), channel_id=1, replica_groups=mesh['ctx'=16,'tp'=8] {'ctx'}, dimensions={1} | all-to-all | bytes 1048576 | tf_op jit(solution)/shard_map/all_to_all | solution.py:491
  80.6 1.7 %collective-permute-start.5 = (bf16[512,512]{1,0:T(8,128)(2,1)S(1)}, bf16[512,512]{1,0:T(8,128)(2,1)S(1)}, u32[]{:S(2)}, u32[]{:S(2)}) collective-permute-start(bf16[512,512]{1,0:T(8,128)(2,1)S(1)} %bitcast.55), channel_id=1, source_target_pairs={{0,2},{1,3},{2,4},{3,5},{4,6},{5,7},{6,0},{7,1},{8,10},{9,11},{10,... | collective-permute-start | bytes 1572872 | tf_op jit(solution)/shard_map/ppermute | solution.py:447
  82.3 2.2 %collective-permute-start.6 = (bf16[512,512]{1,0:T(8,128)(2,1)S(1)}, bf16[512,512]{1,0:T(8,128)(2,1)S(1)}, u32[]{:S(2)}, u32[]{:S(2)}) collective-permute-start(bf16[512,512]{1,0:T(8,128)(2,1)S(1)} %bitcast.56), channel_id=1, source_target_pairs={{0,6},{1,7},{2,0},{3,1},{4,2},{5,3},{6,4},{7,5},{8,14},{9,15},{10,... | collective-permute-start | bytes 1572872 | tf_op jit(solution)/shard_map/ppermute | solution.py:451
  84.5 2.7 %fusion.7 = (bf16[4,32,8192]{2,1,0:T(8,128)(2,1)S(1)}, f32[4,32,8192]{2,1,0:T(8,128)}) fusion(bf16[4,32,8192]{2,1,0:T(8,128)(2,1)S(1)} %collective-permute-done, bf16[4,32,8192]{2,1,0:T(8,128)(2,1)S(1)} %get-tuple-element.28), kind=kLoop, calls=%fused_computation.19 | loop fusion | flops 4194304 | bytes 10485760 | tf_op jit(solution)/shard_map/convert.9
  87.2 1.0 slice_bitcast_fusion.6
  88.2 2.7 %collective-permute-start.3 = (bf16[16,8192]{1,0:T(8,128)(2,1)}, bf16[16,8192]{1,0:T(8,128)(2,1)}, u32[]{:S(2)}, u32[]{:S(2)}) collective-permute-start(bf16[16,8192]{1,0:T(8,128)(2,1)} %get-tuple-element.45), channel_id=1, source_target_pairs={{0,6},{1,7},{2,0},{3,1},{4,2},{5,3},{6,4},{7,5},{8,14},{9,15},{10,... | collective-permute-start | bytes 786440 | tf_op jit(solution)/shard_map/ppermute | solution.py:451
  90.8 2.2 %collective-permute-start.9 = (bf16[512,512]{1,0:T(8,128)(2,1)S(1)}, bf16[512,512]{1,0:T(8,128)(2,1)S(1)}, u32[]{:S(2)}, u32[]{:S(2)}) collective-permute-start(bf16[512,512]{1,0:T(8,128)(2,1)S(1)} %bitcast.57), channel_id=1, source_target_pairs={{0,1},{1,0},{2,3},{3,2},{4,5},{5,4},{6,7},{7,6},{8,9},{9,8},{10,11... | collective-permute-start | bytes 1572872 | tf_op jit(solution)/shard_map/ppermute | solution.py:443
  93.1 3.6 %all-to-all-start.2 = ((bf16[16,64,256]{2,1,0:T(8,128)(2,1)}), bf16[16,64,256]{2,1,0:T(8,128)(2,1)S(1)}, u32[]{:S(2)}, u32[]{:S(2)}) async-start(bf16[16,64,256]{2,1,0:T(8,128)(2,1)} %copy-done.3), calls=%async_computation.2 | async-start | bytes 1048576 | tf_op jit(solution)/shard_map/all_to_all | solution.py:455
  97.5 2.7 %collective-permute-start.8 = (bf16[256,512]{1,0:T(8,128)(2,1)}, bf16[256,512]{1,0:T(8,128)(2,1)}, u32[]{:S(2)}, u32[]{:S(2)}) collective-permute-start(bf16[256,512]{1,0:T(8,128)(2,1)} %slice.48), channel_id=1, source_target_pairs={{0,6},{1,7},{2,0},{3,1},{4,2},{5,3},{6,4},{7,5},{8,14},{9,15},{10,... | collective-permute-start | bytes 786440 | tf_op jit(solution)/shard_map/ppermute | solution.py:451
  101.1 3.7 %collective-permute-start.10 = (bf16[512,512]{1,0:T(8,128)(2,1)S(1)}, bf16[512,512]{1,0:T(8,128)(2,1)}, u32[]{:S(2)}, u32[]{:S(2)}) collective-permute-start(bf16[512,512]{1,0:T(8,128)(2,1)S(1)} %collective-permute-done.5), channel_id=1, source_target_pairs={{0,1},{1,0},{2,3},{3,2},{4,5},{5,4},{6,7},{7,6},{8,9},{9,8},{10,11... | collective-permute-start | bytes 1572872 | tf_op jit(solution)/shard_map/ppermute | solution.py:443
  104.8 1.4 fusion.6
  106.2 1.8 %pad_maximum_fusion.1 = bf16[32,8192]{1,0:T(8,128)(2,1)} fusion(bf16[16,8192]{1,0:T(8,128)(2,1)S(1)} %get-tuple-element.41, bf16[16,8192]{1,0:T(8,128)(2,1)} %get-tuple-element.46), kind=kLoop, calls=%fused_computation.13 | loop fusion | flops 1048576 | bytes 1048576 | tf_op jit(solution)/shard_map/concatenate | solution.py:509
  108.9 1.9 %collective-permute-start.4 = (bf16[32,8192]{1,0:T(8,128)(2,1)}, bf16[32,8192]{1,0:T(8,128)(2,1)}, u32[]{:S(2)}, u32[]{:S(2)}) collective-permute-start(bf16[32,8192]{1,0:T(8,128)(2,1)} %pad_maximum_fusion.1), channel_id=1, source_target_pairs={{0,6},{1,7},{2,0},{3,1},{4,2},{5,3},{6,4},{7,5},{8,14},{9,15},{10,... | collective-permute-start | bytes 1572872 | tf_op jit(solution)/shard_map/ppermute | solution.py:451
  111.5 2.6 %all-to-all-done.2.refs_0_ = bf16[16,64,256]{2,1,0:T(8,128)(2,1)S(1)} async-done(((bf16[16,64,256]{2,1,0:T(8,128)(2,1)}), bf16[16,64,256]{2,1,0:T(8,128)(2,1)S(1)}, u32[]{:S(2)}, u32[]{:S(2)}) %all-to-all-start.2) | async-done | bytes 524320 | tf_op jit(solution)/shard_map/all_to_all | solution.py:455
  114.1 1.0 shard_map.149
  115.1 3.6 %all-to-all-start.3 = ((bf16[16,64,256]{2,1,0:T(8,128)(2,1)}), bf16[16,64,256]{2,1,0:T(8,128)(2,1)S(1)}, u32[]{:S(2)}, u32[]{:S(2)}) async-start(bf16[16,64,256]{2,1,0:T(8,128)(2,1)} %shard_map.149), calls=%async_computation.3 | async-start | bytes 1048576 | tf_op jit(solution)/shard_map/all_to_all | solution.py:455
  118.7 0.9 collective-permute-start.12
  119.8 12.3 %all-to-all-done.3.refs_10_ = bf16[16,64,256]{2,1,0:T(8,128)(2,1)S(1)} async-done(((bf16[16,64,256]{2,1,0:T(8,128)(2,1)}), bf16[16,64,256]{2,1,0:T(8,128)(2,1)S(1)}, u32[]{:S(2)}, u32[]{:S(2)}) %all-to-all-start.3) | async-done | bytes 524320 | tf_op jit(solution)/shard_map/all_to_all | solution.py:455
  132.0 1.0 copy-done.5
  133.1 7.4 %shard_map.150 = (bf16[256,1024]{1,0:T(8,128)(2,1)}, f32[16,256]{1,0:T(8,128)}, bf16[256,256]{1,0:T(8,128)(2,1)}, bf16[256,256]{1,0:T(8,128)(2,1)}) custom-call(f32[16]{0:T(128)} %refs_0_.5, f32[16]{0:T(128)} %refs_1_.5, bf16[256,1024]{1,0:T(8,128)(2,1)} %refs_2_.3, bf16[256,256]{1,0:T(8,128)(2,1)} %bitcast.70, bf16[256,256]{1,0:T(8,128)(2,1)} %bitcast.67, ...), custom_call_target="tpu_custom_call" | custom-call | tf_op jit(solution)/shard_map/pallas_call | solution.py:74
  140.5 0.9 copy-done.7
  141.5 3.4 %shard_map.151.left = bf16[512,4096]{1,0:T(8,128)(2,1)S(1)} custom-call(s32[2]{0:T(128)S(1)} %pad_add_fusion.place, bf16[16,32,512]{2,1,0:T(8,128)(2,1)S(1)} %bitcast.58, bf16[16,32,512]{2,1,0:T(8,128)(2,1)S(1)} %bitcast.59, bf16[16,32,512]{2,1,0:T(8,128)(2,1)S(1)} %bitcast.60, bf16[8,32,512]{2,1,0:T(8,128)(2,1)S(1)} %bitcast.62, ...), custom_call_target="tpu_custom_call" | custom-call | tf_op jit(solution)/shard_map/pallas_call | solution.py:384
  144.9 1.9 %copy-done = bf16[512,4096]{1,0:T(8,128)(2,1)} copy-done((bf16[512,4096]{1,0:T(8,128)(2,1)}, bf16[512,4096]{1,0:T(8,128)(2,1)S(1)}, u32[]{:S(2)}) %copy-start) | copy-done | bytes 4194328
  146.9 2.5 %fusion.2 = bf16[32,8192]{1,0:T(8,128)(2,1)} fusion(f32[4,32,8192]{2,1,0:T(8,128)} %get-tuple-element.43, bf16[32,8192]{1,0:T(8,128)(2,1)} %collective-permute-done.4, bf16[32,8192]{1,0:T(8,128)(2,1)} %collective-permute-done.2), kind=kLoop, calls=%fused_computation.4 | loop fusion | flops 1310720 | bytes 2621440 | tf_op jit(solution)/shard_map/convert_element_type | solution.py:514
  149.3 10.6 %shard_map.152 = bf16[512,1024]{1,0:T(8,128)(2,1)} custom-call(bf16[512,4096]{1,0:T(8,128)(2,1)} %copy-done, bf16[4096,1024]{1,0:T(8,128)(2,1)} %all-gather.5.cloned.1.call-done.right), custom_call_target="tpu_custom_call" | custom-call | tf_op jit(solution)/shard_map/pallas_call | solution.py:417
  (47 shorter events, 4.6 us)
Async XLA Ops:
  7.2 39.7 %all-gather.3.cloned.1.call-start = ((), (), s32[]{:S(2)}) async-start(), calls=%async_computation.5 | async-start | bytes 4718592 | tf_op jit(solution)/shard_map/all_gather | solution.py:484
  7.9 141.4 %all-gather.5.cloned.1.call-start = ((), (), s32[]{:S(2)}) async-start(), calls=%async_computation.6 | async-start | bytes 8912896 | tf_op jit(solution)/shard_map/all_gather | solution.py:490
  46.8 17.0 %copy-start.2 = (f32[256,1024]{1,0:T(8,128)}, f32[256,1024]{1,0:T(8,128)S(1)}, u32[]{:S(2)}) copy-start(f32[256,1024]{1,0:T(8,128)S(1)} %get-tuple-element.30.refs_8_) | copy-start | bytes 3145732
  46.9 2.4 %copy-start.1 = (bf16[256,8192]{1,0:T(8,128)(2,1)S(1)}, bf16[256,8192]{1,0:T(8,128)(2,1)}, u32[]{:S(2)}) copy-start(bf16[256,8192]{1,0:T(8,128)(2,1)} %all-gather.3.cloned.1.call-done.grad) | copy-start | bytes 12582916
  49.4 17.5 %copy-start.8 = (bf16[32,8192]{1,0:T(8,128)(2,1)S(1)}, bf16[32,8192]{1,0:T(8,128)(2,1)}, u32[]{:S(2)}) copy-start(bf16[32,8192]{1,0:T(8,128)(2,1)} %param.19) | copy-start | bytes 1572868
  63.7 23.4 %copy-start.3 = (bf16[16,64,256]{2,1,0:T(8,128)(2,1)}, bf16[16,64,256]{2,1,0:T(8,128)(2,1)S(1)}, u32[]{:S(2)}) copy-start(bf16[16,64,256]{2,1,0:T(8,128)(2,1)S(1)} %get-tuple-element.32) | copy-start | bytes 1572868
  63.8 23.4 %copy-start.4 = (bf16[256,1024]{1,0:T(8,128)(2,1)}, bf16[256,1024]{1,0:T(8,128)(2,1)S(1)}, u32[]{:S(2)}) copy-start(bf16[256,1024]{1,0:T(8,128)(2,1)S(1)} %get-tuple-element.31.refs_9_) | copy-start | bytes 1572868
  63.8 20.8 %collective-permute-start = (bf16[4,32,8192]{2,1,0:T(8,128)(2,1)S(1)}, bf16[4,32,8192]{2,1,0:T(8,128)(2,1)S(1)}, u32[]{:S(2)}, u32[]{:S(2)}) collective-permute-start(bf16[4,32,8192]{2,1,0:T(8,128)(2,1)S(1)} %get-tuple-element.29), channel_id=1, source_target_pairs={{0,1},{1,0},{2,3},{3,2},{4,5},{5,4},{6,7},{7,6},{8,9},{9,8},{10,11... | collective-permute-start | bytes 6291464 | tf_op jit(solution)/shard_map/ppermute | solution.py:443
  80.6 16.0 %collective-permute-start.5 = (bf16[512,512]{1,0:T(8,128)(2,1)S(1)}, bf16[512,512]{1,0:T(8,128)(2,1)S(1)}, u32[]{:S(2)}, u32[]{:S(2)}) collective-permute-start(bf16[512,512]{1,0:T(8,128)(2,1)S(1)} %bitcast.55), channel_id=1, source_target_pairs={{0,2},{1,3},{2,4},{3,5},{4,6},{5,7},{6,0},{7,1},{8,10},{9,11},{10,... | collective-permute-start | bytes 1572872 | tf_op jit(solution)/shard_map/ppermute | solution.py:447
  82.3 14.5 %collective-permute-start.6 = (bf16[512,512]{1,0:T(8,128)(2,1)S(1)}, bf16[512,512]{1,0:T(8,128)(2,1)S(1)}, u32[]{:S(2)}, u32[]{:S(2)}) collective-permute-start(bf16[512,512]{1,0:T(8,128)(2,1)S(1)} %bitcast.56), channel_id=1, source_target_pairs={{0,6},{1,7},{2,0},{3,1},{4,2},{5,3},{6,4},{7,5},{8,14},{9,15},{10,... | collective-permute-start | bytes 1572872 | tf_op jit(solution)/shard_map/ppermute | solution.py:451
  88.2 12.9 %collective-permute-start.1 = (bf16[16,8192]{1,0:T(8,128)(2,1)}, bf16[16,8192]{1,0:T(8,128)(2,1)}, u32[]{:S(2)}, u32[]{:S(2)}) collective-permute-start(bf16[16,8192]{1,0:T(8,128)(2,1)} %get-tuple-element.44), channel_id=1, source_target_pairs={{0,2},{1,3},{2,4},{3,5},{4,6},{5,7},{6,0},{7,1},{8,10},{9,11},{10,... | collective-permute-start | bytes 786440 | tf_op jit(solution)/shard_map/ppermute | solution.py:447
  88.2 16.6 %collective-permute-start.3 = (bf16[16,8192]{1,0:T(8,128)(2,1)}, bf16[16,8192]{1,0:T(8,128)(2,1)}, u32[]{:S(2)}, u32[]{:S(2)}) collective-permute-start(bf16[16,8192]{1,0:T(8,128)(2,1)} %get-tuple-element.45), channel_id=1, source_target_pairs={{0,6},{1,7},{2,0},{3,1},{4,2},{5,3},{6,4},{7,5},{8,14},{9,15},{10,... | collective-permute-start | bytes 786440 | tf_op jit(solution)/shard_map/ppermute | solution.py:451
  90.8 18.0 %collective-permute-start.9 = (bf16[512,512]{1,0:T(8,128)(2,1)S(1)}, bf16[512,512]{1,0:T(8,128)(2,1)S(1)}, u32[]{:S(2)}, u32[]{:S(2)}) collective-permute-start(bf16[512,512]{1,0:T(8,128)(2,1)S(1)} %bitcast.57), channel_id=1, source_target_pairs={{0,1},{1,0},{2,3},{3,2},{4,5},{5,4},{6,7},{7,6},{8,9},{9,8},{10,11... | collective-permute-start | bytes 1572872 | tf_op jit(solution)/shard_map/ppermute | solution.py:443
  93.1 21.0 %all-to-all-start.2 = ((bf16[16,64,256]{2,1,0:T(8,128)(2,1)}), bf16[16,64,256]{2,1,0:T(8,128)(2,1)S(1)}, u32[]{:S(2)}, u32[]{:S(2)}) async-start(bf16[16,64,256]{2,1,0:T(8,128)(2,1)} %copy-done.3), calls=%async_computation.2 | async-start | bytes 1048576 | tf_op jit(solution)/shard_map/all_to_all | solution.py:455
  96.7 11.4 %copy-start.9 = (bf16[16,8192]{1,0:T(8,128)(2,1)S(1)}, bf16[16,8192]{1,0:T(8,128)(2,1)}, u32[]{:S(2)}) copy-start(bf16[16,8192]{1,0:T(8,128)(2,1)} %get-tuple-element.47) | copy-start | bytes 786436
  96.7 14.1 %collective-permute-start.7 = (bf16[256,512]{1,0:T(8,128)(2,1)S(1)}, bf16[256,512]{1,0:T(8,128)(2,1)S(1)}, u32[]{:S(2)}, u32[]{:S(2)}) collective-permute-start(bf16[256,512]{1,0:T(8,128)(2,1)S(1)} %slice.47), channel_id=1, source_target_pairs={{0,2},{1,3},{2,4},{3,5},{4,6},{5,7},{6,0},{7,1},{8,10},{9,11},{10,... | collective-permute-start | bytes 786440 | tf_op jit(solution)/shard_map/ppermute | solution.py:447
  97.5 21.2 %collective-permute-start.8 = (bf16[256,512]{1,0:T(8,128)(2,1)}, bf16[256,512]{1,0:T(8,128)(2,1)}, u32[]{:S(2)}, u32[]{:S(2)}) collective-permute-start(bf16[256,512]{1,0:T(8,128)(2,1)} %slice.48), channel_id=1, source_target_pairs={{0,6},{1,7},{2,0},{3,1},{4,2},{5,3},{6,4},{7,5},{8,14},{9,15},{10,... | collective-permute-start | bytes 786440 | tf_op jit(solution)/shard_map/ppermute | solution.py:451
  101.1 18.6 %collective-permute-start.10 = (bf16[512,512]{1,0:T(8,128)(2,1)S(1)}, bf16[512,512]{1,0:T(8,128)(2,1)}, u32[]{:S(2)}, u32[]{:S(2)}) collective-permute-start(bf16[512,512]{1,0:T(8,128)(2,1)S(1)} %collective-permute-done.5), channel_id=1, source_target_pairs={{0,1},{1,0},{2,3},{3,2},{4,5},{5,4},{6,7},{7,6},{8,9},{9,8},{10,11... | collective-permute-start | bytes 1572872 | tf_op jit(solution)/shard_map/ppermute | solution.py:443
  104.8 35.7 %collective-permute-start.11 = (bf16[512,512]{1,0:T(8,128)(2,1)S(1)}, bf16[512,512]{1,0:T(8,128)(2,1)}, u32[]{:S(2)}, u32[]{:S(2)}) collective-permute-start(bf16[512,512]{1,0:T(8,128)(2,1)S(1)} %collective-permute-done.6), channel_id=1, source_target_pairs={{0,1},{1,0},{2,3},{3,2},{4,5},{5,4},{6,7},{7,6},{8,9},{9,8},{10,11... | collective-permute-start | bytes 1572872 | tf_op jit(solution)/shard_map/ppermute | solution.py:443
  108.9 38.0 %collective-permute-start.4 = (bf16[32,8192]{1,0:T(8,128)(2,1)}, bf16[32,8192]{1,0:T(8,128)(2,1)}, u32[]{:S(2)}, u32[]{:S(2)}) collective-permute-start(bf16[32,8192]{1,0:T(8,128)(2,1)} %pad_maximum_fusion.1), channel_id=1, source_target_pairs={{0,6},{1,7},{2,0},{3,1},{4,2},{5,3},{6,4},{7,5},{8,14},{9,15},{10,... | collective-permute-start | bytes 1572872 | tf_op jit(solution)/shard_map/ppermute | solution.py:451
  110.8 0.7 copy-start.6
  111.5 35.4 %collective-permute-start.2 = (bf16[32,8192]{1,0:T(8,128)(2,1)}, bf16[32,8192]{1,0:T(8,128)(2,1)}, u32[]{:S(2)}, u32[]{:S(2)}) collective-permute-start(bf16[32,8192]{1,0:T(8,128)(2,1)} %pad_maximum_fusion), channel_id=1, source_target_pairs={{0,2},{1,3},{2,4},{3,5},{4,6},{5,7},{6,0},{7,1},{8,10},{9,11},{10,... | collective-permute-start | bytes 1572872 | tf_op jit(solution)/shard_map/ppermute | solution.py:447
  115.1 16.9 %all-to-all-start.3 = ((bf16[16,64,256]{2,1,0:T(8,128)(2,1)}), bf16[16,64,256]{2,1,0:T(8,128)(2,1)S(1)}, u32[]{:S(2)}, u32[]{:S(2)}) async-start(bf16[16,64,256]{2,1,0:T(8,128)(2,1)} %shard_map.149), calls=%async_computation.3 | async-start | bytes 1048576 | tf_op jit(solution)/shard_map/all_to_all | solution.py:455
  118.7 21.8 %collective-permute-start.12 = (bf16[256,512]{1,0:T(8,128)(2,1)}, bf16[256,512]{1,0:T(8,128)(2,1)}, u32[]{:S(2)}, u32[]{:S(2)}) collective-permute-start(bf16[256,512]{1,0:T(8,128)(2,1)} %copy-done.6), channel_id=1, source_target_pairs={{0,1},{1,0},{2,3},{3,2},{4,5},{5,4},{6,7},{7,6},{8,9},{9,8},{10,11... | collective-permute-start | bytes 786440 | tf_op jit(solution)/shard_map/ppermute | solution.py:443
  119.7 20.8 %collective-permute-start.13 = (bf16[256,512]{1,0:T(8,128)(2,1)}, bf16[256,512]{1,0:T(8,128)(2,1)}, u32[]{:S(2)}, u32[]{:S(2)}) collective-permute-start(bf16[256,512]{1,0:T(8,128)(2,1)} %collective-permute-done.8), channel_id=1, source_target_pairs={{0,1},{1,0},{2,3},{3,2},{4,5},{5,4},{6,7},{7,6},{8,9},{9,8},{10,11... | collective-permute-start | bytes 786440 | tf_op jit(solution)/shard_map/ppermute | solution.py:443
  132.0 1.0 copy-start.5
  140.5 1.0 copy-start.7
  144.9 1.9 %copy-start = (bf16[512,4096]{1,0:T(8,128)(2,1)}, bf16[512,4096]{1,0:T(8,128)(2,1)S(1)}, u32[]{:S(2)}) copy-start(bf16[512,4096]{1,0:T(8,128)(2,1)S(1)} %shard_map.151.left) | copy-start | bytes 12582916
Sparse Core Ops, SparseCore 0:
  9.7 35.9 all-gather.2
  47.9 80.6 all-gather.4

commit v3 on v2

--- a/solution.py
+++ b/solution.py
@@ -47,7 +47,7 @@
     return [pltpu.with_memory_space_constraint(a, pltpu.HBM) for a in arrays]
 
 
-def staged(kernel, scalars, arrays, outs):
+def staged(kernel, scalars, arrays, outs, us):
     given = list(scalars) + list(arrays)
     n, m = len(given), len(outs)
 
@@ -81,11 +81,16 @@
         + [pltpu.VMEM(*out) for out in outs]
         + [pltpu.SemaphoreType.DMA((n + m,))],
         compiler_params=params(),
+        cost_estimate=took(us),
     )(*given)
 
 
-def params():
-    return pltpu.CompilerParams(vmem_limit_bytes=32 * 1024 * 1024)
+def took(us):
+    return pl.CostEstimate(flops=int(us * 1.1e9), bytes_accessed=0, transcendentals=0)
+
+
+def params(mib=16):
+    return pltpu.CompilerParams(vmem_limit_bytes=mib * 1024 * 1024)
 
 
 def iota(shape, axis):
@@ -149,7 +154,7 @@
         ((8 * HEADS, ROWS), F32),
         ((ROWS, 8 * HEADS), F32),
     ]
-    return staged(states_kernel, (bias, rate), (x, dt, doc, b), outs)
+    return staged(states_kernel, (bias, rate), (x, dt, doc, b), outs, 3.3)
 
 
 def prefix_kernel(got, out, decay):
@@ -166,7 +171,7 @@
 def prefix(got):
     slabs = got.shape[0]
     outs = [((slabs, DIM, STATE), BF16), ((slabs, STATE), F32)]
-    return staged(prefix_kernel, (), (got,), outs)
+    return staged(prefix_kernel, (), (got,), outs, 0.5)
 
 
 def suffix_kernel(got, decay, out):
@@ -178,7 +183,7 @@
 
 
 def suffix(got, decay):
-    return staged(suffix_kernel, (), (got, decay), [(got.shape, BF16)])[0]
+    return staged(suffix_kernel, (), (got, decay), [(got.shape, BF16)], 1.2)[0]
 
 
 def mixer_kernel(skip, x, b, c, rows, tab_ref, carried, mixed, inner):
@@ -205,7 +210,7 @@
 
 def mixer(skip, x, b, c, rows, tab, carried):
     outs = [((ROWS, WIDE), BF16), ((ROWS, WIDE), F32)]
-    return staged(mixer_kernel, (skip,), (x, b, c, rows, tab, carried), outs)
+    return staged(mixer_kernel, (skip,), (x, b, c, rows, tab, carried), outs, 4.2)
 
 
 def head_sums(pair, values):
@@ -216,9 +221,7 @@
     return nt(own, upper) + nt(own, lower)
 
 
-def backward_kernel(
-    skip, rate, x, b, c, rows, tab_ref, carried, inner, grad, after, grad_x, grad_dt, grad_b, grad_c
-):
+def inside_kernel(x, b, c, rows, tab_ref, carried, inner, grad, part, grad_c, b_part, cum_part):
     tab = tab_ref[...]
     scores = nt(b[...], c[...])
     order_s, order_t = iota((ROWS, ROWS), 0), iota((ROWS, ROWS), 1)
@@ -226,17 +229,10 @@
     mask = jnp.where((order_t >= order_s) & (col(tab, SEG, 0) == seg_row), 0.0, MASKED)
     low = iota((ROWS, 2 * DIM), 1) < DIM
     grad_scores = jnp.zeros((ROWS, ROWS), F32)
-    b_sum = jnp.zeros((ROWS, STATE), F32)
     c_sum = jnp.zeros((ROWS, STATE), F32)
-    step_grad = jnp.zeros((HEADS, ROWS), F32)
     cum_grad = jnp.zeros((HEADS, ROWS), F32)
-    state_dot = jnp.zeros((HEADS, ROWS), F32)
-    tail_dot = jnp.zeros((HEADS, ROWS), F32)
     for j in range(PAIRS):
-        x_pair = x[:, cols_of(j)].astype(F32)
-        step = pair_cols(tab, STEP, j)
-        scaled_f = x_pair * step
-        scaled = scaled_f.astype(BF16)
+        scaled = (x[:, cols_of(j)].astype(F32) * pair_cols(tab, STEP, j)).astype(BF16)
         g = grad[:, cols_of(j)]
         g_f = g.astype(F32)
         zero = jnp.zeros_like(g)
@@ -248,33 +244,63 @@
             own = jnp.where(low if k == 0 else jnp.logical_not(low), g, zero)
             grad_scores = grad_scores + nt(scaled, own) * decay
             parts.append(nn((decay * scores).astype(BF16), g))
+        part[:, cols_of(j)] = jnp.where(low, parts[0], parts[1])
+        prev = carried[2 * j : 2 * j + 2].reshape(2 * DIM, STATE)
+        cum_grad = cum_grad + head_sums(j, g_f * inner[:, cols_of(j)])
+        c_sum = c_sum + nn((pair_cols(tab, ENTRY, j) * g_f).astype(BF16), prev)
+    flow = grad_scores.astype(BF16)
+    b_part[...] = nn(flow, c[...])
+    grad_c[...] = (c_sum + tn(flow, b[...])).astype(BF16)
+    cum_part[...] = cum_grad
+
+
+def inside_grads(x, b, c, rows, tab, carried, inner, grad):
+    outs = [
+        ((ROWS, WIDE), F32),
+        ((ROWS, STATE), BF16),
+        ((ROWS, STATE), F32),
+        ((HEADS, ROWS), F32),
+    ]
+    return staged(inside_kernel, (), (x, b, c, rows, tab, carried, inner, grad), outs, 5.0)
+
+
+def backward_kernel(
+    skip, rate, x, b, rows, tab_ref, carried, grad, part, b_part, cum_part, after, grad_x, grad_dt, grad_b
+):
+    tab = tab_ref[...]
+    low = iota((ROWS, 2 * DIM), 1) < DIM
+    b_sum = b_part[...]
+    step_grad = jnp.zeros((HEADS, ROWS), F32)
+    state_dot = jnp.zeros((HEADS, ROWS), F32)
+    tail_dot = jnp.zeros((HEADS, ROWS), F32)
+    for j in range(PAIRS):
+        x_pair = x[:, cols_of(j)].astype(F32)
+        step = pair_cols(tab, STEP, j)
+        scaled = x_pair * step
+        g_f = grad[:, cols_of(j)].astype(F32)
         nxt = after[2 * j : 2 * j + 2].reshape(2 * DIM, STATE)
         prev = carried[2 * j : 2 * j + 2].reshape(2 * DIM, STATE)
         etail = pair_cols(tab, ETAIL, j)
         from_tail = etail * nt(b[...], nxt)
-        total = jnp.where(low, parts[0], parts[1]) + from_tail
+        total = part[:, cols_of(j)] + from_tail
         gain = jnp.where(low, skip[2 * j], skip[2 * j + 1])
         grad_x[:, cols_of(j)] = (step * total + gain * g_f).astype(BF16)
         step_grad = step_grad + head_sums(j, x_pair * total)
-        cum_grad = cum_grad + head_sums(j, g_f * inner[:, cols_of(j)])
-        tail_dot = tail_dot + head_sums(j, scaled_f * from_tail)
+        tail_dot = tail_dot + head_sums(j, scaled * from_tail)
         product = nxt.astype(F32) * prev.astype(F32)
         head = iota((HEADS, 2 * DIM), 0)
         own_rows = (head == 2 * j + iota((HEADS, 2 * DIM), 1) // DIM).astype(BF16)
         upper = product.astype(BF16)
         lower = (product - upper.astype(F32)).astype(BF16)
         state_dot = state_dot + nn(own_rows, upper) + nn(own_rows, lower)
-        b_sum = b_sum + nn((etail * scaled_f).astype(BF16), nxt)
-        c_sum = c_sum + nn((pair_cols(tab, ENTRY, j) * g_f).astype(BF16), prev)
-    flow = grad_scores.astype(BF16)
-    grad_b[...] = (b_sum + nn(flow, c[...])).astype(BF16)
-    grad_c[...] = (c_sum + tn(flow, b[...])).astype(BF16)
+        b_sum = b_sum + nn((etail * scaled).astype(BF16), nxt)
+    grad_b[...] = b_sum.astype(BF16)
     step_rows = rows[STEP * HEADS : (STEP + 1) * HEADS, :]
     through = rows[THROUGH * HEADS : (THROUGH + 1) * HEADS, :]
     end = jnp.sum(tail_dot, axis=1, keepdims=True) + jnp.sum(
         through * state_dot, axis=1, keepdims=True
     )
-    cum_grad = cum_grad - step_rows * step_grad
+    cum_grad = cum_part[...] - step_rows * step_grad
     since = (iota((ROWS, ROWS), 0) >= iota((ROWS, ROWS), 1)).astype(F32)
     decay_grad = dot(cum_grad, since, ((1,), (0,)), HIGHEST) + end
     head = iota((HEADS, ROWS), 0)
@@ -285,96 +311,190 @@
     grad_dt[...] = (step_grad - rate_rows * decay_grad) * sig
 
 
-def backward(skip, rate, x, b, c, rows, tab, carried, inner, grad, after):
-    outs = [
-        ((ROWS, WIDE), BF16),
-        ((HEADS, ROWS), F32),
-        ((ROWS, STATE), BF16),
-        ((ROWS, STATE), BF16),
-    ]
-    arrays = (x, b, c, rows, tab, carried, inner, grad, after)
-    return staged(backward_kernel, (skip, rate), arrays, outs)
+def backward(skip, rate, x, b, rows, tab, carried, grad, part, b_part, cum_part, after):
+    outs = [((ROWS, WIDE), BF16), ((HEADS, ROWS), F32), ((ROWS, STATE), BF16)]
+    arrays = (x, b, rows, tab, carried, grad, part, b_part, cum_part, after)
+    return staged(backward_kernel, (skip, rate), arrays, outs, 5.0)
 
 
 NEAR_FAR = (0, 1, 3, 2)
+CHUNKS = 8
+
+
+def start(*copies):
+    for copy in copies:
+        copy.start()
+
+
+def wait(*copies):
+    for copy in copies:
+        copy.wait()
+
+
+def paced(loads, ahead=2):
+    for batch in loads[:ahead]:
+        start(*batch)
+    for n, batch in enumerate(loads):
+        wait(*batch)
+        if n + ahead < len(loads):
+            start(*loads[n + ahead])
+        yield n
+
+
+def vmem(n):
+    return [pl.BlockSpec(memory_space=pltpu.VMEM)] * n
 
 
 def project_kernel(
-    place, grad, mixed, weight, rows, c, keep, send, grad_mix, out, ordered, acc
+    place, grad_hbm, weight_hbm, mixed, rows, c, keep, send, grad_mix, out, *scratch
 ):
-    at = pl.program_id(0)
+    grad, weight, ordered, acc, sems = scratch
     plane, core = place[0], place[1]
     planes, _, share, _ = mixed.shape
-
-    @pl.when(at == 0)
-    def _():
-        acc[...] = jnp.zeros_like(acc)
-        for k, step in enumerate(NEAR_FAR):
-            to = (plane + step) % planes
-            ordered[k * share : (k + 1) * share] = mixed[to, core]
-            ordered[(planes + k) * share : (planes + k + 1) * share] = mixed[to, 1 - core]
-
-    acc[...] += nt(weight[...], grad[...])
-    both = nn(ordered[...], weight[...]).astype(BF16)
-    keep[...] = both[: planes * share].reshape(keep.shape)
-    send[...] = both[planes * share :].reshape(send.shape)
-
-    @pl.when(at == pl.num_programs(0) - 1)
-    def _():
-        for h in range(HEADS):
-            part = acc[h * DIM : (h + 1) * DIM].astype(BF16)
-            entry = rows[ENTRY * HEADS + h : ENTRY * HEADS + h + 1, :]
-            out[h] = nn((part.astype(F32) * entry).astype(BF16), c[...]).astype(BF16)
-        for j in range(PAIRS):
-            grad_mix[:, cols_of(j)] = acc[cols_of(j)].T.astype(BF16)
-
-
-def project(place, grad, mixed, weight, rows, c):
+    tile = weight.shape[1] // CHUNKS
+    loads = []
+    for n in range(CHUNKS):
+        cols = pl.ds(n * tile, tile)
+        loads.append(
+            (
+                pltpu.make_async_copy(grad_hbm.at[:, cols], grad.at[:, cols], sems.at[0, n]),
+                pltpu.make_async_copy(weight_hbm.at[:, cols], weight.at[:, cols], sems.at[1, n]),
+            )
+        )
+    for n in paced(loads):
+        if n == 0:
+            for k, step in enumerate(NEAR_FAR):
+                to = (plane + step) % planes
+                ordered[k * share : (k + 1) * share] = mixed[to, core]
+                ordered[(planes + k) * share : (planes + k + 1) * share] = mixed[to, 1 - core]
+        cols = slice(n * tile, (n + 1) * tile)
+        part = nt(weight[:, cols], grad[:, cols])
+        if n == 0:
+            acc[...] = part
+        else:
+            acc[...] += part
+        both = nn(ordered[...], weight[:, cols]).astype(BF16)
+        keep[:, :, cols] = both[: planes * share].reshape(planes, share, tile)
+        send[:, :, cols] = both[planes * share :].reshape(planes, share, tile)
+    for h in range(HEADS):
+        part = acc[h * DIM : (h + 1) * DIM].astype(BF16)
+        entry = rows[ENTRY * HEADS + h : ENTRY * HEADS + h + 1, :]
+        out[h] = nn((part.astype(F32) * entry).astype(BF16), c[...]).astype(BF16)
+    for j in range(PAIRS):
+        grad_mix[:, cols_of(j)] = acc[cols_of(j)].T.astype(BF16)
+
+
+def project(place, grad, weight, mixed, rows, c):
     inner, width = weight.shape
-    planes, sides, share, _ = mixed.shape
-    tile = 1024
-    fixed = lambda s: pl.BlockSpec(s, lambda i, r=len(s): (0,) * r)
-    half = pl.BlockSpec((planes, share, tile), lambda i: (0, 0, i))
-    tall = pl.BlockSpec((inner, tile), lambda i: (0, i))
-    local = (HEADS, DIM, STATE)
+    planes, _, share, _ = mixed.shape
     return pl.pallas_call(
         project_kernel,
-        grid=(width // tile,),
-        in_specs=smem(1)
-        + [pl.BlockSpec((ROWS, tile), lambda i: (0, i)), fixed(mixed.shape), tall]
-        + [fixed(rows.shape), fixed(c.shape)],
-        out_specs=[half, half, fixed((ROWS, inner)), fixed(local)],
+        in_specs=smem(1) + hbm(2) + vmem(3),
+        out_specs=vmem(4),
         out_shape=(
             jax.ShapeDtypeStruct((planes, share, width), BF16),
             jax.ShapeDtypeStruct((planes, share, width), BF16),
             jax.ShapeDtypeStruct((ROWS, inner), BF16),
-            jax.ShapeDtypeStruct(local, BF16),
+            jax.ShapeDtypeStruct((HEADS, DIM, STATE), BF16),
         ),
-        scratch_shapes=[pltpu.VMEM((ROWS, inner), BF16), pltpu.VMEM((inner, ROWS), F32)],
+        scratch_shapes=[
+            pltpu.VMEM(grad.shape, BF16),
+            pltpu.VMEM(weight.shape, BF16),
+            pltpu.VMEM((ROWS, inner), BF16),
+            pltpu.VMEM((inner, ROWS), F32),
+            pltpu.SemaphoreType.DMA((2, CHUNKS)),
+        ],
+        compiler_params=params(36),
+        cost_estimate=took(10.0),
+    )(place, *pinned(grad), weight, mixed, rows, c)
+
+
+def plane_sums(keep, taken, first, rest, outs, combine):
+    n = len(first)
+    shape = keep.shape[1:]
+
+    def body(*refs):
+        a_hbm, b_hbm = refs[:2]
+        extra = refs[2 : 2 + len(rest)]
+        results = refs[2 + len(rest) : 2 + len(rest) + len(outs)]
+        a, b = refs[-3 - len(rest) : -1 - len(rest)]
+        local, sems = refs[-1 - len(rest) : -1], refs[-1]
+        copies = [
+            pltpu.make_async_copy(source, target, sems.at[k])
+            for k, (source, target) in enumerate(zip(extra, local, strict=True))
+        ]
+        for k, plane in enumerate(first):
+            for side, (source, target) in enumerate(((a_hbm, a), (b_hbm, b))):
+                at = len(rest) + 2 * k + side
+                copies.append(pltpu.make_async_copy(source.at[plane], target.at[k], sems.at[at]))
+        start(*copies)
+        wait(*copies)
+        combine(a, b, local, results)
+
+    return pl.pallas_call(
+        body,
+        in_specs=hbm(2 + len(rest)),
+        out_specs=vmem(len(outs)),
+        out_shape=tuple(jax.ShapeDtypeStruct(out, BF16) for out in outs),
+        scratch_shapes=[pltpu.VMEM((n,) + shape, BF16)] * 2
+        + [pltpu.VMEM(r.shape, BF16) for r in rest]
+        + [pltpu.SemaphoreType.DMA((len(rest) + 2 * n,))],
         compiler_params=params(),
-    )(place, grad, mixed, weight, rows, c)
+        cost_estimate=took(1.5),
+    )(keep, taken, *rest)
+
+
+def add(*parts):
+    total = parts[0].astype(F32)
+    for part in parts[1:]:
+        total = total + part.astype(F32)
+    return total
+
+
+def far_sums(a, b, rest, results):
+    half = a.shape[1] // 2
+    for k in range(2):
+        rows = slice(k * half, (k + 1) * half)
+        results[k][...] = add(a[0, rows], b[0, rows]).astype(BF16)
+
+
+def near_sums(a, b, rest, results):
+    half = a.shape[1] // 2
+    for k in range(2):
+        for part in range(2):
+            rows = slice(part * half, (part + 1) * half)
+            extra = (rest[k][...],) if part == k else ()
+            results[k][rows] = add(a[k, rows], b[k, rows], *extra).astype(BF16)
+
+
+def last_sum(a, b, rest, results):
+    results[0][...] = add(a[0], b[0], rest[0][...], rest[1][...]).astype(BF16)
 
 
 def arrange_kernel(place, *refs):
-    pieces, out, tokens, sems = refs[:10], refs[10], refs[11], refs[12]
+    pieces, result, tokens, out, sems = refs[:8], refs[8], refs[9], refs[10], refs[11]
     slabs, sides, share, cols = tokens.shape
     copies = []
     for side in range(2):
         core = place[1] if side == 0 else 1 - place[1]
-        steps = (0, 3, 1, 2, 2)
-        for k, piece in enumerate(pieces[side * 5 : side * 5 + 5]):
-            at = 2 * ((place[0] + steps[k]) % 4) + core
-            half = slabs // 2
-            low, many = ((0, slabs), (0, slabs), (0, slabs), (0, half), (half, half))[k]
-            target = tokens.at[low : low + many, at]
-            copies.append(pltpu.make_async_copy(piece, target, sems.at[side * 5 + k]))
+        for k, piece in enumerate(pieces[side * 4 : side * 4 + 4]):
+            at = 2 * ((place[0] + (0, 3, 1, 2)[k]) % 4) + core
+            copies.append(pltpu.make_async_copy(piece, tokens.at[:, at], sems.at[side * 4 + k]))
     for copy in copies:
         copy.start()
     for copy in copies:
         copy.wait()
     wide = sides * share
+    stores = []
     for k in range(slabs):
         out[:, k * wide : (k + 1) * wide] = tokens[k].reshape(wide, cols).T
+        if k % 4 == 3:
+            done = pl.ds((k - 3) * wide, 4 * wide)
+            stores.append(
+                pltpu.make_async_copy(out.at[:, done], result.at[:, done], sems.at[8 + k // 4])
+            )
+            start(stores[-1])
+    wait(*stores)
 
 
 def arrange(place, pieces, slabs):
@@ -384,47 +504,56 @@
     return pl.pallas_call(
         arrange_kernel,
         in_specs=smem(1) + hbm(len(views)),
-        out_specs=pl.BlockSpec(memory_space=pltpu.VMEM),
+        out_specs=hbm(1)[0],
         out_shape=jax.ShapeDtypeStruct((cols, slabs * 8 * share), BF16),
         scratch_shapes=[
             pltpu.VMEM((slabs, 8, share, cols), BF16),
-            pltpu.SemaphoreType.DMA((len(views),)),
+            pltpu.VMEM((cols, slabs * 8 * share), BF16),
+            pltpu.SemaphoreType.DMA((len(views) + slabs // 4,)),
         ],
         compiler_params=params(),
+        cost_estimate=took(3.5),
     )(place, *views)
 
 
-def weight_kernel(left, right, out, acc):
-    at = pl.program_id(0)
-
-    @pl.when(at == 0)
-    def _():
-        acc[...] = nn(left[...], right[...])
-
-    @pl.when(at > 0)
-    def _():
-        acc[...] += nn(left[...], right[...])
-
-    @pl.when(at == pl.num_programs(0) - 1)
-    def _():
-        out[...] = acc[...].astype(BF16)
+def weight_kernel(left_hbm, right_hbm, out, left, right, acc, sems):
+    steps = sems.shape[1]
+    tile = left.shape[1] // steps
+    spans = [pl.ds(n * tile, tile) for n in range(steps)]
+    loads = [
+        (
+            pltpu.make_async_copy(left_hbm.at[:, span], left.at[:, span], sems.at[0, n]),
+            pltpu.make_async_copy(right_hbm.at[span], right.at[span], sems.at[1, n]),
+        )
+        for n, span in enumerate(spans)
+    ]
+    for n in paced(loads):
+        span = slice(n * tile, (n + 1) * tile)
+        part = nn(left[:, span], right[span])
+        if n == 0:
+            acc[...] = part
+        elif n < steps - 1:
+            acc[...] += part
+        else:
+            out[...] = (acc[...] + part).astype(BF16)
 
 
 def weight_grad(left, right):
-    cols, deep = left.shape
+    cols, _ = left.shape
     wide = right.shape[1]
-    tile = 512
     return pl.pallas_call(
         weight_kernel,
-        grid=(deep // tile,),
-        in_specs=[
-            pl.BlockSpec((cols, tile), lambda i: (0, i)),
-            pl.BlockSpec((tile, wide), lambda i: (i, 0)),
+        in_specs=hbm(2),
+        out_specs=vmem(1)[0],
+        out_shape=jax.ShapeDtypeStruct((cols, wide), BF16),
+        scratch_shapes=[
+            pltpu.VMEM(left.shape, BF16),
+            pltpu.VMEM(right.shape, BF16),
+            pltpu.VMEM((cols, wide), F32),
+            pltpu.SemaphoreType.DMA((2, 4)),
         ],
-        out_specs=pl.BlockSpec((cols, wide), lambda i: (0, 0)),
-        out_shape=jax.ShapeDtypeStruct((cols, wide), BF16),
-        scratch_shapes=[pltpu.VMEM((cols, wide), F32)],
-        compiler_params=params(),
+        compiler_params=params(22),
+        cost_estimate=took(7.0),
     )(*pinned(left, right))
 
 
@@ -483,37 +612,45 @@
 
     grad_full = lax.all_gather(grad_out, "tp", axis=0, tiled=True)
     payload, rows, tab = states(bias, rate, x, dt, doc, b)
+    rows, tab = pinned(rows, tab)
     carried, decay = prefix(over_slabs(payload))
-    carried = over_slabs(carried)
+    (carried,) = pinned(over_slabs(carried))
     mixed, inner = mixer(skip, x, b, c, rows, tab, carried)
     (inner,) = pinned(inner)
     mixed_all = lax.all_gather(mixed, "ctx", axis=0, tiled=True)
     columns = lax.all_to_all(after(grad_out, decay), "ctx", 1, 0, tiled=True)
 
     keep, send, grad_mix, local = project(
-        place, grad_full, mixed.reshape(4, 2, share, WIDE), weight, rows, c
-    )
+        place, grad_full, weight, mixed.reshape(4, 2, share, WIDE), rows, c
+    )
+    local, columns, send = lax.optimization_barrier((local, columns, send))
+    c_up, c_down = up(columns), down(columns)
     local = over_slabs(local)
     taken = swap(send)
     half = share // 2
-    columns = after(columns, keep)
-    c_up, c_down = up(columns), down(columns)
-
-    next_grad = over_slabs(suffix(local, decay))
-    pair = keep.astype(F32) + taken.astype(F32)
-    far_up, far_down = up(pair[3, :half].astype(BF16)), down(pair[3, half:].astype(BF16))
-    split = columns.shape[0] // 2
-    mine = (columns, c_up, c_down, up(c_up[:split]), down(c_down[split:]))
+    keep, grad_mix = pinned(keep, grad_mix)
+    far = plane_sums(keep, taken, (3,), (), ((half, width),) * 2, far_sums)
+    far = up(far[0]), down(far[1])
+    c_far = up(c_up)
+    next_grad = suffix(local, decay)
+    next_grad, taken, grad_mix, c_down = lax.optimization_barrier(
+        (next_grad, taken, grad_mix, c_down)
+    )
+    next_grad = over_slabs(next_grad)
+    grads = inside_grads(x, b, c, rows, tab, carried, inner, grad_mix)
+    grad_c = grads[1]
+    part, b_part, cum_part = pinned(grads[0], grads[2], grads[3])
+    near = plane_sums(keep, taken, (1, 2), far, ((share, width),) * 2, near_sums)
+    near = up(near[0]), down(near[1])
+    mine = (columns, c_up, c_down, c_far)
     pieces = mine + tuple(swap(piece) for piece in mine)
-    top = jnp.concatenate([pair[1, :half] + far_up.astype(F32), pair[1, half:]], 0)
-    low = jnp.concatenate([pair[2, :half], pair[2, half:] + far_down.astype(F32)], 0)
-    from_low, from_top = up(top.astype(BF16)), down(low.astype(BF16))
-    grad_x, grad_dt, grad_b, grad_c = backward(
-        skip, rate, x, b, c, rows, tab, carried, inner, grad_mix, next_grad
-    )
-    layer_out = (pair[0] + from_low.astype(F32) + from_top.astype(F32)).astype(BF16)
     left = arrange(place, pieces, n_ctx)
-    weight_sum = weight_grad(left, mixed_all)
+    next_grad, left = lax.optimization_barrier((next_grad, left))
+    grad_x, grad_dt, grad_b = backward(
+        skip, rate, x, b, rows, tab, carried, grad_mix, part, b_part, cum_part, next_grad
+    )
+    (layer_out,) = plane_sums(keep, taken, (0,), near, ((share, width),), last_sum)
+    weight_sum = weight_grad(left, after(mixed_all, layer_out))
     return (
         layer_out,
         grad_x,

time: 168 us -> 160 us (0.952)
  blocking collectives: 44.7 us -> 31.6 us
  other arithmetic: 9.27 us -> 0.08 us
  Pallas kernels: 44.6 us -> 53.5 us
  starting transfers between devices: 28.5 us -> 34.3 us
    all_to_all x1 -> x0, blocking collectives: 13.7 us -> none  [shards(): columns = lax.all_to_all(after(grad_out, decay), 'ctx', 1, 0, tiled=True)]
    all_to_all x2, waiting for transfers between devices: 14.9 us -> 3.33 us  [over_slabs(): return lax.all_to_all(value, 'ctx', 0, 0, tiled=True)]
    ppermute x4, waiting for transfers between devices: 0.89 us -> 10.9 us  [up(): return lax.ppermute(value, 'tp', along_z(1))]
    all_to_all x2, starting transfers between devices: 7.16 us -> 13.4 us  [over_slabs(): return lax.all_to_all(value, 'ctx', 0, 0, tiled=True)]
    another operation x2 -> x0, other arithmetic: 4.1 us -> none
    ppermute x4 -> x3, starting transfers between devices: 9.43 us -> 5.51 us  [down(): return lax.ppermute(value, 'tp', along_z(-1))]
    all_to_all x0 -> x1, starting transfers between devices: none -> 3.75 us  [shards(): columns = lax.all_to_all(after(grad_out, decay), 'ctx', 1, 0, tiled=True)]
    pallas_call x2 -> x5, Pallas kernels: 25 us -> 28.7 us  [the longest x1 14.2 us: project(): pl.pallas_call(project_kernel, in_specs=smem(1) + hbm(2) + vmem(3), out_s...]
  transfers between devices with their start and end apart: 18 -> 17, of which waited for: 3 -> 4; matrix products, arithmetic and copies ran while one was open for 7% -> 1% of each run, Pallas kernels for 20% -> 29%
where the time goes in v3:
time: 160 us; the launch traced here: 159 us
  Pallas kernels  53.5 us (33%)
  starting transfers between devices  34.3 us (21%)
  blocking collectives  31.6 us (20%)
  waiting for transfers between devices  15 us (9%)
  between operations  14.3 us (9%)
  local copies, waits for them, and re-layouts  10.2 us (6%)
    all_to_all x2, blocking collectives, over_slabs(): return lax.all_to_all(value, 'ctx', 0, 0, tiled=True)  31.6 us
    pallas_call x6, Pallas kernels, staged(): pl.pallas_call(body, in_specs=hbm(n), out_specs=hbm(m), out_shape=tuple((...  19.8 us
    pallas_call x1, Pallas kernels, project(): pl.pallas_call(project_kernel, in_specs=smem(1) + hbm(2) + vmem(3), out_s...  14.2 us
    all_to_all x2, starting transfers between devices, over_slabs(): return lax.all_to_all(value, 'ctx', 0, 0, tiled=True)  13.4 us
    ppermute x4, waiting for transfers between devices, up(): return lax.ppermute(value, 'tp', along_z(1))  10.9 us
    ppermute x5, starting transfers between devices, swap(): return lax.ppermute(value, 'tp', SWAP)  9.54 us
    unnamed x22, local copies, waits for them, and re-layouts  9.31 us
    pallas_call x1, Pallas kernels, weight_grad(): pl.pallas_call(weight_kernel, in_specs=hbm(2), out_specs=vmem(1)[0], out_...  7.63 us
  transfers between devices with their start and end apart: 17, of which 4 were waited for; matrix products, arithmetic and copies ran while one was open for 1% of the time, Pallas kernels for 29%

profile of v3, /device:TPU:1, one launch (start us, length us, event | category | flops | bytes accessed | tf_op | source)
XLA Modules:
  0.0 158.9 jit_solution(15037577579621227645)
XLA Ops:
  7.9 3.3 %shard_map.145 = (bf16[16,72,256]{2,1,0:T(8,128)(2,1)S(1)}, f32[128,256]{1,0:T(8,128)S(1)}, f32[256,128]{1,0:T(8,128)S(1)}) custom-call(f32[16]{0:T(128)} %refs_0_.4, f32[16]{0:T(128)} %refs_1_.5, bf16[256,1024]{1,0:T(8,128)(2,1)} %refs_2_.3, f32[16,256]{1,0:T(8,128)} %bitcast.38, s32[1,256]{1,0:T(1,128)} %bitcast.39, bf16[256,256]{1,0:T(8,128)(2,1)} %bitcast.34), custom_call_target="tpu_custom_call" | custom-call | flops 3630000128 | tf_op jit(solution)/shard_map/pallas_call | solution.py:74
  12.5 18.6 %all_to_all.39.refs_0_ = bf16[16,72,256]{2,1,0:T(8,128)(2,1)S(1)} all-to-all(bf16[16,72,256]{2,1,0:T(8,128)(2,1)S(1)} %get-tuple-element.41), channel_id=1, replica_groups=mesh['ctx'=16,'tp'=8] {'ctx'}, dimensions={0} | all-to-all | bytes 1179648 | tf_op jit(solution)/shard_map/all_to_all | solution.py:584
  31.5 13.0 %all_to_all.40.refs_6_.refs_5_ = bf16[16,64,256]{2,1,0:T(8,128)(2,1)} all-to-all(bf16[16,64,256]{2,1,0:T(8,128)(2,1)S(1)} %get-tuple-element.42), channel_id=1, replica_groups=mesh['ctx'=16,'tp'=8] {'ctx'}, dimensions={0} | all-to-all | bytes 1048576 | tf_op jit(solution)/shard_map/all_to_all | solution.py:584
  44.5 4.5 %shard_map.147 = (bf16[256,1024]{1,0:T(8,128)(2,1)}, f32[256,1024]{1,0:T(8,128)S(1)}) custom-call(f32[16]{0:T(128)} %refs_0_.7, bf16[256,1024]{1,0:T(8,128)(2,1)} %refs_2_.3, bf16[256,256]{1,0:T(8,128)(2,1)} %bitcast.35, bf16[256,256]{1,0:T(8,128)(2,1)} %bitcast.31, f32[128,256]{1,0:T(8,128)} %copy-done.7, f32[256,128]{1,0:T(8,128)} %copy-done.8, ...), custom_call_target="tpu_custom_call" | custom-call | flops 4620000256 | tf_op jit(solution)/shard_map/pallas_call | solution.py:74
  49.0 1.0 copy-done.3
  51.0 3.8 %all-to-all-start.2 = ((bf16[32,16,512]{2,0,1:T(8,128)(2,1)}), bf16[32,16,512]{2,0,1:T(8,128)(2,1)S(1)}, u32[]{:S(2)}, u32[]{:S(2)}) async-start(bf16[32,16,512]{2,0,1:T(8,128)(2,1)} %bitcast.24), calls=%async_computation.2 | async-start | bytes 1048576 | tf_op jit(solution)/shard_map/all_to_all | solution.py:621
  54.8 14.2 %shard_map.148 = (bf16[4,32,8192]{2,1,0:T(8,128)(2,1)S(1)}, bf16[4,32,8192]{2,1,0:T(8,128)(2,1)S(1)}, bf16[256,1024]{1,0:T(8,128)(2,1)S(1)}, bf16[16,64,256]{2,1,0:T(8,128)(2,1)}) custom-call(s32[2]{0:T(128)S(1)} %pad_add_fusion.place, bf16[256,8192]{1,0:T(8,128)(2,1)} %all-gather.3.cloned.1.call-done.grad_hbm, bf16[1024,8192]{1,0:T(8,128)(2,1)} %weight_hbm.1, ...), custom_call_target="tpu_custom_call" | custom-call | flops 11000000512 | tf_op jit(solution)/shard_map/pallas_call | solution.py:390
  68.9 1.3 copy-done
  70.3 1.3 copy-done.1
  72.4 2.8 %collective-permute-start = (bf16[4,32,8192]{2,1,0:T(8,128)(2,1)}, bf16[4,32,8192]{2,1,0:T(8,128)(2,1)S(1)}, u32[]{:S(2)}, u32[]{:S(2)}) collective-permute-start(bf16[4,32,8192]{2,1,0:T(8,128)(2,1)} %copy-done), channel_id=1, source_target_pairs={{0,1},{1,0},{2,3},{3,2},{4,5},{5,4},{6,7},{7,6},{8,9},{9,8},{10,11... | collective-permute-start | bytes 6291464 | tf_op jit(solution)/shard_map/ppermute | solution.py:572
  75.2 1.7 %collective-permute-start.6 = (bf16[512,512]{1,0:T(8,128)(2,1)S(1)}, bf16[512,512]{1,0:T(8,128)(2,1)}, u32[]{:S(2)}, u32[]{:S(2)}) collective-permute-start(bf16[512,512]{1,0:T(8,128)(2,1)S(1)} %bitcast.25), channel_id=1, source_target_pairs={{0,2},{1,3},{2,4},{3,5},{4,6},{5,7},{6,0},{7,1},{8,10},{9,11},{10,... | collective-permute-start | bytes 1572872 | tf_op jit(solution)/shard_map/ppermute | solution.py:576
  76.9 6.7 %all-to-all-start.3 = ((bf16[16,64,256]{2,1,0:T(8,128)(2,1)}), bf16[16,64,256]{2,1,0:T(8,128)(2,1)S(1)}, u32[]{:S(2)}, u32[]{:S(2)}) async-start(bf16[16,64,256]{2,1,0:T(8,128)(2,1)} %get-tuple-element.49), calls=%async_computation.3 | async-start | bytes 1048576 | tf_op jit(solution)/shard_map/all_to_all | solution.py:584
  83.6 7.9 %collective-permute-done.6 = bf16[512,512]{1,0:T(8,128)(2,1)} collective-permute-done((bf16[512,512]{1,0:T(8,128)(2,1)S(1)}, bf16[512,512]{1,0:T(8,128)(2,1)}, u32[]{:S(2)}, u32[]{:S(2)}) %collective-permute-start.6) | collective-permute-done | bytes 524320 | tf_op jit(solution)/shard_map/ppermute | solution.py:576
  91.5 2.7 %collective-permute-start.1 = (bf16[512,512]{1,0:T(8,128)(2,1)S(1)}, bf16[512,512]{1,0:T(8,128)(2,1)}, u32[]{:S(2)}, u32[]{:S(2)}) collective-permute-start(bf16[512,512]{1,0:T(8,128)(2,1)S(1)} %bitcast.26), channel_id=1, source_target_pairs={{0,6},{1,7},{2,0},{3,1},{4,2},{5,3},{6,4},{7,5},{8,14},{9,15},{10,... | collective-permute-start | bytes 1572872 | tf_op jit(solution)/shard_map/ppermute | solution.py:580
  94.2 1.9 %shard_map.150 = (bf16[16,8192]{1,0:T(8,128)(2,1)}, bf16[16,8192]{1,0:T(8,128)(2,1)}) custom-call(bf16[4,32,8192]{2,1,0:T(8,128)(2,1)} %copy-done.1, bf16[4,32,8192]{2,1,0:T(8,128)(2,1)S(1)} %collective-permute-done.refs_1_), custom_call_target="tpu_custom_call" | custom-call | flops 1650000000 | tf_op jit(solution)/shard_map/pallas_call | solution.py:434
  96.2 1.2 collective-permute-start.8
  97.4 3.3 %all-to-all-done.3.refs_0_ = bf16[16,64,256]{2,1,0:T(8,128)(2,1)S(1)} async-done(((bf16[16,64,256]{2,1,0:T(8,128)(2,1)}), bf16[16,64,256]{2,1,0:T(8,128)(2,1)S(1)}, u32[]{:S(2)}, u32[]{:S(2)}) %all-to-all-start.3) | async-done | bytes 524320 | tf_op jit(solution)/shard_map/all_to_all | solution.py:584
  100.7 1.0 shard_map.149
  101.7 1.3 collective-permute-start.9
  103.0 2.9 %collective-permute-done.7 = bf16[512,512]{1,0:T(8,128)(2,1)} collective-permute-done((bf16[512,512]{1,0:T(8,128)(2,1)}, bf16[512,512]{1,0:T(8,128)(2,1)}, u32[]{:S(2)}, u32[]{:S(2)}) %collective-permute-start.7) | collective-permute-done | bytes 524320 | tf_op jit(solution)/shard_map/ppermute | solution.py:576
  105.9 2.5 %collective-permute-start.11 = (bf16[512,512]{1,0:T(8,128)(2,1)}, bf16[512,512]{1,0:T(8,128)(2,1)}, u32[]{:S(2)}, u32[]{:S(2)}) collective-permute-start(bf16[512,512]{1,0:T(8,128)(2,1)} %collective-permute-done.7), channel_id=1, source_target_pairs={{0,1},{1,0},{2,3},{3,2},{4,5},{5,4},{6,7},{7,6},{8,9},{9,8},{10,11... | collective-permute-start | bytes 1572872 | tf_op jit(solution)/shard_map/ppermute | solution.py:572
  108.7 6.7 %all-to-all-start.4 = ((bf16[16,64,256]{2,1,0:T(8,128)(2,1)}), bf16[16,64,256]{2,1,0:T(8,128)(2,1)S(1)}, u32[]{:S(2)}, u32[]{:S(2)}) async-start(bf16[16,64,256]{2,1,0:T(8,128)(2,1)} %shard_map.149), calls=%async_computation.4 | async-start | bytes 1048576 | tf_op jit(solution)/shard_map/all_to_all | solution.py:584
  115.4 1.8 %collective-permute-start.10 = (bf16[512,512]{1,0:T(8,128)(2,1)}, bf16[512,512]{1,0:T(8,128)(2,1)S(1)}, u32[]{:S(2)}, u32[]{:S(2)}) collective-permute-start(bf16[512,512]{1,0:T(8,128)(2,1)} %collective-permute-done.1), channel_id=1, source_target_pairs={{0,1},{1,0},{2,3},{3,2},{4,5},{5,4},{6,7},{7,6},{8,9},{9,8},{10,11... | collective-permute-start | bytes 1572872 | tf_op jit(solution)/shard_map/ppermute | solution.py:572
  117.2 5.5 %shard_map.153 = (f32[256,1024]{1,0:T(8,128)S(1)}, bf16[256,256]{1,0:T(8,128)(2,1)}, f32[256,256]{1,0:T(8,128)S(1)}, f32[16,256]{1,0:T(8,128)S(1)}) custom-call(bf16[256,1024]{1,0:T(8,128)(2,1)} %refs_2_.3, bf16[256,256]{1,0:T(8,128)(2,1)} %bitcast.36, bf16[256,256]{1,0:T(8,128)(2,1)} %bitcast.33, f32[128,256]{1,0:T(8,128)} %copy-done.7, ...), custom_call_target="tpu_custom_call" | custom-call | flops 5500000256 | tf_op jit(solution)/shard_map/pallas_call | solution.py:74
  122.7 1.0 copy-done.4
  124.3 2.6 %shard_map.151 = (bf16[32,8192]{1,0:T(8,128)(2,1)}, bf16[32,8192]{1,0:T(8,128)(2,1)}) custom-call(bf16[4,32,8192]{2,1,0:T(8,128)(2,1)} %copy-done.1, bf16[4,32,8192]{2,1,0:T(8,128)(2,1)S(1)} %collective-permute-done.refs_1_, bf16[16,8192]{1,0:T(8,128)(2,1)S(1)} %collective-permute-done.2.refs_2_, bf16[16,8192]{1,0:T(8,128)(2,1)} %collective-permute-done.3.refs_3_), custom_call_target="tpu_custom_call" | custom-call | flops 1650000000 | tf_op jit(solution)/shard_map/pallas_call | solution.py:434
  127.1 2.6 %collective-permute-start.5 = (bf16[32,8192]{1,0:T(8,128)(2,1)}, bf16[32,8192]{1,0:T(8,128)(2,1)}, u32[]{:S(2)}, u32[]{:S(2)}) collective-permute-start(bf16[32,8192]{1,0:T(8,128)(2,1)} %get-tuple-element.57), channel_id=1, source_target_pairs={{0,6},{1,7},{2,0},{3,1},{4,2},{5,3},{6,4},{7,5},{8,14},{9,15},{10,... | collective-permute-start | bytes 1572872 | tf_op jit(solution)/shard_map/ppermute | solution.py:580
  129.7 5.0 %shard_map.154.left_hbm = bf16[512,4096]{1,0:T(8,128)(2,1)S(1)} custom-call(s32[2]{0:T(128)S(1)} %pad_add_fusion.place, bf16[16,32,512]{2,1,0:T(8,128)(2,1)S(1)} %bitcast.28, bf16[16,32,512]{2,1,0:T(8,128)(2,1)} %bitcast.10.refs_1_, bf16[16,32,512]{2,1,0:T(8,128)(2,1)} %bitcast.11.refs_2_, bf16[16,32,512]{2,1,0:T(8,128)(2,1)} %bitcast.12.refs_3_, ...), custom_call_target="tpu_custom_call" | custom-call | flops 3849999872 | tf_op jit(solution)/shard_map/pallas_call | solution.py:504
  134.6 2.0 %copy-done.2 = bf16[512,4096]{1,0:T(8,128)(2,1)} copy-done((bf16[512,4096]{1,0:T(8,128)(2,1)}, bf16[512,4096]{1,0:T(8,128)(2,1)S(1)}, u32[]{:S(2)}) %copy-start.2) | copy-done | bytes 4194328
  136.6 5.2 %shard_map.155 = (bf16[256,1024]{1,0:T(8,128)(2,1)}, f32[16,256]{1,0:T(8,128)}, bf16[256,256]{1,0:T(8,128)(2,1)}) custom-call(f32[16]{0:T(128)} %refs_0_.7, f32[16]{0:T(128)} %refs_1_.5, bf16[256,1024]{1,0:T(8,128)(2,1)} %refs_2_.3, bf16[256,256]{1,0:T(8,128)(2,1)} %bitcast.37, f32[128,256]{1,0:T(8,128)} %copy-done.7, f32[256,128]{1,0:T(8,128)} %copy-done.8, ...), custom_call_target="tpu_custom_call" | custom-call | flops 5500000256 | tf_op jit(solution)/shard_map/pallas_call | solution.py:74
  142.0 2.4 %shard_map.152 = bf16[32,8192]{1,0:T(8,128)(2,1)} custom-call(bf16[4,32,8192]{2,1,0:T(8,128)(2,1)} %copy-done.1, bf16[4,32,8192]{2,1,0:T(8,128)(2,1)S(1)} %collective-permute-done.refs_1_, bf16[32,8192]{1,0:T(8,128)(2,1)} %collective-permute-done.4.refs_2_, bf16[32,8192]{1,0:T(8,128)(2,1)} %collective-permute-done.5.refs_3_), custom_call_target="tpu_custom_call" | custom-call | flops 1650000000 | tf_op jit(solution)/shard_map/pallas_call | solution.py:434
  144.4 7.6 %shard_map.156 = bf16[512,1024]{1,0:T(8,128)(2,1)} custom-call(bf16[512,4096]{1,0:T(8,128)(2,1)} %copy-done.2, bf16[4096,1024]{1,0:T(8,128)(2,1)} %all-gather.5.cloned.1.call-done.right_hbm), custom_call_target="tpu_custom_call" | custom-call | flops 7699999744 | tf_op jit(solution)/shard_map/pallas_call | solution.py:544
  (42 shorter events, 5.5 us)
Async XLA Ops:
  7.2 47.6 %all-gather.3.cloned.1.call-start = ((), (), s32[]{:S(2)}) async-start(), calls=%async_computation.5 | async-start | bytes 4718592 | tf_op jit(solution)/shard_map/all_gather | solution.py:613
  7.9 136.5 %all-gather.5.cloned.1.call-start = ((), (), s32[]{:S(2)}) async-start(), calls=%async_computation.6 | async-start | bytes 8912896 | tf_op jit(solution)/shard_map/all_gather | solution.py:620
  11.2 0.6 copy-start.7
  11.9 0.7 copy-start.8
  44.5 5.6 %copy-start.10 = (bf16[32,8192]{1,0:T(8,128)(2,1)S(1)}, bf16[32,8192]{1,0:T(8,128)(2,1)}, u32[]{:S(2)}) copy-start(bf16[32,8192]{1,0:T(8,128)(2,1)} %param.19) | copy-start | bytes 1572868
  49.0 1.0 copy-start.3
  51.0 21.4 %all-to-all-start.2 = ((bf16[32,16,512]{2,0,1:T(8,128)(2,1)}), bf16[32,16,512]{2,0,1:T(8,128)(2,1)S(1)}, u32[]{:S(2)}, u32[]{:S(2)}) async-start(bf16[32,16,512]{2,0,1:T(8,128)(2,1)} %bitcast.24), calls=%async_computation.2 | async-start | bytes 1048576 | tf_op jit(solution)/shard_map/all_to_all | solution.py:621
  68.9 1.4 copy-start
  70.3 1.3 copy-start.1
  71.6 0.8 copy-start.5
  72.4 21.8 %collective-permute-start = (bf16[4,32,8192]{2,1,0:T(8,128)(2,1)}, bf16[4,32,8192]{2,1,0:T(8,128)(2,1)S(1)}, u32[]{:S(2)}, u32[]{:S(2)}) collective-permute-start(bf16[4,32,8192]{2,1,0:T(8,128)(2,1)} %copy-done), channel_id=1, source_target_pairs={{0,1},{1,0},{2,3},{3,2},{4,5},{5,4},{6,7},{7,6},{8,9},{9,8},{10,11... | collective-permute-start | bytes 6291464 | tf_op jit(solution)/shard_map/ppermute | solution.py:572
  75.2 16.3 %collective-permute-start.6 = (bf16[512,512]{1,0:T(8,128)(2,1)S(1)}, bf16[512,512]{1,0:T(8,128)(2,1)}, u32[]{:S(2)}, u32[]{:S(2)}) collective-permute-start(bf16[512,512]{1,0:T(8,128)(2,1)S(1)} %bitcast.25), channel_id=1, source_target_pairs={{0,2},{1,3},{2,4},{3,5},{4,6},{5,7},{6,0},{7,1},{8,10},{9,11},{10,... | collective-permute-start | bytes 1572872 | tf_op jit(solution)/shard_map/ppermute | solution.py:576
  76.9 23.9 %all-to-all-start.3 = ((bf16[16,64,256]{2,1,0:T(8,128)(2,1)}), bf16[16,64,256]{2,1,0:T(8,128)(2,1)S(1)}, u32[]{:S(2)}, u32[]{:S(2)}) async-start(bf16[16,64,256]{2,1,0:T(8,128)(2,1)} %get-tuple-element.49), calls=%async_computation.3 | async-start | bytes 1048576 | tf_op jit(solution)/shard_map/all_to_all | solution.py:584
  91.5 14.4 %collective-permute-start.7 = (bf16[512,512]{1,0:T(8,128)(2,1)}, bf16[512,512]{1,0:T(8,128)(2,1)}, u32[]{:S(2)}, u32[]{:S(2)}) collective-permute-start(bf16[512,512]{1,0:T(8,128)(2,1)} %collective-permute-done.6), channel_id=1, source_target_pairs={{0,2},{1,3},{2,4},{3,5},{4,6},{5,7},{6,0},{7,1},{8,10},{9,11},{10,... | collective-permute-start | bytes 1572872 | tf_op jit(solution)/shard_map/ppermute | solution.py:576
  91.5 16.9 %collective-permute-start.1 = (bf16[512,512]{1,0:T(8,128)(2,1)S(1)}, bf16[512,512]{1,0:T(8,128)(2,1)}, u32[]{:S(2)}, u32[]{:S(2)}) collective-permute-start(bf16[512,512]{1,0:T(8,128)(2,1)S(1)} %bitcast.26), channel_id=1, source_target_pairs={{0,6},{1,7},{2,0},{3,1},{4,2},{5,3},{6,4},{7,5},{8,14},{9,15},{10,... | collective-permute-start | bytes 1572872 | tf_op jit(solution)/shard_map/ppermute | solution.py:580
  96.1 19.3 %collective-permute-start.2 = (bf16[16,8192]{1,0:T(8,128)(2,1)}, bf16[16,8192]{1,0:T(8,128)(2,1)S(1)}, u32[]{:S(2)}, u32[]{:S(2)}) collective-permute-start(bf16[16,8192]{1,0:T(8,128)(2,1)} %get-tuple-element.54), channel_id=1, source_target_pairs={{0,2},{1,3},{2,4},{3,5},{4,6},{5,7},{6,0},{7,1},{8,10},{9,11},{10,... | collective-permute-start | bytes 786440 | tf_op jit(solution)/shard_map/ppermute | solution.py:576
  96.2 30.9 %collective-permute-start.8 = (bf16[512,512]{1,0:T(8,128)(2,1)S(1)}, bf16[512,512]{1,0:T(8,128)(2,1)}, u32[]{:S(2)}, u32[]{:S(2)}) collective-permute-start(bf16[512,512]{1,0:T(8,128)(2,1)S(1)} %bitcast.27), channel_id=1, source_target_pairs={{0,1},{1,0},{2,3},{3,2},{4,5},{5,4},{6,7},{7,6},{8,9},{9,8},{10,11... | collective-permute-start | bytes 1572872 | tf_op jit(solution)/shard_map/ppermute | solution.py:572
  101.7 27.9 %collective-permute-start.9 = (bf16[512,512]{1,0:T(8,128)(2,1)}, bf16[512,512]{1,0:T(8,128)(2,1)}, u32[]{:S(2)}, u32[]{:S(2)}) collective-permute-start(bf16[512,512]{1,0:T(8,128)(2,1)} %collective-permute-done.6), channel_id=1, source_target_pairs={{0,1},{1,0},{2,3},{3,2},{4,5},{5,4},{6,7},{7,6},{8,9},{9,8},{10,11... | collective-permute-start | bytes 1572872 | tf_op jit(solution)/shard_map/ppermute | solution.py:572
  105.9 23.7 %collective-permute-start.11 = (bf16[512,512]{1,0:T(8,128)(2,1)}, bf16[512,512]{1,0:T(8,128)(2,1)}, u32[]{:S(2)}, u32[]{:S(2)}) collective-permute-start(bf16[512,512]{1,0:T(8,128)(2,1)} %collective-permute-done.7), channel_id=1, source_target_pairs={{0,1},{1,0},{2,3},{3,2},{4,5},{5,4},{6,7},{7,6},{8,9},{9,8},{10,11... | collective-permute-start | bytes 1572872 | tf_op jit(solution)/shard_map/ppermute | solution.py:572
  108.4 15.9 %collective-permute-start.3 = (bf16[16,8192]{1,0:T(8,128)(2,1)}, bf16[16,8192]{1,0:T(8,128)(2,1)}, u32[]{:S(2)}, u32[]{:S(2)}) collective-permute-start(bf16[16,8192]{1,0:T(8,128)(2,1)} %get-tuple-element.55), channel_id=1, source_target_pairs={{0,6},{1,7},{2,0},{3,1},{4,2},{5,3},{6,4},{7,5},{8,14},{9,15},{10,... | collective-permute-start | bytes 786440 | tf_op jit(solution)/shard_map/ppermute | solution.py:580
  108.7 27.9 %all-to-all-start.4 = ((bf16[16,64,256]{2,1,0:T(8,128)(2,1)}), bf16[16,64,256]{2,1,0:T(8,128)(2,1)S(1)}, u32[]{:S(2)}, u32[]{:S(2)}) async-start(bf16[16,64,256]{2,1,0:T(8,128)(2,1)} %shard_map.149), calls=%async_computation.4 | async-start | bytes 1048576 | tf_op jit(solution)/shard_map/all_to_all | solution.py:584
  115.4 14.2 %collective-permute-start.10 = (bf16[512,512]{1,0:T(8,128)(2,1)}, bf16[512,512]{1,0:T(8,128)(2,1)S(1)}, u32[]{:S(2)}, u32[]{:S(2)}) collective-permute-start(bf16[512,512]{1,0:T(8,128)(2,1)} %collective-permute-done.1), channel_id=1, source_target_pairs={{0,1},{1,0},{2,3},{3,2},{4,5},{5,4},{6,7},{7,6},{8,9},{9,8},{10,11... | collective-permute-start | bytes 1572872 | tf_op jit(solution)/shard_map/ppermute | solution.py:572
  122.7 1.0 copy-start.4
  123.7 0.6 copy-start.9
  124.3 5.4 %copy-start.6 = (f32[256,256]{1,0:T(8,128)}, f32[256,256]{1,0:T(8,128)S(1)}, u32[]{:S(2)}) copy-start(f32[256,256]{1,0:T(8,128)S(1)} %get-tuple-element.61.refs_9_) | copy-start | bytes 786436
  126.9 15.1 %collective-permute-start.4 = (bf16[32,8192]{1,0:T(8,128)(2,1)}, bf16[32,8192]{1,0:T(8,128)(2,1)}, u32[]{:S(2)}, u32[]{:S(2)}) collective-permute-start(bf16[32,8192]{1,0:T(8,128)(2,1)} %get-tuple-element.56), channel_id=1, source_target_pairs={{0,2},{1,3},{2,4},{3,5},{4,6},{5,7},{6,0},{7,1},{8,10},{9,11},{10,... | collective-permute-start | bytes 1572872 | tf_op jit(solution)/shard_map/ppermute | solution.py:576
  127.1 14.9 %collective-permute-start.5 = (bf16[32,8192]{1,0:T(8,128)(2,1)}, bf16[32,8192]{1,0:T(8,128)(2,1)}, u32[]{:S(2)}, u32[]{:S(2)}) collective-permute-start(bf16[32,8192]{1,0:T(8,128)(2,1)} %get-tuple-element.57), channel_id=1, source_target_pairs={{0,6},{1,7},{2,0},{3,1},{4,2},{5,3},{6,4},{7,5},{8,14},{9,15},{10,... | collective-permute-start | bytes 1572872 | tf_op jit(solution)/shard_map/ppermute | solution.py:580
  134.6 2.0 %copy-start.2 = (bf16[512,4096]{1,0:T(8,128)(2,1)}, bf16[512,4096]{1,0:T(8,128)(2,1)S(1)}, u32[]{:S(2)}) copy-start(bf16[512,4096]{1,0:T(8,128)(2,1)S(1)} %shard_map.154.left_hbm) | copy-start | bytes 12582916
Sparse Core Ops, SparseCore 0:
  9.7 35.9 all-gather.2
  50.1 82.8 all-gather.4

commit v4 on v3

--- a/solution.py
+++ b/solution.py
@@ -47,7 +47,7 @@
     return [pltpu.with_memory_space_constraint(a, pltpu.HBM) for a in arrays]
 
 
-def staged(kernel, scalars, arrays, outs, us):
+def staged(kernel, scalars, arrays, outs, us, mib=16):
     given = list(scalars) + list(arrays)
     n, m = len(given), len(outs)
 
@@ -80,7 +80,7 @@
         + [pltpu.VMEM(a.shape, a.dtype) for a in arrays]
         + [pltpu.VMEM(*out) for out in outs]
         + [pltpu.SemaphoreType.DMA((n + m,))],
-        compiler_params=params(),
+        compiler_params=params(mib),
         cost_estimate=took(us),
     )(*given)
 
@@ -210,7 +210,7 @@
 
 def mixer(skip, x, b, c, rows, tab, carried):
     outs = [((ROWS, WIDE), BF16), ((ROWS, WIDE), F32)]
-    return staged(mixer_kernel, (skip,), (x, b, c, rows, tab, carried), outs, 4.2)
+    return staged(mixer_kernel, (skip,), (x, b, c, rows, tab, carried), outs, 4.2, 60)
 
 
 def head_sums(pair, values):
@@ -261,7 +261,7 @@
         ((ROWS, STATE), F32),
         ((HEADS, ROWS), F32),
     ]
-    return staged(inside_kernel, (), (x, b, c, rows, tab, carried, inner, grad), outs, 5.0)
+    return staged(inside_kernel, (), (x, b, c, rows, tab, carried, inner, grad), outs, 5.0, 60)
 
 
 def backward_kernel(
@@ -404,7 +404,7 @@
             pltpu.VMEM((inner, ROWS), F32),
             pltpu.SemaphoreType.DMA((2, CHUNKS)),
         ],
-        compiler_params=params(36),
+        compiler_params=params(60),
         cost_estimate=took(10.0),
     )(place, *pinned(grad), weight, mixed, rows, c)
 
@@ -441,7 +441,7 @@
         + [pltpu.SemaphoreType.DMA((len(rest) + 2 * n,))],
         compiler_params=params(),
         cost_estimate=took(1.5),
-    )(keep, taken, *rest)
+    )(*pinned(keep, taken, *rest))
 
 
 def add(*parts):
@@ -511,7 +511,7 @@
             pltpu.VMEM((cols, slabs * 8 * share), BF16),
             pltpu.SemaphoreType.DMA((len(views) + slabs // 4,)),
         ],
-        compiler_params=params(),
+        compiler_params=params(60),
         cost_estimate=took(3.5),
     )(place, *views)
 
@@ -612,7 +612,6 @@
 
     grad_full = lax.all_gather(grad_out, "tp", axis=0, tiled=True)
     payload, rows, tab = states(bias, rate, x, dt, doc, b)
-    rows, tab = pinned(rows, tab)
     carried, decay = prefix(over_slabs(payload))
     (carried,) = pinned(over_slabs(carried))
     mixed, inner = mixer(skip, x, b, c, rows, tab, carried)
@@ -628,29 +627,29 @@
     local = over_slabs(local)
     taken = swap(send)
     half = share // 2
-    keep, grad_mix = pinned(keep, grad_mix)
+    (grad_mix,) = pinned(grad_mix)
     far = plane_sums(keep, taken, (3,), (), ((half, width),) * 2, far_sums)
     far = up(far[0]), down(far[1])
+    next_grad = suffix(local, decay)
+    next_grad, grad_mix, c_up, c_down = lax.optimization_barrier(
+        (next_grad, grad_mix, c_up, c_down)
+    )
     c_far = up(c_up)
-    next_grad = suffix(local, decay)
-    next_grad, taken, grad_mix, c_down = lax.optimization_barrier(
-        (next_grad, taken, grad_mix, c_down)
-    )
     next_grad = over_slabs(next_grad)
     grads = inside_grads(x, b, c, rows, tab, carried, inner, grad_mix)
     grad_c = grads[1]
+    next_grad, taken, c_down = lax.optimization_barrier((next_grad, taken, c_down))
     part, b_part, cum_part = pinned(grads[0], grads[2], grads[3])
     near = plane_sums(keep, taken, (1, 2), far, ((share, width),) * 2, near_sums)
     near = up(near[0]), down(near[1])
-    mine = (columns, c_up, c_down, c_far)
+    mine = (after(columns, taken), c_up, c_down, after(c_far, taken))
     pieces = mine + tuple(swap(piece) for piece in mine)
     left = arrange(place, pieces, n_ctx)
-    next_grad, left = lax.optimization_barrier((next_grad, left))
     grad_x, grad_dt, grad_b = backward(
         skip, rate, x, b, rows, tab, carried, grad_mix, part, b_part, cum_part, next_grad
     )
     (layer_out,) = plane_sums(keep, taken, (0,), near, ((share, width),), last_sum)
-    weight_sum = weight_grad(left, after(mixed_all, layer_out))
+    weight_sum = weight_grad(left, after(mixed_all, grad_x))
     return (
         layer_out,
         grad_x,

time: 160 us -> 157 us (0.981)
  local copies, waits for them, and re-layouts: 10.2 us -> 3.29 us
  waiting for transfers between devices: 15 us -> 18.4 us
    all_to_all x2, waiting for transfers between devices: 3.33 us -> 14.2 us  [over_slabs(): return lax.all_to_all(value, 'ctx', 0, 0, tiled=True)]
    ppermute x4, waiting for transfers between devices: 10.9 us -> 3.47 us  [up(): return lax.ppermute(value, 'tp', along_z(1))]
    unnamed x22 -> x20, local copies, waits for them, and re-layouts: 9.31 us -> 2.45 us
    ppermute x5, starting transfers between devices: 9.54 us -> 6.46 us  [swap(): return lax.ppermute(value, 'tp', SWAP)]
    ppermute x4, starting transfers between devices: 1.98 us -> 4.95 us  [up(): return lax.ppermute(value, 'tp', along_z(1))]
  transfers between devices with their start and end apart: 17 -> 17, of which waited for: 4 -> 4; matrix products, arithmetic and copies ran while one was open for 1% -> 1% of each run, Pallas kernels for 29% -> 30%
where the time goes in v4:
time: 157 us; the launch traced here: 156 us
  Pallas kernels  54.7 us (35%)
  starting transfers between devices  33.3 us (21%)
  blocking collectives  31.7 us (20%)
  waiting for transfers between devices  18.4 us (12%)
  between operations  14.3 us (9%)
  local copies, waits for them, and re-layouts  3.29 us (2%)
    all_to_all x2, blocking collectives, over_slabs(): return lax.all_to_all(value, 'ctx', 0, 0, tiled=True)  31.7 us
    pallas_call x6, Pallas kernels, staged(): pl.pallas_call(body, in_specs=hbm(n), out_specs=hbm(m), out_shape=tuple((...  20.4 us
    pallas_call x1, Pallas kernels, project(): pl.pallas_call(project_kernel, in_specs=smem(1) + hbm(2) + vmem(3), out_s...  15.3 us
    all_to_all x2, waiting for transfers between devices, over_slabs(): return lax.all_to_all(value, 'ctx', 0, 0, tiled=True)  14.2 us
    all_to_all x2, starting transfers between devices, over_slabs(): return lax.all_to_all(value, 'ctx', 0, 0, tiled=True)  13.2 us
    pallas_call x1, Pallas kernels, weight_grad(): pl.pallas_call(weight_kernel, in_specs=hbm(2), out_specs=vmem(1)[0], out_...  7.63 us
    ppermute x5, starting transfers between devices, swap(): return lax.ppermute(value, 'tp', SWAP)  6.46 us
    pallas_call x3, Pallas kernels, plane_sums(): pl.pallas_call(body, in_specs=hbm(2 + len(rest)), out_specs=vmem(len(outs...  6.01 us
  transfers between devices with their start and end apart: 17, of which 4 were waited for; matrix products, arithmetic and copies ran while one was open for 1% of the time, Pallas kernels for 30%

profile of v4, /device:TPU:1, one launch (start us, length us, event | category | flops | bytes accessed | tf_op | source)
XLA Modules:
  0.0 156.2 jit_solution(10380064951822162705)
XLA Ops:
  7.2 0.7 all-gather.3.cloned.1.call-update
  7.9 3.3 %shard_map.145 = (bf16[16,72,256]{2,1,0:T(8,128)(2,1)S(1)}, f32[128,256]{1,0:T(8,128)S(1)}, f32[256,128]{1,0:T(8,128)S(1)}) custom-call(f32[16]{0:T(128)} %refs_0_.4, f32[16]{0:T(128)} %refs_1_.5, bf16[256,1024]{1,0:T(8,128)(2,1)} %refs_2_.3, f32[16,256]{1,0:T(8,128)} %bitcast.41, s32[1,256]{1,0:T(1,128)} %bitcast.42, bf16[256,256]{1,0:T(8,128)(2,1)} %bitcast.37), custom_call_target="tpu_custom_call" | custom-call | flops 3630000128 | tf_op jit(solution)/shard_map/pallas_call | solution.py:74
  11.2 18.7 %all_to_all.39.refs_0_ = bf16[16,72,256]{2,1,0:T(8,128)(2,1)S(1)} all-to-all(bf16[16,72,256]{2,1,0:T(8,128)(2,1)S(1)} %get-tuple-element.44), channel_id=1, replica_groups=mesh['ctx'=16,'tp'=8] {'ctx'}, dimensions={0} | all-to-all | bytes 1179648 | tf_op jit(solution)/shard_map/all_to_all | solution.py:584
  30.2 13.0 %all_to_all.40.refs_6_.refs_5_ = bf16[16,64,256]{2,1,0:T(8,128)(2,1)} all-to-all(bf16[16,64,256]{2,1,0:T(8,128)(2,1)S(1)} %get-tuple-element.45), channel_id=1, replica_groups=mesh['ctx'=16,'tp'=8] {'ctx'}, dimensions={0} | all-to-all | bytes 1048576 | tf_op jit(solution)/shard_map/all_to_all | solution.py:584
  43.3 4.8 %shard_map.147 = (bf16[256,1024]{1,0:T(8,128)(2,1)}, f32[256,1024]{1,0:T(8,128)}) custom-call(f32[16]{0:T(128)} %refs_0_.7, bf16[256,1024]{1,0:T(8,128)(2,1)} %refs_2_.3, bf16[256,256]{1,0:T(8,128)(2,1)} %bitcast.38, bf16[256,256]{1,0:T(8,128)(2,1)} %bitcast.34, f32[128,256]{1,0:T(8,128)} %copy-done, f32[256,128]{1,0:T(8,128)} %copy-done.2, ...), custom_call_target="tpu_custom_call" | custom-call | flops 4620000256 | tf_op jit(solution)/shard_map/pallas_call | solution.py:74
  48.8 0.8 copy.20
  49.6 3.8 %all-to-all-start.2 = ((bf16[32,16,512]{2,0,1:T(8,128)(2,1)}), bf16[32,16,512]{2,0,1:T(8,128)(2,1)S(1)}, u32[]{:S(2)}, u32[]{:S(2)}) async-start(bf16[32,16,512]{2,0,1:T(8,128)(2,1)} %bitcast.24), calls=%async_computation.2 | async-start | bytes 1048576 | tf_op jit(solution)/shard_map/all_to_all | solution.py:620
  53.4 15.3 %shard_map.148 = (bf16[4,32,8192]{2,1,0:T(8,128)(2,1)}, bf16[4,32,8192]{2,1,0:T(8,128)(2,1)}, bf16[256,1024]{1,0:T(8,128)(2,1)}, bf16[16,64,256]{2,1,0:T(8,128)(2,1)}) custom-call(s32[2]{0:T(128)} %pad_add_fusion.place, bf16[256,8192]{1,0:T(8,128)(2,1)} %all-gather.3.cloned.1.call-done.grad_hbm, bf16[1024,8192]{1,0:T(8,128)(2,1)} %weight_hbm.1, ...), custom_call_target="tpu_custom_call" | custom-call | flops 11000000512 | tf_op jit(solution)/shard_map/pallas_call | solution.py:390
  68.7 3.0 %collective-permute-start.2 = (bf16[4,32,8192]{2,1,0:T(8,128)(2,1)}, bf16[4,32,8192]{2,1,0:T(8,128)(2,1)S(1)}, u32[]{:S(2)}, u32[]{:S(2)}) collective-permute-start(bf16[4,32,8192]{2,1,0:T(8,128)(2,1)} %get-tuple-element.56), channel_id=1, source_target_pairs={{0,1},{1,0},{2,3},{3,2},{4,5},{5,4},{6,7},{7,6},{8,9},{9,8},{10,11... | collective-permute-start | bytes 6291464 | tf_op jit(solution)/shard_map/ppermute | solution.py:572
  71.7 6.7 %all-to-all-start.3 = ((bf16[16,64,256]{2,1,0:T(8,128)(2,1)}), bf16[16,64,256]{2,1,0:T(8,128)(2,1)S(1)}, u32[]{:S(2)}, u32[]{:S(2)}) async-start(bf16[16,64,256]{2,1,0:T(8,128)(2,1)} %get-tuple-element.52), calls=%async_computation.3 | async-start | bytes 1048576 | tf_op jit(solution)/shard_map/all_to_all | solution.py:584
  78.4 1.8 %collective-permute-start = (bf16[512,512]{1,0:T(8,128)(2,1)S(1)}, bf16[512,512]{1,0:T(8,128)(2,1)}, u32[]{:S(2)}, u32[]{:S(2)}) collective-permute-start(bf16[512,512]{1,0:T(8,128)(2,1)S(1)} %bitcast.27), channel_id=1, source_target_pairs={{0,2},{1,3},{2,4},{3,5},{4,6},{5,7},{6,0},{7,1},{8,10},{9,11},{10,... | collective-permute-start | bytes 1572872 | tf_op jit(solution)/shard_map/ppermute | solution.py:576
  80.2 2.2 %collective-permute-start.1 = (bf16[512,512]{1,0:T(8,128)(2,1)S(1)}, bf16[512,512]{1,0:T(8,128)(2,1)}, u32[]{:S(2)}, u32[]{:S(2)}) collective-permute-start(bf16[512,512]{1,0:T(8,128)(2,1)S(1)} %bitcast.28), channel_id=1, source_target_pairs={{0,6},{1,7},{2,0},{3,1},{4,2},{5,3},{6,4},{7,5},{8,14},{9,15},{10,... | collective-permute-start | bytes 1572872 | tf_op jit(solution)/shard_map/ppermute | solution.py:580
  82.4 7.9 %all-to-all-done.3.refs_0_ = bf16[16,64,256]{2,1,0:T(8,128)(2,1)S(1)} async-done(((bf16[16,64,256]{2,1,0:T(8,128)(2,1)}), bf16[16,64,256]{2,1,0:T(8,128)(2,1)S(1)}, u32[]{:S(2)}, u32[]{:S(2)}) %all-to-all-start.3) | async-done | bytes 524320 | tf_op jit(solution)/shard_map/all_to_all | solution.py:584
  90.3 1.0 shard_map.149
  91.3 3.2 %collective-permute-done = bf16[512,512]{1,0:T(8,128)(2,1)} collective-permute-done((bf16[512,512]{1,0:T(8,128)(2,1)S(1)}, bf16[512,512]{1,0:T(8,128)(2,1)}, u32[]{:S(2)}, u32[]{:S(2)}) %collective-permute-start) | collective-permute-done | bytes 524320 | tf_op jit(solution)/shard_map/ppermute | solution.py:576
  94.8 1.9 %collective-permute-start.9 = (bf16[512,512]{1,0:T(8,128)(2,1)}, bf16[512,512]{1,0:T(8,128)(2,1)}, u32[]{:S(2)}, u32[]{:S(2)}) collective-permute-start(bf16[512,512]{1,0:T(8,128)(2,1)} %collective-permute-done), channel_id=1, source_target_pairs={{0,1},{1,0},{2,3},{3,2},{4,5},{5,4},{6,7},{7,6},{8,9},{9,8},{10,11... | collective-permute-start | bytes 1572872 | tf_op jit(solution)/shard_map/ppermute | solution.py:572
  96.7 6.5 %all-to-all-start.4 = ((bf16[16,64,256]{2,1,0:T(8,128)(2,1)}), bf16[16,64,256]{2,1,0:T(8,128)(2,1)S(1)}, u32[]{:S(2)}, u32[]{:S(2)}) async-start(bf16[16,64,256]{2,1,0:T(8,128)(2,1)} %shard_map.149), calls=%async_computation.4 | async-start | bytes 1048576 | tf_op jit(solution)/shard_map/all_to_all | solution.py:584
  103.2 1.3 copy-done.6
  104.5 1.4 shard_map.150
  105.9 1.4 collective-permute-start.3
  107.3 1.3 collective-permute-start.4
  108.6 5.6 %shard_map.153 = (f32[256,1024]{1,0:T(8,128)}, bf16[256,256]{1,0:T(8,128)(2,1)}, f32[256,256]{1,0:T(8,128)}, f32[16,256]{1,0:T(8,128)}) custom-call(bf16[256,1024]{1,0:T(8,128)(2,1)} %refs_2_.3, bf16[256,256]{1,0:T(8,128)(2,1)} %bitcast.39, bf16[256,256]{1,0:T(8,128)(2,1)} %bitcast.36, f32[128,256]{1,0:T(8,128)} %copy-done, f32[256,128]{1,0:T(8,128)} %copy-done.2, ...), custom_call_target="tpu_custom_call" | custom-call | flops 5500000256 | tf_op jit(solution)/shard_map/pallas_call | solution.py:74
  114.3 6.3 %all-to-all-done.4.refs_11_ = bf16[16,64,256]{2,1,0:T(8,128)(2,1)S(1)} async-done(((bf16[16,64,256]{2,1,0:T(8,128)(2,1)}), bf16[16,64,256]{2,1,0:T(8,128)(2,1)S(1)}, u32[]{:S(2)}, u32[]{:S(2)}) %all-to-all-start.4) | async-done | bytes 524320 | tf_op jit(solution)/shard_map/all_to_all | solution.py:584
  120.5 1.1 collective-permute-start.8
  122.2 2.0 %shard_map.151 = (bf16[32,8192]{1,0:T(8,128)(2,1)S(1)}, bf16[32,8192]{1,0:T(8,128)(2,1)S(1)}) custom-call(bf16[4,32,8192]{2,1,0:T(8,128)(2,1)} %get-tuple-element.47.refs_0_, bf16[4,32,8192]{2,1,0:T(8,128)(2,1)} %copy-done.6, bf16[16,8192]{1,0:T(8,128)(2,1)} %collective-permute-done.3.refs_2_, bf16[16,8192]{1,0:T(8,128)(2,1)} %collective-permute-done.4.refs_3_), custom_call_target="tpu_custom_call" | custom-call | flops 1650000000 | tf_op jit(solution)/shard_map/pallas_call | solution.py:434
  124.2 1.5 collective-permute-start.5
  125.7 1.3 collective-permute-start.6
  127.0 5.3 %shard_map.154 = (bf16[256,1024]{1,0:T(8,128)(2,1)}, f32[16,256]{1,0:T(8,128)}, bf16[256,256]{1,0:T(8,128)(2,1)}) custom-call(f32[16]{0:T(128)} %refs_0_.7, f32[16]{0:T(128)} %refs_1_.5, bf16[256,1024]{1,0:T(8,128)(2,1)} %refs_2_.3, bf16[256,256]{1,0:T(8,128)(2,1)} %bitcast.40, f32[128,256]{1,0:T(8,128)S(1)} %copy-done.1, f32[256,128]{1,0:T(8,128)S(1)} %copy-done.3, ...), custom_call_target="tpu_custom_call" | custom-call | flops 5500000256 | tf_op jit(solution)/shard_map/pallas_call | solution.py:74
  132.4 0.7 copy-done.7
  133.5 5.3 %shard_map.155.left_hbm = bf16[512,4096]{1,0:T(8,128)(2,1)} custom-call(s32[2]{0:T(128)} %pad_add_fusion.place, bf16[16,32,512]{2,1,0:T(8,128)(2,1)} %bitcast.30, bf16[16,32,512]{2,1,0:T(8,128)(2,1)} %bitcast.13.refs_1_, bf16[16,32,512]{2,1,0:T(8,128)(2,1)} %bitcast.14.refs_2_, bf16[16,32,512]{2,1,0:T(8,128)(2,1)} %bitcast.15.refs_3_, ...), custom_call_target="tpu_custom_call" | custom-call | flops 3849999872 | tf_op jit(solution)/shard_map/pallas_call | solution.py:504
  139.1 2.6 %shard_map.152 = bf16[32,8192]{1,0:T(8,128)(2,1)} custom-call(bf16[4,32,8192]{2,1,0:T(8,128)(2,1)} %get-tuple-element.47.refs_0_, bf16[4,32,8192]{2,1,0:T(8,128)(2,1)} %copy-done.6, bf16[32,8192]{1,0:T(8,128)(2,1)} %collective-permute-done.5.refs_2_, bf16[32,8192]{1,0:T(8,128)(2,1)} %collective-permute-done.6.refs_3_), custom_call_target="tpu_custom_call" | custom-call | flops 1650000000 | tf_op jit(solution)/shard_map/pallas_call | solution.py:434
  141.7 7.6 %shard_map.156 = bf16[512,1024]{1,0:T(8,128)(2,1)} custom-call(bf16[512,4096]{1,0:T(8,128)(2,1)} %shard_map.155.left_hbm, bf16[4096,1024]{1,0:T(8,128)(2,1)} %all-gather.5.cloned.1.call-done.right_hbm), custom_call_target="tpu_custom_call" | custom-call | flops 7699999744 | tf_op jit(solution)/shard_map/pallas_call | solution.py:544
  (40 shorter events, 2.6 us)
Async XLA Ops:
  7.2 46.2 %all-gather.3.cloned.1.call-start = ((), (), s32[]{:S(2)}) async-start(), calls=%async_computation.5 | async-start | bytes 4718592 | tf_op jit(solution)/shard_map/all_gather | solution.py:613
  7.9 133.8 %all-gather.5.cloned.1.call-start = ((), (), s32[]{:S(2)}) async-start(), calls=%async_computation.6 | async-start | bytes 8912896 | tf_op jit(solution)/shard_map/all_gather | solution.py:619
  11.2 32.0 %copy-start = (f32[128,256]{1,0:T(8,128)}, f32[128,256]{1,0:T(8,128)S(1)}, u32[]{:S(2)}) copy-start(f32[128,256]{1,0:T(8,128)S(1)} %get-tuple-element.42.refs_4_.rows.refs_3_) | copy-start | bytes 393220
  11.2 32.0 %copy-start.2 = (f32[256,128]{1,0:T(8,128)}, f32[256,128]{1,0:T(8,128)S(1)}, u32[]{:S(2)}) copy-start(f32[256,128]{1,0:T(8,128)S(1)} %get-tuple-element.43.refs_5_.refs_4_) | copy-start | bytes 393220
  43.2 5.5 %copy-start.4 = (bf16[32,8192]{1,0:T(8,128)(2,1)S(1)}, bf16[32,8192]{1,0:T(8,128)(2,1)}, u32[]{:S(2)}) copy-start(bf16[32,8192]{1,0:T(8,128)(2,1)} %param.19) | copy-start | bytes 1572868
  49.6 19.1 %all-to-all-start.2 = ((bf16[32,16,512]{2,0,1:T(8,128)(2,1)}), bf16[32,16,512]{2,0,1:T(8,128)(2,1)S(1)}, u32[]{:S(2)}, u32[]{:S(2)}) async-start(bf16[32,16,512]{2,0,1:T(8,128)(2,1)} %bitcast.24), calls=%async_computation.2 | async-start | bytes 1048576 | tf_op jit(solution)/shard_map/all_to_all | solution.py:620
  68.7 51.8 %copy-start.5 = (bf16[32,16,512]{2,0,1:T(8,128)(2,1)}, bf16[32,16,512]{2,0,1:T(8,128)(2,1)S(1)}, u32[]{:S(2)}) copy-start(bf16[32,16,512]{2,0,1:T(8,128)(2,1)S(1)} %all-to-all-done.2) | copy-start | bytes 1572868
  68.7 34.4 %collective-permute-start.2 = (bf16[4,32,8192]{2,1,0:T(8,128)(2,1)}, bf16[4,32,8192]{2,1,0:T(8,128)(2,1)S(1)}, u32[]{:S(2)}, u32[]{:S(2)}) collective-permute-start(bf16[4,32,8192]{2,1,0:T(8,128)(2,1)} %get-tuple-element.56), channel_id=1, source_target_pairs={{0,1},{1,0},{2,3},{3,2},{4,5},{5,4},{6,7},{7,6},{8,9},{9,8},{10,11... | collective-permute-start | bytes 6291464 | tf_op jit(solution)/shard_map/ppermute | solution.py:572
  71.7 18.6 %all-to-all-start.3 = ((bf16[16,64,256]{2,1,0:T(8,128)(2,1)}), bf16[16,64,256]{2,1,0:T(8,128)(2,1)S(1)}, u32[]{:S(2)}, u32[]{:S(2)}) async-start(bf16[16,64,256]{2,1,0:T(8,128)(2,1)} %get-tuple-element.52), calls=%async_computation.3 | async-start | bytes 1048576 | tf_op jit(solution)/shard_map/all_to_all | solution.py:584
  78.4 16.1 %collective-permute-start = (bf16[512,512]{1,0:T(8,128)(2,1)S(1)}, bf16[512,512]{1,0:T(8,128)(2,1)}, u32[]{:S(2)}, u32[]{:S(2)}) collective-permute-start(bf16[512,512]{1,0:T(8,128)(2,1)S(1)} %bitcast.27), channel_id=1, source_target_pairs={{0,2},{1,3},{2,4},{3,5},{4,6},{5,7},{6,0},{7,1},{8,10},{9,11},{10,... | collective-permute-start | bytes 1572872 | tf_op jit(solution)/shard_map/ppermute | solution.py:576
  80.2 14.3 %collective-permute-start.1 = (bf16[512,512]{1,0:T(8,128)(2,1)S(1)}, bf16[512,512]{1,0:T(8,128)(2,1)}, u32[]{:S(2)}, u32[]{:S(2)}) collective-permute-start(bf16[512,512]{1,0:T(8,128)(2,1)S(1)} %bitcast.28), channel_id=1, source_target_pairs={{0,6},{1,7},{2,0},{3,1},{4,2},{5,3},{6,4},{7,5},{8,14},{9,15},{10,... | collective-permute-start | bytes 1572872 | tf_op jit(solution)/shard_map/ppermute | solution.py:580
  94.5 26.0 %collective-permute-start.7 = (bf16[512,512]{1,0:T(8,128)(2,1)}, bf16[512,512]{1,0:T(8,128)(2,1)}, u32[]{:S(2)}, u32[]{:S(2)}) collective-permute-start(bf16[512,512]{1,0:T(8,128)(2,1)} %collective-permute-done), channel_id=1, source_target_pairs={{0,2},{1,3},{2,4},{3,5},{4,6},{5,7},{6,0},{7,1},{8,10},{9,11},{10,... | collective-permute-start | bytes 1572872 | tf_op jit(solution)/shard_map/ppermute | solution.py:576
  94.8 30.9 %collective-permute-start.9 = (bf16[512,512]{1,0:T(8,128)(2,1)}, bf16[512,512]{1,0:T(8,128)(2,1)}, u32[]{:S(2)}, u32[]{:S(2)}) collective-permute-start(bf16[512,512]{1,0:T(8,128)(2,1)} %collective-permute-done), channel_id=1, source_target_pairs={{0,1},{1,0},{2,3},{3,2},{4,5},{5,4},{6,7},{7,6},{8,9},{9,8},{10,11... | collective-permute-start | bytes 1572872 | tf_op jit(solution)/shard_map/ppermute | solution.py:572
  96.7 23.9 %all-to-all-start.4 = ((bf16[16,64,256]{2,1,0:T(8,128)(2,1)}), bf16[16,64,256]{2,1,0:T(8,128)(2,1)S(1)}, u32[]{:S(2)}, u32[]{:S(2)}) async-start(bf16[16,64,256]{2,1,0:T(8,128)(2,1)} %shard_map.149), calls=%async_computation.4 | async-start | bytes 1048576 | tf_op jit(solution)/shard_map/all_to_all | solution.py:584
  103.2 1.3 copy-start.6
  105.9 15.9 %collective-permute-start.3 = (bf16[16,8192]{1,0:T(8,128)(2,1)S(1)}, bf16[16,8192]{1,0:T(8,128)(2,1)}, u32[]{:S(2)}, u32[]{:S(2)}) collective-permute-start(bf16[16,8192]{1,0:T(8,128)(2,1)S(1)} %get-tuple-element.59), channel_id=1, source_target_pairs={{0,2},{1,3},{2,4},{3,5},{4,6},{5,7},{6,0},{7,1},{8,10},{9,11},{10,... | collective-permute-start | bytes 786440 | tf_op jit(solution)/shard_map/ppermute | solution.py:576
  107.3 14.9 %collective-permute-start.4 = (bf16[16,8192]{1,0:T(8,128)(2,1)S(1)}, bf16[16,8192]{1,0:T(8,128)(2,1)}, u32[]{:S(2)}, u32[]{:S(2)}) collective-permute-start(bf16[16,8192]{1,0:T(8,128)(2,1)S(1)} %get-tuple-element.60), channel_id=1, source_target_pairs={{0,6},{1,7},{2,0},{3,1},{4,2},{5,3},{6,4},{7,5},{8,14},{9,15},{10,... | collective-permute-start | bytes 786440 | tf_op jit(solution)/shard_map/ppermute | solution.py:580
  114.3 12.7 %copy-start.1 = (f32[128,256]{1,0:T(8,128)S(1)}, f32[128,256]{1,0:T(8,128)}, u32[]{:S(2)}) copy-start(f32[128,256]{1,0:T(8,128)} %copy-done) | copy-start | bytes 393220
  114.3 12.7 %copy-start.3 = (f32[256,128]{1,0:T(8,128)S(1)}, f32[256,128]{1,0:T(8,128)}, u32[]{:S(2)}) copy-start(f32[256,128]{1,0:T(8,128)} %copy-done.2) | copy-start | bytes 393220
  120.5 11.8 %collective-permute-start.8 = (bf16[512,512]{1,0:T(8,128)(2,1)S(1)}, bf16[512,512]{1,0:T(8,128)(2,1)S(1)}, u32[]{:S(2)}, u32[]{:S(2)}) collective-permute-start(bf16[512,512]{1,0:T(8,128)(2,1)S(1)} %bitcast.29), channel_id=1, source_target_pairs={{0,1},{1,0},{2,3},{3,2},{4,5},{5,4},{6,7},{7,6},{8,9},{9,8},{10,11... | collective-permute-start | bytes 1572872 | tf_op jit(solution)/shard_map/ppermute | solution.py:572
  121.7 10.7 %collective-permute-start.10 = (bf16[512,512]{1,0:T(8,128)(2,1)}, bf16[512,512]{1,0:T(8,128)(2,1)S(1)}, u32[]{:S(2)}, u32[]{:S(2)}) collective-permute-start(bf16[512,512]{1,0:T(8,128)(2,1)} %collective-permute-done.1), channel_id=1, source_target_pairs={{0,1},{1,0},{2,3},{3,2},{4,5},{5,4},{6,7},{7,6},{8,9},{9,8},{10,11... | collective-permute-start | bytes 1572872 | tf_op jit(solution)/shard_map/ppermute | solution.py:572
  121.8 10.6 %collective-permute-start.11 = (bf16[512,512]{1,0:T(8,128)(2,1)}, bf16[512,512]{1,0:T(8,128)(2,1)S(1)}, u32[]{:S(2)}, u32[]{:S(2)}) collective-permute-start(bf16[512,512]{1,0:T(8,128)(2,1)} %collective-permute-done.7), channel_id=1, source_target_pairs={{0,1},{1,0},{2,3},{3,2},{4,5},{5,4},{6,7},{7,6},{8,9},{9,8},{10,11... | collective-permute-start | bytes 1572872 | tf_op jit(solution)/shard_map/ppermute | solution.py:572
  124.2 14.9 %collective-permute-start.5 = (bf16[32,8192]{1,0:T(8,128)(2,1)S(1)}, bf16[32,8192]{1,0:T(8,128)(2,1)}, u32[]{:S(2)}, u32[]{:S(2)}) collective-permute-start(bf16[32,8192]{1,0:T(8,128)(2,1)S(1)} %get-tuple-element.61), channel_id=1, source_target_pairs={{0,2},{1,3},{2,4},{3,5},{4,6},{5,7},{6,0},{7,1},{8,10},{9,11},{10,... | collective-permute-start | bytes 1572872 | tf_op jit(solution)/shard_map/ppermute | solution.py:576
  125.7 13.4 %collective-permute-start.6 = (bf16[32,8192]{1,0:T(8,128)(2,1)S(1)}, bf16[32,8192]{1,0:T(8,128)(2,1)}, u32[]{:S(2)}, u32[]{:S(2)}) collective-permute-start(bf16[32,8192]{1,0:T(8,128)(2,1)S(1)} %get-tuple-element.62), channel_id=1, source_target_pairs={{0,6},{1,7},{2,0},{3,1},{4,2},{5,3},{6,4},{7,5},{8,14},{9,15},{10,... | collective-permute-start | bytes 1572872 | tf_op jit(solution)/shard_map/ppermute | solution.py:580
  132.4 0.8 copy-start.7
  132.4 0.9 copy-start.8
  132.4 1.1 copy-start.9
Sparse Core Ops, SparseCore 0:
  9.7 35.9 all-gather.2
  48.2 80.5 all-gather.4
